TPU v7x, 32 devices: a whole 2x2x4 slice. The times are simulated.
32 devices in a mesh: gx: 16 (over z, y, x), gz: 2 (over core).
Axes of the slice: x: 2, y: 2, z: 4, core: 2. Of those that a mesh axis runs over, the one named last changes fastest.
Arguments:
- density: float32 [32, 64, 256], P('gx', None, 'gz'), may hold values from 0.1 to 1
- anchor_mask: int32 [32, 64, 256], P('gx', None, 'gz'), may hold values 0 or 1
- port_mask: int32 [32, 64, 256], P('gx', None, 'gz'), may hold values 0 or 1
- heater_owner: int32 [16, 2, 256, 1], P('gx', 'gz'), may hold values from 0 to 15; in each aligned block of 256 rows (0 to 255, 256 to 511, ..., all dimensions but the last counted through in order) at most 32 rows name the same one
- heater_cell: int32 [16, 2, 256], P('gx', 'gz'), may hold values from 0 to 16383
- heater_power: float32 [16, 2, 256], P('gx', 'gz'), may hold values from 1 to 10
Outputs:
- temperature: float32 [32, 64, 256], P('gx', None, 'gz')
- temperature_adjoint: float32 [32, 64, 256], P('gx', None, 'gz')
- displacement: float32 [3, 32, 64, 256], P(None, 'gx', None, 'gz')
- displacement_adjoint: float32 [3, 32, 64, 256], P(None, 'gx', None, 'gz')
- thermal_residual: float32 [2, 32, 64, 256], P(None, 'gx', None, 'gz')
- elastic_residual: float32 [2, 3, 32, 64, 256], P(None, None, 'gx', None, 'gz')
Inputs may be any that keep to these rules, and one draw needn't show every extreme that they name: `heater_owner`: among the entries of one device, each block is named at most 32 times.
All inputs are finite; a program needn't handle non-finite values. No bound on the sum of `anchor_mask` or of `port_mask` on one device may be relied on, other than what follows from the above.
Results may differ from a plain program's by a relative error of at most 0.00018.
Values sent between devices are 32-bit elements; how exact they have to be, the bound alone decides.
No kernel may reach another device: no remote copies, remote signals or barrier semaphores. Data moves between devices by JAX's collectives and lax.ppermute only.
A program may use at most 64 MiB of HBM per device.

v0:
```python
import jax
import jax.numpy as jnp
from jax import lax
from jax.sharding import PartitionSpec as P

ITERS = 2


KAPPA_MIN = 0.05
MODULUS_MINIMUM = 0.02
CONVECTION = 0.2
PENALTY = 10.0
JOULE_GAIN = 1.0
SIGMA_MIN = 0.1
EXPANSION = 4.0
PORT_DIRECTION = (1.0, 0.5, -0.5)


def with_halo(cells, sides, width):
    for axis, dim in sides:
        count = lax.axis_size(axis)
        ends = count - 1
        head = lax.slice_in_dim(cells, 0, width, axis=dim)
        tail = lax.slice_in_dim(cells, cells.shape[dim] - width, cells.shape[dim], axis=dim)
        cells = jnp.concatenate(
            [
                lax.ppermute(tail, axis, [(i, (i + 1) % count) for i in range(ends)]),
                cells,
                lax.ppermute(head, axis, [((i + 1) % count, i) for i in range(ends)]),
            ],
            axis=dim,
        )
    return cells


def coefficients(cubed, symmetry, floor_value):
    scalar_pairing = cubed[1:-1, 1:-1, 1:-1]
    lower_x = (floor_value + 0.5 * (scalar_pairing + cubed[:-2, 1:-1, 1:-1])) * symmetry
    upper_x = floor_value + 0.5 * (scalar_pairing + cubed[2:, 1:-1, 1:-1])
    lower_y = floor_value + 0.5 * (scalar_pairing + cubed[1:-1, :-2, 1:-1])
    upper_y = floor_value + 0.5 * (scalar_pairing + cubed[1:-1, 2:, 1:-1])
    lower_z = floor_value + 0.5 * (scalar_pairing + cubed[1:-1, 1:-1, :-2])
    upper_z = floor_value + 0.5 * (scalar_pairing + cubed[1:-1, 1:-1, 2:])
    return (lower_x, upper_x, lower_y, upper_y, lower_z, upper_z)


def stencil(padded, values, weights, diagonal_term):
    lower_x, upper_x, lower_y, upper_y, lower_z, upper_z = weights
    result = diagonal_term * values
    result = result + lower_x * (values - padded[..., :-2, 1:-1, 1:-1])
    result = result + upper_x * (values - padded[..., 2:, 1:-1, 1:-1])
    result = result + lower_y * (values - padded[..., 1:-1, :-2, 1:-1])
    result = result + upper_y * (values - padded[..., 1:-1, 2:, 1:-1])
    result = result + lower_z * (values - padded[..., 1:-1, 1:-1, :-2])
    result = result + upper_z * (values - padded[..., 1:-1, 1:-1, 2:])
    return result


def pad_second(values):
    widths = [(0, 0)] * (values.ndim - 2) + [(1, 1), (0, 0)]
    return jnp.pad(values, widths)


def inner_products(one_side, other_side):
    return jnp.sum(one_side * other_side, axis=tuple(range(1, one_side.ndim)))


def widen(scalars):
    return scalars[:, None, None, None, None]


def symmetry_mask(layers):
    first_layer = lax.broadcasted_iota(jnp.int32, (layers, 1, 1), 0) == 0
    on_plane = jnp.logical_and(first_layer, lax.axis_index("gx") == 0)
    return jnp.where(on_plane, 0.0, 1.0).astype(jnp.float32)


def deliver_heat(heater_owner, heater_cell, heater_power, local_shape):
    owner_block = heater_owner.reshape(-1)
    cell_index = heater_cell.reshape(-1)
    power_value = heater_power.reshape(-1)
    entry_lists = jnp.stack(
        [owner_block.astype(jnp.float32), cell_index.astype(jnp.float32), power_value]
    )
    everyone = lax.all_gather(entry_lists, "gx", axis=1, tiled=True)
    targets = everyone[1].astype(jnp.int32)
    amounts = jnp.where(everyone[0].astype(jnp.int32) == lax.axis_index("gx"), everyone[2], 0.0)
    cells_total = local_shape[0] * local_shape[1] * local_shape[2]
    heater = jnp.zeros((cells_total,), jnp.float32).at[targets].add(amounts)
    return heater.reshape(local_shape)


def per_device(density, anchor_mask, port_mask, heater_owner, heater_cell, heater_power):
    layers = density.shape[0]
    bordered = with_halo(density, (("gx", 0), ("gz", 2)), 1)
    cubed = pad_second(bordered) ** 3
    scalar_pairing = cubed[1:-1, 1:-1, 1:-1]
    symmetry = symmetry_mask(layers)
    thermal_weights = coefficients(cubed, symmetry, KAPPA_MIN)
    elastic_weights = coefficients(cubed, symmetry, MODULUS_MINIMUM)
    heater = deliver_heat(heater_owner, heater_cell, heater_power, density.shape)
    source = JOULE_GAIN * (SIGMA_MIN + scalar_pairing) + heater
    port_field = port_mask.astype(jnp.float32)
    joule_power_array = jnp.stack([source, port_field])
    bordered_rhs = with_halo(joule_power_array, (("gx", 1), ("gz", 3)), 1)
    applied = stencil(pad_second(bordered_rhs), joule_power_array, thermal_weights, CONVECTION)
    thermal_norm, thermal_curve = lax.psum(
        (
            inner_products(joule_power_array, joule_power_array),
            inner_products(joule_power_array, applied),
        ),
        ("gx", "gz"),
    )
    correction_magnitude = thermal_norm / thermal_curve
    thermal_readings = correction_magnitude[:, None, None, None] * joule_power_array
    thermal_residual = joule_power_array - correction_magnitude[:, None, None, None] * applied
    mechanical_tension = (MODULUS_MINIMUM + scalar_pairing) * thermal_readings[0]
    spread = with_halo(mechanical_tension, (("gx", 0), ("gz", 2)), 1)
    mirrored = jnp.where(
        lax.axis_index("gx") == 0, jnp.pad(mechanical_tension[0], ((0, 0), (1, 1))), spread[0]
    )
    spread = pad_second(spread.at[0].set(mirrored))
    thermal_force = (
        EXPANSION
        * 0.5
        * jnp.stack(
            [
                spread[2:, 1:-1, 1:-1] - spread[:-2, 1:-1, 1:-1],
                spread[1:-1, 2:, 1:-1] - spread[1:-1, :-2, 1:-1],
                spread[1:-1, 1:-1, 2:] - spread[1:-1, 1:-1, :-2],
            ]
        )
    )
    direction_vector = jnp.array(PORT_DIRECTION, jnp.float32)[:, None, None, None]
    elastic_rhs = jnp.stack([thermal_force, port_field[None] * direction_vector])
    anchor_term = PENALTY * anchor_mask.astype(jnp.float32)
    first_border = with_halo(elastic_rhs, (("gx", 2), ("gz", 4)), 1)
    first_applied = stencil(pad_second(first_border), elastic_rhs, elastic_weights, anchor_term)

    def joint_products(values, image_values):
        return lax.psum(
            (inner_products(values, values), inner_products(values, image_values)), ("gx", "gz")
        )

    computed_solution = jnp.zeros_like(elastic_rhs)
    residual = elastic_rhs
    applied = first_applied
    norm_now, product = joint_products(residual, applied)
    correction_magnitude = norm_now / product
    direction = residual
    along_image = applied
    for iteration in range(ITERS):
        computed_solution = computed_solution + widen(correction_magnitude) * direction
        residual = residual - widen(correction_magnitude) * along_image
        if iteration + 1 < ITERS:
            bordered_values = with_halo(residual, (("gx", 2), ("gz", 4)), 1)
            applied = stencil(pad_second(bordered_values), residual, elastic_weights, anchor_term)
            norm_next, product = joint_products(residual, applied)
            ratio_next = norm_next / norm_now
            correction_magnitude = norm_next / (
                product - ratio_next * norm_next / correction_magnitude
            )
            direction = residual + widen(ratio_next) * direction
            along_image = applied + widen(ratio_next) * along_image
            norm_now = norm_next
    return (
        thermal_readings[0],
        thermal_readings[1],
        computed_solution[0],
        computed_solution[1],
        thermal_residual,
        residual,
    )


def solution(mesh):
    in_specs = (
        P("gx", None, "gz"),
        P("gx", None, "gz"),
        P("gx", None, "gz"),
        P("gx", "gz", None, None),
        P("gx", "gz", None),
        P("gx", "gz", None),
    )
    out_specs = (
        P("gx", None, "gz"),
        P("gx", None, "gz"),
        P(None, "gx", None, "gz"),
        P(None, "gx", None, "gz"),
        P(None, "gx", None, "gz"),
        P(None, None, "gx", None, "gz"),
    )
    return jax.shard_map(
        per_device, mesh=mesh, in_specs=in_specs, out_specs=out_specs, check_vma=False
    )
```

profile of v0, /device:TPU:0, one launch (start us, length us, event | category | flops | bytes accessed | tf_op | source)
XLA Modules:
  0.0 272.1 jit_solution(7036077150451142261)
XLA Ops:
  2.7 5.5 %collective-permute-start = (f32[1,64,128]{2,1,0:T(8,128)S(1)}, f32[1,64,128]{2,1,0:T(8,128)S(1)}, u32[]{:S(2)}, u32[]{:S(2)}) collective-permute-start(f32[1,64,128]{2,1,0:T(8,128)S(1)} %get-tuple-element.87), channel_id=1, source_target_pairs={{0,2},{2,4},{4,6},{6,8},{8,10},{10,12},{12,14},{14,16},{16,18},{18... | collective-permute-start | bytes 98312 | tf_op jit(solution)/shard_map/ppermute | solution.py:27
  10.3 39.7 %all_gather.3 = f32[3,4096]{1,0:T(4,128)S(1)} all-gather(f32[3,256]{1,0:T(4,128)S(1)} %pad_maximum_fusion.39), channel_id=1, replica_groups=mesh['gx'=16,'gz'=2] {'gx'}, dimensions={1}, use_global_device_ids=true | all-gather | bytes 52224 | tf_op jit(solution)/shard_map/all_gather | solution.py:85
  51.0 1.3 collective-permute-start.2
  54.5 21.9 %scatter_custom_fusion = f32[16384]{0:T(1024)S(1)} fusion(s32[4096]{0:T(1024)S(1)} %bitcast.47, f32[4096]{0:T(1024)S(1)} %bitcast.46, f32[]{:T(128)} %constant.47.clone.1), kind=kCustom, calls=%fused_computation.190 | custom fusion | flops 4096 | bytes 65540 | tf_op jit(solution)/shard_map/scatter-add | solution.py:89
  80.2 4.6 %collective-permute-done.5 = f32[2,1,64,128]{3,2,1,0:T(8,128)S(1)} collective-permute-done((f32[2,1,64,128]{3,2,1,0:T(8,128)S(1)}, f32[2,1,64,128]{3,2,1,0:T(8,128)S(1)}, u32[]{:S(2)}, u32[]{:S(2)}) %collective-permute-start.5) | collective-permute-done | bytes 65568 | tf_op jit(solution)/shard_map/ppermute | solution.py:29
  84.9 2.0 collective-permute-start.6
  88.5 1.9 collective-permute-done.7
  91.0 37.8 %all-reduce.8 = (f32[2]{0:T(128)S(1)}, f32[2]{0:T(128)S(1)}) all-reduce(f32[2]{0:T(128)S(1)} %get-tuple-element.29, f32[2]{0:T(128)S(1)} %get-tuple-element.28), channel_id=1, replica_groups=mesh['gx'=16,'gz'=2] {'gx','gz'}, use_global_device_ids=true, to_apply=%region_2.3 | all-reduce | flops 4 | bytes 32 | tf_op jit(solution)/shard_map/psum | solution.py:107
  131.5 4.8 %collective-permute-start.8 = (f32[1,64,128]{2,1,0:T(8,128)S(1)}, f32[1,64,128]{2,1,0:T(8,128)S(1)}, u32[]{:S(2)}, u32[]{:S(2)}) collective-permute-start(f32[1,64,128]{2,1,0:T(8,128)S(1)} %get-tuple-element.83), channel_id=1, source_target_pairs={{0,2},{2,4},{4,6},{6,8},{8,10},{10,12},{12,14},{14,16},{16,18},{18... | collective-permute-start | bytes 98312 | tf_op jit(solution)/shard_map/ppermute | solution.py:27
  136.4 1.6 collective-permute-done.8
  138.0 1.3 collective-permute-start.10
  140.8 1.8 collective-permute-done.11
  143.1 4.8 %collective-permute-start.12 = (f32[2,3,1,64,128]{4,3,2,1,0:T(8,128)S(1)}, f32[2,3,1,64,128]{4,3,2,1,0:T(8,128)S(1)}, u32[]{:S(2)}, u32[]{:S(2)}) collective-permute-start(f32[2,3,1,64,128]{4,3,2,1,0:T(8,128)S(1)} %get-tuple-element.53), channel_id=1, source_target_pairs={{0,2},{2,4},{4,6},{6,8},{8,10},{10,12},{12,14},{14,16},{16,18},{18... | collective-permute-start | bytes 589832 | tf_op jit(solution)/shard_map/ppermute | solution.py:27
  149.2 3.1 %collective-permute-done.12 = f32[2,3,1,64,128]{4,3,2,1,0:T(8,128)S(1)} collective-permute-done((f32[2,3,1,64,128]{4,3,2,1,0:T(8,128)S(1)}, f32[2,3,1,64,128]{4,3,2,1,0:T(8,128)S(1)}, u32[]{:S(2)}, u32[]{:S(2)}) %collective-permute-start.12) | collective-permute-done | bytes 196640 | tf_op jit(solution)/shard_map/ppermute | solution.py:27
  152.4 7.9 %collective-permute-done.13 = f32[2,3,1,64,128]{4,3,2,1,0:T(8,128)S(1)} collective-permute-done((f32[2,3,1,64,128]{4,3,2,1,0:T(8,128)S(1)}, f32[2,3,1,64,128]{4,3,2,1,0:T(8,128)S(1)}, u32[]{:S(2)}, u32[]{:S(2)}) %collective-permute-start.13) | collective-permute-done | bytes 196640 | tf_op jit(solution)/shard_map/ppermute | solution.py:29
  161.2 1.3 collective-permute-start.15
  162.5 3.0 %collective-permute-start.14 = (f32[2,3,4,64,1]{3,2,4,1,0:T(4,128)S(1)}, f32[2,3,4,64,1]{3,2,4,1,0:T(4,128)S(1)}, u32[]{:S(2)}, u32[]{:S(2)}) collective-permute-start(f32[2,3,4,64,1]{3,2,4,1,0:T(4,128)S(1)} %copy.32), channel_id=1, source_target_pairs={{0,1},{2,3},{4,5},{6,7},{8,9},{10,11},{12,13},{14,15},{16,17},{18,... | collective-permute-start | bytes 18440 | tf_op jit(solution)/shard_map/ppermute | solution.py:27
  168.6 41.3 %all-reduce.7 = (f32[2]{0:T(128)S(1)}, f32[2]{0:T(128)S(1)}) all-reduce(f32[2]{0:T(128)S(1)} %get-tuple-element.27, f32[2]{0:T(128)S(1)} %get-tuple-element.26), channel_id=1, replica_groups=mesh['gx'=16,'gz'=2] {'gx','gz'}, use_global_device_ids=true, to_apply=%region_6.7 | all-reduce | flops 4 | bytes 32 | tf_op jit(solution)/shard_map/psum | solution.py:141
  210.1 4.2 %collective-permute-start.16 = (f32[2,3,1,64,128]{4,3,2,1,0:T(8,128)S(1)}, f32[2,3,1,64,128]{4,3,2,1,0:T(8,128)S(1)}, u32[]{:S(2)}, u32[]{:S(2)}) collective-permute-start(f32[2,3,1,64,128]{4,3,2,1,0:T(8,128)S(1)} %get-tuple-element.51), channel_id=1, source_target_pairs={{0,2},{2,4},{4,6},{6,8},{8,10},{10,12},{12,14},{14,16},{16,18},{18... | collective-permute-start | bytes 589832 | tf_op jit(solution)/shard_map/ppermute | solution.py:27
  215.6 6.1 %collective-permute-done.16 = f32[2,3,1,64,128]{4,3,2,1,0:T(8,128)S(1)} collective-permute-done((f32[2,3,1,64,128]{4,3,2,1,0:T(8,128)S(1)}, f32[2,3,1,64,128]{4,3,2,1,0:T(8,128)S(1)}, u32[]{:S(2)}, u32[]{:S(2)}) %collective-permute-start.16) | collective-permute-done | bytes 196640 | tf_op jit(solution)/shard_map/ppermute | solution.py:27
  221.7 1.6 collective-permute-done.17
  224.2 1.3 collective-permute-start.19
  225.5 3.0 %collective-permute-start.18 = (f32[2,3,4,64,1]{3,2,4,1,0:T(4,128)S(1)}, f32[2,3,4,64,1]{3,2,4,1,0:T(4,128)S(1)}, u32[]{:S(2)}, u32[]{:S(2)}) collective-permute-start(f32[2,3,4,64,1]{3,2,4,1,0:T(4,128)S(1)} %copy.38), channel_id=1, source_target_pairs={{0,1},{2,3},{4,5},{6,7},{8,9},{10,11},{12,13},{14,15},{16,17},{18,... | collective-permute-start | bytes 18440 | tf_op jit(solution)/shard_map/ppermute | solution.py:27
  231.8 38.0 %all-reduce.6 = (f32[2]{0:T(128)S(1)}, f32[2]{0:T(128)S(1)}) all-reduce(f32[2]{0:T(128)S(1)} %get-tuple-element.25, f32[2]{0:T(128)S(1)} %get-tuple-element.24), channel_id=1, replica_groups=mesh['gx'=16,'gz'=2] {'gx','gz'}, use_global_device_ids=true, to_apply=%region_10.11 | all-reduce | flops 4 | bytes 32 | tf_op jit(solution)/shard_map/psum | solution.py:141
  (111 shorter events, 30.9 us)
Async XLA Ops:
  1.4 49.5 %collective-permute-start.1 = (f32[1,64,128]{2,1,0:T(8,128)S(1)}, f32[1,64,128]{2,1,0:T(8,128)S(1)}, u32[]{:S(2)}, u32[]{:S(2)}) collective-permute-start(f32[1,64,128]{2,1,0:T(8,128)S(1)} %get-tuple-element.86), channel_id=1, source_target_pairs={{2,0},{4,2},{6,4},{8,6},{10,8},{12,10},{14,12},{16,14},{18,16},{20... | collective-permute-start | bytes 98312 | tf_op jit(solution)/shard_map/ppermute | solution.py:29
  2.7 47.3 %collective-permute-start = (f32[1,64,128]{2,1,0:T(8,128)S(1)}, f32[1,64,128]{2,1,0:T(8,128)S(1)}, u32[]{:S(2)}, u32[]{:S(2)}) collective-permute-start(f32[1,64,128]{2,1,0:T(8,128)S(1)} %get-tuple-element.87), channel_id=1, source_target_pairs={{0,2},{2,4},{4,6},{6,8},{8,10},{10,12},{12,14},{14,16},{16,18},{18... | collective-permute-start | bytes 98312 | tf_op jit(solution)/shard_map/ppermute | solution.py:27
  51.0 25.4 %collective-permute-start.2 = (f32[4,64,1]{2,1,0:T(8,128)S(1)}, f32[4,64,1]{2,1,0:T(8,128)S(1)}, u32[]{:S(2)}, u32[]{:S(2)}) collective-permute-start(f32[4,64,1]{2,1,0:T(8,128)S(1)} %get-tuple-element.79), channel_id=1, source_target_pairs={{0,1},{2,3},{4,5},{6,7},{8,9},{10,11},{12,13},{14,15},{16,17},{18,... | collective-permute-start | bytes 3080 | tf_op jit(solution)/shard_map/ppermute | solution.py:27
  52.3 24.1 %collective-permute-start.3 = (f32[4,64,1]{2,1,0:T(8,128)S(1)}, f32[4,64,1]{2,1,0:T(8,128)S(1)}, u32[]{:S(2)}, u32[]{:S(2)}) collective-permute-start(f32[4,64,1]{2,1,0:T(8,128)S(1)} %get-tuple-element.80), channel_id=1, source_target_pairs={{1,0},{3,2},{5,4},{7,6},{9,8},{11,10},{13,12},{15,14},{17,16},{19,... | collective-permute-start | bytes 3080 | tf_op jit(solution)/shard_map/ppermute | solution.py:29
  76.8 3.4 %collective-permute-start.4 = (f32[2,1,64,128]{3,2,1,0:T(8,128)S(1)}, f32[2,1,64,128]{3,2,1,0:T(8,128)S(1)}, u32[]{:S(2)}, u32[]{:S(2)}) collective-permute-start(f32[2,1,64,128]{3,2,1,0:T(8,128)S(1)} %get-tuple-element.77), channel_id=1, source_target_pairs={{0,2},{2,4},{4,6},{6,8},{8,10},{10,12},{12,14},{14,16},{16,18},{18... | collective-permute-start | bytes 196616 | tf_op jit(solution)/shard_map/ppermute | solution.py:27
  78.1 6.7 %collective-permute-start.5 = (f32[2,1,64,128]{3,2,1,0:T(8,128)S(1)}, f32[2,1,64,128]{3,2,1,0:T(8,128)S(1)}, u32[]{:S(2)}, u32[]{:S(2)}) collective-permute-start(f32[2,1,64,128]{3,2,1,0:T(8,128)S(1)} %get-tuple-element.78), channel_id=1, source_target_pairs={{2,0},{4,2},{6,4},{8,6},{10,8},{12,10},{14,12},{16,14},{18,16},{20... | collective-permute-start | bytes 196616 | tf_op jit(solution)/shard_map/ppermute | solution.py:29
  84.9 3.6 %collective-permute-start.6 = (f32[2,4,64,1]{3,2,1,0:T(8,128)S(1)}, f32[2,4,64,1]{3,2,1,0:T(8,128)S(1)}, u32[]{:S(2)}, u32[]{:S(2)}) collective-permute-start(f32[2,4,64,1]{3,2,1,0:T(8,128)S(1)} %get-tuple-element.71), channel_id=1, source_target_pairs={{0,1},{2,3},{4,5},{6,7},{8,9},{10,11},{12,13},{14,15},{16,17},{18,... | collective-permute-start | bytes 6152 | tf_op jit(solution)/shard_map/ppermute | solution.py:27
  87.0 3.4 %collective-permute-start.7 = (f32[2,4,64,1]{3,2,1,0:T(8,128)S(1)}, f32[2,4,64,1]{3,2,1,0:T(8,128)S(1)}, u32[]{:S(2)}, u32[]{:S(2)}) collective-permute-start(f32[2,4,64,1]{3,2,1,0:T(8,128)S(1)} %get-tuple-element.72), channel_id=1, source_target_pairs={{1,0},{3,2},{5,4},{7,6},{9,8},{11,10},{13,12},{15,14},{17,16},{19,... | collective-permute-start | bytes 6152 | tf_op jit(solution)/shard_map/ppermute | solution.py:29
  88.5 79.4 %copy-start.2 = (f32[2,64,128]{2,1,0:T(8,128)}, f32[2,64,128]{2,1,0:T(8,128)S(1)}, u32[]{:S(2)}) copy-start(f32[2,64,128]{2,1,0:T(8,128)S(1)} %get-tuple-element.55) | copy-start | bytes 196612
  88.5 79.4 %copy-start.4 = (f32[2,64,128]{2,1,0:T(8,128)}, f32[2,64,128]{2,1,0:T(8,128)S(1)}, u32[]{:S(2)}) copy-start(f32[2,64,128]{2,1,0:T(8,128)S(1)} %get-tuple-element.57) | copy-start | bytes 196612
  88.5 79.4 %copy-start.6 = (f32[2,64,128]{2,1,0:T(8,128)}, f32[2,64,128]{2,1,0:T(8,128)S(1)}, u32[]{:S(2)}) copy-start(f32[2,64,128]{2,1,0:T(8,128)S(1)} %get-tuple-element.58) | copy-start | bytes 196612
  88.5 79.4 %copy-start.8 = (f32[2,64,128]{2,1,0:T(8,128)}, f32[2,64,128]{2,1,0:T(8,128)S(1)}, u32[]{:S(2)}) copy-start(f32[2,64,128]{2,1,0:T(8,128)S(1)} %get-tuple-element.59) | copy-start | bytes 196612
  130.2 6.1 %collective-permute-start.9 = (f32[1,64,128]{2,1,0:T(8,128)S(1)}, f32[1,64,128]{2,1,0:T(8,128)S(1)}, u32[]{:S(2)}, u32[]{:S(2)}) collective-permute-start(f32[1,64,128]{2,1,0:T(8,128)S(1)} %get-tuple-element.82), channel_id=1, source_target_pairs={{2,0},{4,2},{6,4},{8,6},{10,8},{12,10},{14,12},{16,14},{18,16},{20... | collective-permute-start | bytes 98312 | tf_op jit(solution)/shard_map/ppermute | solution.py:29
  131.5 6.4 %collective-permute-start.8 = (f32[1,64,128]{2,1,0:T(8,128)S(1)}, f32[1,64,128]{2,1,0:T(8,128)S(1)}, u32[]{:S(2)}, u32[]{:S(2)}) collective-permute-start(f32[1,64,128]{2,1,0:T(8,128)S(1)} %get-tuple-element.83), channel_id=1, source_target_pairs={{0,2},{2,4},{4,6},{6,8},{8,10},{10,12},{12,14},{14,16},{16,18},{18... | collective-permute-start | bytes 98312 | tf_op jit(solution)/shard_map/ppermute | solution.py:27
  138.0 2.7 collective-permute-start.10
  139.4 3.2 %collective-permute-start.11 = (f32[4,64,1]{2,1,0:T(8,128)S(1)}, f32[4,64,1]{2,1,0:T(8,128)S(1)}, u32[]{:S(2)}, u32[]{:S(2)}) collective-permute-start(f32[4,64,1]{2,1,0:T(8,128)S(1)} %get-tuple-element.76), channel_id=1, source_target_pairs={{1,0},{3,2},{5,4},{7,6},{9,8},{11,10},{13,12},{15,14},{17,16},{19,... | collective-permute-start | bytes 3080 | tf_op jit(solution)/shard_map/ppermute | solution.py:29
  143.1 9.3 %collective-permute-start.12 = (f32[2,3,1,64,128]{4,3,2,1,0:T(8,128)S(1)}, f32[2,3,1,64,128]{4,3,2,1,0:T(8,128)S(1)}, u32[]{:S(2)}, u32[]{:S(2)}) collective-permute-start(f32[2,3,1,64,128]{4,3,2,1,0:T(8,128)S(1)} %get-tuple-element.53), channel_id=1, source_target_pairs={{0,2},{2,4},{4,6},{6,8},{8,10},{10,12},{12,14},{14,16},{16,18},{18... | collective-permute-start | bytes 589832 | tf_op jit(solution)/shard_map/ppermute | solution.py:27
  147.9 12.3 %collective-permute-start.13 = (f32[2,3,1,64,128]{4,3,2,1,0:T(8,128)S(1)}, f32[2,3,1,64,128]{4,3,2,1,0:T(8,128)S(1)}, u32[]{:S(2)}, u32[]{:S(2)}) collective-permute-start(f32[2,3,1,64,128]{4,3,2,1,0:T(8,128)S(1)} %get-tuple-element.54), channel_id=1, source_target_pairs={{2,0},{4,2},{6,4},{8,6},{10,8},{12,10},{14,12},{16,14},{18,16},{20... | collective-permute-start | bytes 589832 | tf_op jit(solution)/shard_map/ppermute | solution.py:29
  161.2 5.5 %collective-permute-start.15 = (f32[2,3,4,64,1]{3,2,4,1,0:T(4,128)S(1)}, f32[2,3,4,64,1]{3,2,4,1,0:T(4,128)S(1)}, u32[]{:S(2)}, u32[]{:S(2)}) collective-permute-start(f32[2,3,4,64,1]{3,2,4,1,0:T(4,128)S(1)} %copy.33), channel_id=1, source_target_pairs={{1,0},{3,2},{5,4},{7,6},{9,8},{11,10},{13,12},{15,14},{17,16},{19,... | collective-permute-start | bytes 18440 | tf_op jit(solution)/shard_map/ppermute | solution.py:29
  162.5 3.9 %collective-permute-start.14 = (f32[2,3,4,64,1]{3,2,4,1,0:T(4,128)S(1)}, f32[2,3,4,64,1]{3,2,4,1,0:T(4,128)S(1)}, u32[]{:S(2)}, u32[]{:S(2)}) collective-permute-start(f32[2,3,4,64,1]{3,2,4,1,0:T(4,128)S(1)} %copy.32), channel_id=1, source_target_pairs={{0,1},{2,3},{4,5},{6,7},{8,9},{10,11},{12,13},{14,15},{16,17},{18,... | collective-permute-start | bytes 18440 | tf_op jit(solution)/shard_map/ppermute | solution.py:27
  210.1 11.6 %collective-permute-start.16 = (f32[2,3,1,64,128]{4,3,2,1,0:T(8,128)S(1)}, f32[2,3,1,64,128]{4,3,2,1,0:T(8,128)S(1)}, u32[]{:S(2)}, u32[]{:S(2)}) collective-permute-start(f32[2,3,1,64,128]{4,3,2,1,0:T(8,128)S(1)} %get-tuple-element.51), channel_id=1, source_target_pairs={{0,2},{2,4},{4,6},{6,8},{8,10},{10,12},{12,14},{14,16},{16,18},{18... | collective-permute-start | bytes 589832 | tf_op jit(solution)/shard_map/ppermute | solution.py:27
  214.3 9.0 %collective-permute-start.17 = (f32[2,3,1,64,128]{4,3,2,1,0:T(8,128)S(1)}, f32[2,3,1,64,128]{4,3,2,1,0:T(8,128)S(1)}, u32[]{:S(2)}, u32[]{:S(2)}) collective-permute-start(f32[2,3,1,64,128]{4,3,2,1,0:T(8,128)S(1)} %get-tuple-element.52), channel_id=1, source_target_pairs={{2,0},{4,2},{6,4},{8,6},{10,8},{12,10},{14,12},{16,14},{18,16},{20... | collective-permute-start | bytes 589832 | tf_op jit(solution)/shard_map/ppermute | solution.py:29
  224.2 5.5 %collective-permute-start.19 = (f32[2,3,4,64,1]{3,2,4,1,0:T(4,128)S(1)}, f32[2,3,4,64,1]{3,2,4,1,0:T(4,128)S(1)}, u32[]{:S(2)}, u32[]{:S(2)}) collective-permute-start(f32[2,3,4,64,1]{3,2,4,1,0:T(4,128)S(1)} %copy.39), channel_id=1, source_target_pairs={{1,0},{3,2},{5,4},{7,6},{9,8},{11,10},{13,12},{15,14},{17,16},{19,... | collective-permute-start | bytes 18440 | tf_op jit(solution)/shard_map/ppermute | solution.py:29
  225.5 3.9 %collective-permute-start.18 = (f32[2,3,4,64,1]{3,2,4,1,0:T(4,128)S(1)}, f32[2,3,4,64,1]{3,2,4,1,0:T(4,128)S(1)}, u32[]{:S(2)}, u32[]{:S(2)}) collective-permute-start(f32[2,3,4,64,1]{3,2,4,1,0:T(4,128)S(1)} %copy.38), channel_id=1, source_target_pairs={{0,1},{2,3},{4,5},{6,7},{8,9},{10,11},{12,13},{14,15},{16,17},{18,... | collective-permute-start | bytes 18440 | tf_op jit(solution)/shard_map/ppermute | solution.py:27
  (13 other events, 242.6 us)
where the time goes:
time: 273 us; the launch traced here: 272 us
  blocking collectives  157 us (58%)
  starting transfers between devices  44.2 us (16%)
  other arithmetic  32.8 us (12%)
  waiting for transfers between devices  30.3 us (11%)
  local copies, waits for them, and re-layouts  6.71 us (2%)
    psum x2, blocking collectives, joint_products(): lax.psum((inner_products(values, values), inner_products(values, image_va...  79.3 us
    all_gather x1, blocking collectives, deliver_heat(): everyone = lax.all_gather(entry_lists, 'gx', axis=1, tiled=True)  39.7 us
    psum x1, blocking collectives, per_device(): lax.psum((inner_products(joule_power_array, joule_power_array), inner_pro...  37.8 us
    ppermute x10, starting transfers between devices, with_halo(): lax.ppermute(tail, axis, [(i, (i + 1) % count) for i in range(ends)])  31.3 us
    scatter-add x1, other arithmetic, deliver_heat(): heater = jnp.zeros((cells_total,), jnp.float32).at[targets].add(amounts)  21.9 us
    ppermute x10, waiting for transfers between devices, with_halo(): lax.ppermute(head, axis, [((i + 1) % count, i) for i in range(ends)])  17.8 us
    ppermute x10, starting transfers between devices, with_halo(): lax.ppermute(head, axis, [((i + 1) % count, i) for i in range(ends)])  12.9 us
    ppermute x10, waiting for transfers between devices, with_halo(): lax.ppermute(tail, axis, [(i, (i + 1) % count) for i in range(ends)])  12.6 us
  transfers between devices with their start and end apart: 20, of which 11 were waited for; matrix products, arithmetic and copies ran while one was open for 10% of the time, Pallas kernels for 0%

commit v1 on v0

v1 whole, which is shorter than its diff:
```python
import functools

import jax
import jax.numpy as jnp
from jax import lax
from jax.experimental import pallas as pl
from jax.experimental.pallas import tpu as pltpu
from jax.sharding import PartitionSpec as P

KAPPA_MIN = 0.05
MODULUS_MINIMUM = 0.02
CONVECTION = 0.2
PENALTY = 10.0
JOULE_GAIN = 1.0
SIGMA_MIN = 0.1
EXPANSION = 4.0
PORT_DIRECTION = (1.0, 0.5, -0.5)

HALO = 3
WIDTH = 128
EDGE = 8
F32 = jnp.float32


def swap_pairs(count, offset, distance):
    pairs = []
    for low in range(offset, count - distance):
        if ((low - offset) // distance) % 2 == 0:
            pairs += [(low, low + distance), (low + distance, low)]
    return pairs


def across_z(values):
    count = lax.axis_size("gz")
    if count == 2:
        return lax.ppermute(values, "gz", [(0, 1), (1, 0)])
    upper = lax.ppermute(values, "gz", [(i + 1, i) for i in range(count - 1)])
    lower = lax.ppermute(values, "gz", [(i, i + 1) for i in range(count - 1)])
    lanes = lax.broadcasted_iota(jnp.int32, values.shape, values.ndim - 1)
    return jnp.where(lanes < WIDTH // 2, upper, lower)


def heater_kernel(entries_ref, heat_ref, rows_ref, lanes_ref, total_ref, *, layers, height, block):
    sources = entries_ref.shape[0]
    entries = entries_ref.shape[2]
    slabs = layers + 2 * HALO
    base = lax.axis_index("gx") * layers - HALO
    row_ids = lax.broadcasted_iota(jnp.int32, (slabs * height, entries), 0)
    lane_ids = lax.broadcasted_iota(jnp.int32, (WIDTH, entries), 0)
    plane = height * WIDTH

    def one_block(start):
        for k in range(block):
            table = entries_ref[start + k]
            owner = table[0:1].astype(jnp.int32)
            cell = table[1:2].astype(jnp.int32)
            power = table[2:3]
            rest = cell % plane
            row = (owner * layers + cell // plane - base) * height + rest // WIDTH
            lane = rest % WIDTH
            high = power.astype(jnp.bfloat16).astype(F32)
            low = power - high
            here = slice(k * entries, (k + 1) * entries)
            rows_ref[:, here] = jnp.where(row_ids == row, 1.0, 0.0).astype(jnp.bfloat16)
            match = lane_ids == lane
            lanes_ref[0:WIDTH, here] = jnp.where(match, high, 0.0).astype(jnp.bfloat16)
            lanes_ref[WIDTH:, here] = jnp.where(match, low, 0.0).astype(jnp.bfloat16)
        return lax.dot_general(
            rows_ref[...], lanes_ref[...], (((1,), (1,)), ((), ())), preferred_element_type=F32
        )

    total = one_block(0)
    if sources > block:
        total_ref[...] = total

        @pl.loop(1, sources // block)
        def _(step):
            total_ref[...] += one_block(step * block)

        total = total_ref[...]
    heat = total[:, :WIDTH] + total[:, WIDTH:]
    heat_ref[...] = heat.reshape(heat_ref.shape)


def scatter_heat(entries, layers, height):
    sources, _, count = entries.shape
    block = min(sources, 16)
    slabs = layers + 2 * HALO
    return pl.pallas_call(
        functools.partial(heater_kernel, layers=layers, height=height, block=block),
        out_shape=jax.ShapeDtypeStruct((slabs, height, WIDTH), F32),
        in_specs=[pl.BlockSpec(memory_space=pltpu.VMEM)],
        out_specs=pl.BlockSpec(memory_space=pltpu.VMEM),
        scratch_shapes=[
            pltpu.VMEM((slabs * height, block * count), jnp.bfloat16),
            pltpu.VMEM((2 * WIDTH, block * count), jnp.bfloat16),
            pltpu.VMEM((slabs * height, 2 * WIDTH), F32),
        ],
        name="heater_scatter",
    )(entries)


def main_kernel(
    density_ref, anchor_ref, port_ref, own_z_ref, first_ref, first_z_ref, second_ref, second_z_ref,
    far_ref, far_z_ref, heat_ref, heat_z_ref,
    source_ref, applied_ref, force_ref, image_ref, image2_ref, pimage_ref, pimage2_ref, sums_ref,
    cub, stress, src, prt, force, image,
):
    height = density_ref.shape[1]
    gx = lax.axis_index("gx")
    gz = lax.axis_index("gz")
    last_x = lax.axis_size("gx") - 1
    last_z = lax.axis_size("gz") - 1
    even = gx % 2 == 0
    low_pair = gx % 4 < 2

    def flag(condition):
        return jnp.where(condition, 1.0, 0.0).astype(F32)

    tile = (height, WIDTH)
    lanes = lax.broadcasted_iota(jnp.int32, tile, 1)
    is_last = lanes == WIDTH - 1
    is_first = lanes == 0
    z_valid = jnp.where(lanes < WIDTH // 2, flag(gz < last_z), flag(gz > 0))
    x_valid = [
        flag(gx >= 2), flag(gx >= 1), flag(gx >= 1), None, None,
        flag(gx < last_x), flag(gx < last_x), flag(gx < last_x - 1),
    ]
    symmetry = flag(gx > 0)

    def masked(side, layer, value):
        if side:
            value = value * z_valid
        if x_valid[layer] is not None:
            value = value * x_valid[layer]
        return value

    def load(ref, side, layer, shift=0):
        return ref[side, layer, EDGE + shift : EDGE + shift + height, :]

    def store(ref, side, layer, value):
        ref[side, layer, EDGE : EDGE + height, :] = value

    def z_up(pair):
        a, b = (pltpu.roll(v, WIDTH - 1, 1) for v in pair)
        return jnp.where(is_last, b, a), jnp.where(is_last, a, b)

    def z_down(pair):
        a, b = (pltpu.roll(v, 1, 1) for v in pair)
        return jnp.where(is_first, b, a), jnp.where(is_first, a, b)

    edge_rows = jnp.zeros((EDGE, WIDTH), F32)
    for ref in (cub, stress, src, prt, force, image):
        for side in range(2):
            for layer in range(ref.shape[1]):
                ref[side, layer, 0:EDGE, :] = edge_rows
                ref[side, layer, EDGE + height :, :] = edge_rows

    def lower(side, k):
        a, b = (first_z_ref, second_z_ref) if side else (first_ref, second_ref)
        return jnp.where(even, b[k], a[k])

    def upper(side, k):
        a, b = (first_z_ref, second_z_ref) if side else (first_ref, second_ref)
        return jnp.where(even, a[k], b[k])

    def far(side, low):
        ref = far_z_ref if side else far_ref
        return jnp.where(low_pair, ref[1], ref[0]) if low else jnp.where(low_pair, ref[0], ref[1])

    def density_of(side, layer):
        if layer == 0:
            return far(side, True)
        if layer == 7:
            return far(side, False)
        if layer in (1, 2):
            return lower(side, layer - 1)
        if layer in (5, 6):
            return upper(side, layer - 5)
        return own_z_ref[layer - 3] if side else density_ref[layer - 3]

    def port_of(side, layer):
        if layer in (1, 2):
            return lower(side, layer + 1)
        if layer in (5, 6):
            return upper(side, layer - 3)
        return own_z_ref[layer - 1] if side else port_ref[layer - 3].astype(F32)

    def anchor_of(side, layer):
        if layer == 2:
            return lower(side, 4)
        if layer == 5:
            return upper(side, 4)
        return own_z_ref[layer + 1] if side else anchor_ref[layer - 3].astype(F32)

    for layer in range(8):
        for side in range(2):
            d = masked(side, layer, density_of(side, layer))
            c = d * d * d
            heat = (heat_z_ref if side else heat_ref)[layer]
            s = masked(side, layer, JOULE_GAIN * (SIGMA_MIN + c) + heat)
            store(cub, side, layer, c)
            store(stress, side, layer, (MODULUS_MINIMUM + c) * s)
            if 2 <= layer <= 5:
                store(src, side, layer - 2, s)
            if side == 0 and layer in (3, 4):
                source_ref[layer - 3] = s
            if 1 <= layer <= 6:
                store(prt, side, layer - 1, masked(side, layer, port_of(side, layer)))
    for side in range(2):
        for layer, block in ((0, 1), (2, 0)):
            mirrored = jnp.where(gx == block, load(stress, side, layer + 1), load(stress, side, layer))
            store(stress, side, layer, mirrored)

    half = EXPANSION * 0.5
    for layer in range(1, 7):
        pair = [load(stress, side, layer) for side in range(2)]
        up, down = z_up(pair), z_down(pair)
        for side in range(2):
            parts = (
                load(stress, side, layer + 1) - load(stress, side, layer - 1),
                load(stress, side, layer, 1) - load(stress, side, layer, -1),
                up[side] - down[side],
            )
            for k in range(3):
                value = masked(side, layer, half * parts[k])
                store(force, side, k * 6 + layer - 1, value)
                if side == 0 and layer in (3, 4):
                    force_ref[k, layer - 3] = value

    def face(a, b):
        return MODULUS_MINIMUM + 0.5 * (a + b)

    sums = {}

    def accumulate(name, value):
        value = jnp.sum(value.reshape(height // 8, 8, WIDTH), axis=0)
        sums[name] = value if name not in sums else sums[name] + value

    def weights_of(layer):
        pair = [load(cub, side, layer) for side in range(2)]
        up, down = z_up(pair), z_down(pair)
        result = []
        for side in range(2):
            c = pair[side]
            x_low = face(load(cub, side, layer - 1), c)
            if layer == 3:
                x_low = x_low * symmetry
            result.append(
                (
                    x_low,
                    face(load(cub, side, layer + 1), c),
                    face(load(cub, side, layer, -1), c),
                    face(load(cub, side, layer, 1), c),
                    face(down[side], c),
                    face(up[side], c),
                )
            )
        return result

    def differences(ref, index, sides):
        pair = [load(ref, side, index) for side in range(2)]
        up, down = z_up(pair), z_down(pair)
        result = []
        for side in sides:
            v = pair[side]
            result.append(
                (
                    v,
                    (
                        v - load(ref, side, index - 1),
                        v - load(ref, side, index + 1),
                        v - load(ref, side, index, -1),
                        v - load(ref, side, index, 1),
                        v - down[side],
                        v - up[side],
                    ),
                )
            )
        return result

    def weighted(weights, parts):
        total = weights[0] * parts[0]
        for w, p in zip(weights[1:], parts[1:]):
            total = total + w * p
        return total

    own_weights, own_anchor = {}, {}
    spread = KAPPA_MIN - MODULUS_MINIMUM
    for layer in range(2, 6):
        weights = weights_of(layer)
        anchors = [PENALTY * anchor_of(side, layer) for side in range(2)]
        own = layer in (3, 4)
        if own:
            own_weights[layer], own_anchor[layer] = weights[0], anchors[0]
        for k in range(4):
            ref, index = (force, k * 6 + layer - 1) if k < 3 else (prt, layer - 1)
            for side, (v, parts) in enumerate(differences(ref, index, range(2))):
                flux = weighted(weights[side], parts)
                value = masked(side, layer, flux + anchors[side] * v)
                store(image, side, k * 4 + layer - 2, value)
                if own and side == 0:
                    if k < 3:
                        image_ref[k, layer - 3] = value
                        accumulate("n0", v * v)
                        accumulate("m0", v * value)
                    else:
                        pimage_ref[layer - 3] = value
                        accumulate("n1", v * v)
                        accumulate("m1", v * value)
                        first = parts[0] * symmetry if layer == 3 else parts[0]
                        plain = first + parts[1] + parts[2] + parts[3] + parts[4] + parts[5]
                        heat_image = flux + spread * plain + CONVECTION * v
                        applied_ref[1, layer - 3] = heat_image
                        accumulate("k1", v * heat_image)
        if own:
            v, parts = differences(src, layer - 2, (0,))[0]
            heat_weights = [w + spread for w in weights[0]]
            if layer == 3:
                heat_weights[0] = weights[0][0] + spread * symmetry
            heat_image = weighted(heat_weights, parts) + CONVECTION * v
            applied_ref[0, layer - 3] = heat_image
            accumulate("k", v * heat_image)
            accumulate("q", v * v)

    def total(value):
        return jnp.sum(jnp.sum(value, axis=0, keepdims=True), axis=1, keepdims=True)

    final = {name: total(sums[name]) for name in ("n0", "m0", "n1", "m1", "k", "q", "k1")}
    shift = []
    for member in range(2):
        n, m = final["n%d" % member], final["m%d" % member]
        shift.append(jnp.where(n > 0.0, m / jnp.where(n > 0.0, n, 1.0), 0.0))
    for layer in (3, 4):
        for k in range(4):
            v, parts = differences(image, k * 4 + layer - 2, (0,))[0]
            value = weighted(own_weights[layer], parts) + own_anchor[layer] * v
            if k < 3:
                image2_ref[k, layer - 3] = value
                start = load(force, 0, k * 6 + layer - 1)
            else:
                pimage2_ref[layer - 3] = value
                start = load(prt, 0, layer - 1)
            theta = shift[k // 3]
            r = v - theta * start
            y = value - theta * v
            accumulate("s%d" % (k // 3), r * r)
            accumulate("t%d" % (k // 3), r * y)
            accumulate("c%d" % (k // 3), start * y)
    for member in range(2):
        for name in "stc":
            final[name + str(member)] = total(sums[name + str(member)])
    columns = (
        final["q"], final["k"], final["n1"], final["k1"],
        final["n0"], final["m0"], final["s0"], final["t0"], final["c0"] + final["s0"],
        final["n1"], final["m1"], final["s1"], final["t1"], final["c1"] + final["s1"],
    )
    lane = lax.broadcasted_iota(jnp.int32, (1, WIDTH), 1)
    row = jnp.zeros((1, WIDTH), F32)
    for k, column in enumerate(columns):
        row = jnp.where(lane == k, column, row)
    sums_ref[...] = jnp.broadcast_to(row[None], sums_ref.shape)


def main_stage(arguments, devices, layers, height):
    own = (layers, height, WIDTH)
    vectors = (3,) + own
    shapes = [own, (2,) + own, vectors, vectors, vectors, own, own, (devices, 1, WIDTH)]

    def field(count):
        return pltpu.VMEM((2, count, height + 2 * EDGE, WIDTH), F32)

    vmem = pl.BlockSpec(memory_space=pltpu.VMEM)
    return pl.pallas_call(
        main_kernel,
        out_shape=[jax.ShapeDtypeStruct(s, F32) for s in shapes],
        in_specs=[vmem] * len(arguments),
        out_specs=[vmem] * len(shapes),
        scratch_shapes=[field(8), field(8), field(4), field(6), field(18), field(16)],
        name="operators",
    )(*arguments)


def final_kernel(
    table_ref, source_ref, port_ref, applied_ref, force_ref, image_ref, image2_ref, pimage_ref, pimage2_ref,
    temperature_ref, adjoint_ref, displacement_ref, displacement_adjoint_ref, thermal_ref, elastic_ref,
):
    table = table_ref[...].reshape(table_ref.shape[0], WIDTH)

    def column(k):
        return table[:, k : k + 1]

    def total(value):
        return jnp.sum(value, axis=0, keepdims=True)

    step0 = total(column(0)) / total(column(1))
    step1 = total(column(2)) / total(column(3))

    def solve(first):
        n_all, m_all = column(first), column(first + 1)
        n, m = total(n_all), total(m_all)
        theta = m / n
        local = jnp.where(n_all > 0.0, m_all / jnp.where(n_all > 0.0, n_all, 1.0), 0.0)
        gap = local - theta
        s = total(column(first + 2) + gap * gap * n_all)
        t = total(column(first + 3) + gap * column(first + 4) + gap * gap * m_all)
        alpha0 = n / m
        beta = s * alpha0 * alpha0 / n
        alpha1 = s / (t - s * s / m)
        return alpha0, beta, alpha1

    def outcome(coefficients, b, w, u):
        alpha0, beta, alpha1 = coefficients
        r = b - alpha0 * w
        x = alpha0 * b + alpha1 * (r + beta * b)
        r = r - alpha1 * ((w - alpha0 * u) + beta * w)
        return x, r

    forward, adjoint = solve(4), solve(9)
    for layer in range(source_ref.shape[0]):
        source = source_ref[layer]
        port = port_ref[layer].astype(F32)
        temperature_ref[layer] = step0 * source
        adjoint_ref[layer] = step1 * port
        thermal_ref[0, layer] = source - step0 * applied_ref[0, layer]
        thermal_ref[1, layer] = port - step1 * applied_ref[1, layer]
        for k in range(3):
            x, r = outcome(forward, force_ref[k, layer], image_ref[k, layer], image2_ref[k, layer])
            displacement_ref[k, layer] = step0 * x
            elastic_ref[0, k, layer] = step0 * r
        x, r = outcome(adjoint, port, pimage_ref[layer], pimage2_ref[layer])
        for k in range(3):
            displacement_adjoint_ref[k, layer] = PORT_DIRECTION[k] * x
            elastic_ref[1, k, layer] = PORT_DIRECTION[k] * r


def final_stage(arguments, layers, height):
    own = (layers, height, WIDTH)
    shapes = [own, own, (3,) + own, (3,) + own, (2,) + own, (2, 3) + own]
    vmem = pl.BlockSpec(memory_space=pltpu.VMEM)
    return pl.pallas_call(
        final_kernel,
        out_shape=[jax.ShapeDtypeStruct(s, F32) for s in shapes],
        in_specs=[vmem] * len(arguments),
        out_specs=[vmem] * len(shapes),
        name="outputs",
    )(*arguments)


def per_device(density, anchor_mask, port_mask, heater_owner, heater_cell, heater_power):
    layers, height, _ = density.shape
    count = lax.axis_size("gx")
    devices = count * lax.axis_size("gz")
    gx = lax.axis_index("gx")
    entries = jnp.stack(
        [heater_owner.reshape(-1).astype(F32), heater_cell.reshape(-1).astype(F32), heater_power.reshape(-1)]
    )
    entries = lax.all_to_all(
        jnp.broadcast_to(entries[None], (count,) + entries.shape), "gx", 0, 0, tiled=True
    )
    port = port_mask.astype(F32)
    anchor = anchor_mask.astype(F32)
    even = gx % 2 == 0
    low_pair = gx % 4 < 2
    core = jnp.concatenate([density, port])
    first = jnp.concatenate([core, jnp.where(even, anchor[1:2], anchor[0:1])])
    second = jnp.concatenate([core, jnp.where(even, anchor[0:1], anchor[1:2])])
    far_one = jnp.where(low_pair, density[1:2], density[0:1])
    far_two = jnp.where(low_pair, density[0:1], density[1:2])
    first = lax.ppermute(first, "gx", swap_pairs(count, 0, 1))
    second = lax.ppermute(second, "gx", swap_pairs(count, 1, 1))
    far_one = lax.ppermute(far_one, "gx", swap_pairs(count, 0, 2))
    far_two = lax.ppermute(far_two, "gx", swap_pairs(count, 2, 2))
    far = jnp.concatenate([far_one, far_two])
    own_z = across_z(jnp.concatenate([core, anchor]))
    first_z = across_z(first)
    second_z = across_z(second)
    far_z = across_z(far)
    heat = scatter_heat(entries, layers, height)
    heat_z = across_z(heat)
    source, applied, force, image, image2, pimage, pimage2, sums = main_stage(
        (density, anchor_mask, port_mask, own_z, first, first_z, second, second_z, far, far_z, heat, heat_z),
        devices, layers, height,
    )
    table = lax.all_to_all(sums, ("gx", "gz"), 0, 0, tiled=True)
    return tuple(
        final_stage(
            (table, source, port_mask, applied, force, image, image2, pimage, pimage2), layers, height
        )
    )


def solution(mesh):
    in_specs = (
        P("gx", None, "gz"),
        P("gx", None, "gz"),
        P("gx", None, "gz"),
        P("gx", "gz", None, None),
        P("gx", "gz", None),
        P("gx", "gz", None),
    )
    out_specs = (
        P("gx", None, "gz"),
        P("gx", None, "gz"),
        P(None, "gx", None, "gz"),
        P(None, "gx", None, "gz"),
        P(None, "gx", None, "gz"),
        P(None, None, "gx", None, "gz"),
    )
    return jax.shard_map(
        per_device, mesh=mesh, in_specs=in_specs, out_specs=out_specs, check_vma=False
    )
```

time: 273 us -> 49.3 us (0.18)
  blocking collectives: 157 us -> 11.8 us
  other arithmetic: 32.8 us -> 0.77 us
  waiting for transfers between devices: 30.3 us -> 3.06 us
  starting transfers between devices: 44.2 us -> 18.5 us
  Pallas kernels: 0 us -> 9.6 us
    psum x3 -> x0, blocking collectives: 117 us -> none  [the longest x2 79.3 us: joint_products(): lax.psum((inner_products(values, values), inner_products(values, image_va...]
    all_gather x1 -> x0, blocking collectives: 39.7 us -> none  [deliver_heat(): everyone = lax.all_gather(entry_lists, 'gx', axis=1, tiled=True)]
    ppermute x20 -> x9, starting transfers between devices: 44.2 us -> 10 us  [the longest x1 4.68 us: per_device(): far_one = lax.ppermute(far_one, 'gx', swap_pairs(count, 0, 2))]
    ppermute x20 -> x9, waiting for transfers between devices: 30.3 us -> 3.05 us  [the longest x1 2.13 us: per_device(): first = lax.ppermute(first, 'gx', swap_pairs(count, 0, 1))]
    scatter-add x1 -> x0, other arithmetic: 21.9 us -> none  [deliver_heat(): heater = jnp.zeros((cells_total,), jnp.float32).at[targets].add(amounts)]
    all_to_all x0 -> x1, blocking collectives: none -> 11.8 us  [per_device(): table = lax.all_to_all(sums, ('gx', 'gz'), 0, 0, tiled=True)]
    pallas_call x0 -> x3, Pallas kernels: none -> 9.6 us  [the longest x1 3.97 us: main_stage(): pl.pallas_call(main_kernel, out_shape=[jax.ShapeDtypeStruct(s, F32) for s...]
    all_to_all x0 -> x1, starting transfers between devices: none -> 8.47 us  [per_device(): lax.all_to_all(jnp.broadcast_to(entries[None], (count,) + entries.shape),...]
  transfers between devices with their start and end apart: 20 -> 10, of which waited for: 11 -> 2; matrix products, arithmetic and copies ran while one was open for 10% -> 0% of each run, Pallas kernels for 0% -> 6%
where the time goes in v1:
time: 49.3 us; the launch traced here: 48.9 us
  starting transfers between devices  18.5 us (38%)
  blocking collectives  11.8 us (24%)
  Pallas kernels  9.6 us (19%)
  local copies, waits for them, and re-layouts  4.26 us (9%)
  waiting for transfers between devices  3.06 us (6%)
  between operations  0.84 us (2%)
  other arithmetic  0.77 us (2%)
    all_to_all x1, blocking collectives, per_device(): table = lax.all_to_all(sums, ('gx', 'gz'), 0, 0, tiled=True)  11.8 us
    all_to_all x1, starting transfers between devices, per_device(): lax.all_to_all(jnp.broadcast_to(entries[None], (count,) + entries.shape),...  8.47 us
    ppermute x1, starting transfers between devices, per_device(): far_one = lax.ppermute(far_one, 'gx', swap_pairs(count, 0, 2))  4.68 us
    pallas_call x1, Pallas kernels, main_stage(): pl.pallas_call(main_kernel, out_shape=[jax.ShapeDtypeStruct(s, F32) for s...  3.97 us
    unnamed x29, local copies, waits for them, and re-layouts  3.61 us
    pallas_call x1, Pallas kernels, scatter_heat(): pl.pallas_call(functools.partial(heater_kernel, layers=layers, height=hei...  3.03 us
    ppermute x1, starting transfers between devices, per_device(): first = lax.ppermute(first, 'gx', swap_pairs(count, 0, 1))  2.8 us
    pallas_call x1, Pallas kernels, final_stage(): pl.pallas_call(final_kernel, out_shape=[jax.ShapeDtypeStruct(s, F32) for...  2.6 us
  transfers between devices with their start and end apart: 10, of which 2 were waited for; matrix products, arithmetic and copies ran while one was open for 0% of the time, Pallas kernels for 6%

profile of v1, /device:TPU:0, one launch (start us, length us, event | category | flops | bytes accessed | tf_op | source)
XLA Modules:
  0.0 48.9 jit_solution(17715414313289479324)
XLA Ops:
  0.6 0.7 %convert_bitcast_fusion.1 = f32[1,256]{1,0:T(1,128)S(1)} fusion(s32[1,1,256,1]{2,3,1,0:T(1,128)} %param.9), kind=kLoop, calls=%fused_computation.12 | loop fusion | flops 256 | bytes 2048 | tf_op jit(solution)/shard_map/convert_element_type | solution.py:456
  1.3 0.7 %copy-done.12 = f32[1,1,256]{2,1,0:T(1,128)S(1)} copy-done((f32[1,1,256]{2,1,0:T(1,128)S(1)}, f32[1,1,256]{2,1,0:T(1,128)}, u32[]{:S(2)}) %copy-start.12) | copy-done | bytes 1048
  2.0 0.6 %broadcast_in_dim.2 = f32[16,3,256]{2,1,0:T(4,128)} broadcast(f32[3,256]{1,0:T(4,128)S(1)} %pad_maximum_fusion.4), dimensions={1,2} | broadcast | bytes 52224 | tf_op jit(solution)/shard_map/broadcast_in_dim | solution.py:459
  2.7 8.5 %all-to-all-start = ((f32[16,3,256]{2,1,0:T(4,128)}), f32[16,3,256]{2,1,0:T(4,128)S(1)}, u32[]{:S(2)}, u32[]{:S(2)}) async-start(f32[16,3,256]{2,1,0:T(4,128)} %broadcast_in_dim.2), calls=%async_computation | async-start | bytes 131072 | tf_op jit(solution)/shard_map/all_to_all | solution.py:458
  11.2 0.7 %collective-permute-start.6 = (f32[1,64,128]{2,1,0:T(8,128)S(1)}, f32[1,64,128]{2,1,0:T(8,128)S(1)}, u32[]{:S(2)}, u32[]{:S(2)}) collective-permute-start(f32[1,64,128]{2,1,0:T(8,128)S(1)} %get-tuple-element.24), channel_id=1, source_target_pairs={{4,8},{8,4},{6,10},{10,6},{12,16},{16,12},{14,18},{18,14},{20,24},... | collective-permute-start | bytes 98312 | tf_op jit(solution)/shard_map/ppermute | solution.py:473
  11.9 4.7 %collective-permute-start.5 = (f32[1,64,128]{2,1,0:T(8,128)S(1)}, f32[1,64,128]{2,1,0:T(8,128)S(1)}, u32[]{:S(2)}, u32[]{:S(2)}) collective-permute-start(f32[1,64,128]{2,1,0:T(8,128)S(1)} %get-tuple-element.25), channel_id=1, source_target_pairs={{0,4},{4,0},{2,6},{6,2},{8,12},{12,8},{10,14},{14,10},{16,20},{20,... | collective-permute-start | bytes 98312 | tf_op jit(solution)/shard_map/ppermute | solution.py:472
  16.6 0.8 %copy-done.1 = s32[2,64,128]{2,1,0:T(8,128)S(1)} copy-done((s32[2,64,128]{2,1,0:T(8,128)S(1)}, s32[2,64,128]{2,1,0:T(8,128)}, u32[]{:S(2)}) %copy-start.1) | copy-done | bytes 65560
  17.4 0.7 %collective-permute-start.3 = (f32[5,64,128]{2,1,0:T(8,128)S(1)}, f32[5,64,128]{2,1,0:T(8,128)S(1)}, u32[]{:S(2)}, u32[]{:S(2)}) collective-permute-start(f32[5,64,128]{2,1,0:T(8,128)S(1)} %get-tuple-element.22), channel_id=1, source_target_pairs={{2,4},{4,2},{6,8},{8,6},{10,12},{12,10},{14,16},{16,14},{18,20},{2... | collective-permute-start | bytes 491528 | tf_op jit(solution)/shard_map/ppermute | solution.py:471
  18.1 2.8 %collective-permute-start.1 = (f32[5,64,128]{2,1,0:T(8,128)S(1)}, f32[5,64,128]{2,1,0:T(8,128)S(1)}, u32[]{:S(2)}, u32[]{:S(2)}) collective-permute-start(f32[5,64,128]{2,1,0:T(8,128)S(1)} %get-tuple-element.23), channel_id=1, source_target_pairs={{0,2},{2,0},{4,6},{6,4},{8,10},{10,8},{12,14},{14,12},{16,18},{18,... | collective-permute-start | bytes 491528 | tf_op jit(solution)/shard_map/ppermute | solution.py:470
  20.9 0.1 collective-permute-start
  21.0 0.6 %copy-done.2 = f32[16,3,256]{2,1,0:T(4,128)} copy-done((f32[16,3,256]{2,1,0:T(4,128)}, f32[16,3,256]{2,1,0:T(4,128)S(1)}, u32[]{:S(2)}) %copy-start.2) | copy-done | bytes 49176
  21.7 3.0 %heater_scatter.1.heat_ref = f32[8,64,128]{2,1,0:T(8,128)} custom-call(f32[16,3,256]{2,1,0:T(4,128)} %copy-done.2), custom_call_target="tpu_custom_call" | custom-call | tf_op jit(solution)/shard_map/heater_scatter/pallas_call | solution.py:89
  24.7 0.5 collective-permute-start.8
  25.2 0.1 collective-permute-start.4
  25.3 2.1 %collective-permute-done.1.first_ref = f32[5,64,128]{2,1,0:T(8,128)S(1)} collective-permute-done((f32[5,64,128]{2,1,0:T(8,128)S(1)}, f32[5,64,128]{2,1,0:T(8,128)S(1)}, u32[]{:S(2)}, u32[]{:S(2)}) %collective-permute-start.1) | collective-permute-done | bytes 163872 | tf_op jit(solution)/shard_map/ppermute | solution.py:470
  27.5 0.6 %collective-permute-start.7 = (f32[2,64,128]{2,1,0:T(8,128)S(1)}, f32[2,64,128]{2,1,0:T(8,128)S(1)}, u32[]{:S(2)}, u32[]{:S(2)}) collective-permute-start(f32[2,64,128]{2,1,0:T(8,128)S(1)} %constant_dynamic-update-slice_fusion.far_ref), channel_id=1, source_target_pairs={{0,1},{1,0},{2,3},{3,2},{4,5},{5,4},{6,7},{7,6},{8,9},{9,8},{10,11... | collective-permute-start | bytes 196616 | tf_op jit(solution)/shard_map/ppermute | solution.py:36
  28.0 0.9 %collective-permute-done.7.far_z_ref = f32[2,64,128]{2,1,0:T(8,128)S(1)} collective-permute-done((f32[2,64,128]{2,1,0:T(8,128)S(1)}, f32[2,64,128]{2,1,0:T(8,128)S(1)}, u32[]{:S(2)}, u32[]{:S(2)}) %collective-permute-start.7) | collective-permute-done | bytes 65568 | tf_op jit(solution)/shard_map/ppermute | solution.py:36
  29.0 0.5 %copy-done.11 = f32[2,64,128]{2,1,0:T(8,128)} copy-done((f32[2,64,128]{2,1,0:T(8,128)}, f32[2,64,128]{2,1,0:T(8,128)S(1)}, u32[]{:S(2)}) %copy-start.11) | copy-done | bytes 65560
  29.6 0.1 copy-done.5
  29.7 0.1 copy-done.9
  29.7 0.7 %copy-done.3 = f32[8,64,128]{2,1,0:T(8,128)} copy-done((f32[8,64,128]{2,1,0:T(8,128)}, f32[8,64,128]{2,1,0:T(8,128)S(1)}, u32[]{:S(2)}) %copy-start.3) | copy-done | bytes 262168
  30.5 4.0 %operators.1 = (f32[2,64,128]{2,1,0:T(8,128)}, f32[2,2,64,128]{3,2,1,0:T(8,128)}, f32[3,2,64,128]{3,2,1,0:T(8,128)}, f32[3,2,64,128]{3,2,1,0:T(8,128)}, f32[3,2,...) custom-call(f32[2,64,128]{2,1,0:T(8,128)} %density_ref.1, ...), custom_call_target="tpu_custom_call" | custom-call | tf_op jit(solution)/shard_map/operators/pallas_call | solution.py:374
  34.4 11.8 %all_to_all.10.table_ref = f32[32,1,128]{2,1,0:T(1,128)} all-to-all(f32[32,1,128]{2,1,0:T(1,128)} %get-tuple-element.14), channel_id=1, replica_groups=mesh['gx'=16,'gz'=2] {'gx','gz'}, dimensions={0} | all-to-all | bytes 32768 | tf_op jit(solution)/shard_map/all_to_all | solution.py:485
  46.3 2.6 %outputs.1 = (f32[2,64,128]{2,1,0:T(8,128)}, f32[2,64,128]{2,1,0:T(8,128)}, f32[3,2,64,128]{3,2,1,0:T(8,128)}, f32[3,2,64,128]{3,2,1,0:T(8,128)}, f32[2,2,64,128...) custom-call(f32[32,1,128]{2,1,0:T(1,128)} %all_to_all.10.table_ref, f32[2,64,128]{2,1,0:T(8,128)} %get-tuple-element.15.source_ref, ...), custom_call_target="tpu_custom_call" | custom-call | tf_op jit(solution)/shard_map/outputs/pallas_call | solution.py:441
  (40 shorter events, 0.2 us)
Async XLA Ops:
  0.6 0.7 %copy-start.13 = (s32[1,1,256]{2,1,0:T(1,128)S(1)}, s32[1,1,256]{2,1,0:T(1,128)}, u32[]{:S(2)}) copy-start(s32[1,1,256]{2,1,0:T(1,128)} %param.10) | copy-start | bytes 3076
  1.3 0.7 %copy-start.12 = (f32[1,1,256]{2,1,0:T(1,128)S(1)}, f32[1,1,256]{2,1,0:T(1,128)}, u32[]{:S(2)}) copy-start(f32[1,1,256]{2,1,0:T(1,128)} %param.11) | copy-start | bytes 3076
  2.7 8.5 %copy-start = (f32[2,64,128]{2,1,0:T(8,128)S(1)}, f32[2,64,128]{2,1,0:T(8,128)}, u32[]{:S(2)}) copy-start(f32[2,64,128]{2,1,0:T(8,128)} %density_ref.1) | copy-start | bytes 196612
  2.7 18.4 %all-to-all-start = ((f32[16,3,256]{2,1,0:T(4,128)}), f32[16,3,256]{2,1,0:T(4,128)S(1)}, u32[]{:S(2)}, u32[]{:S(2)}) async-start(f32[16,3,256]{2,1,0:T(4,128)} %broadcast_in_dim.2), calls=%async_computation | async-start | bytes 131072 | tf_op jit(solution)/shard_map/all_to_all | solution.py:458
  11.2 5.4 %copy-start.4 = (s32[2,64,128]{2,1,0:T(8,128)S(1)}, s32[2,64,128]{2,1,0:T(8,128)}, u32[]{:S(2)}) copy-start(s32[2,64,128]{2,1,0:T(8,128)} %anchor_ref.1) | copy-start | bytes 196612
  11.2 16.2 %collective-permute-start.6 = (f32[1,64,128]{2,1,0:T(8,128)S(1)}, f32[1,64,128]{2,1,0:T(8,128)S(1)}, u32[]{:S(2)}, u32[]{:S(2)}) collective-permute-start(f32[1,64,128]{2,1,0:T(8,128)S(1)} %get-tuple-element.24), channel_id=1, source_target_pairs={{4,8},{8,4},{6,10},{10,6},{12,16},{16,12},{14,18},{18,14},{20,24},... | collective-permute-start | bytes 98312 | tf_op jit(solution)/shard_map/ppermute | solution.py:473
  11.9 12.8 %collective-permute-start.5 = (f32[1,64,128]{2,1,0:T(8,128)S(1)}, f32[1,64,128]{2,1,0:T(8,128)S(1)}, u32[]{:S(2)}, u32[]{:S(2)}) collective-permute-start(f32[1,64,128]{2,1,0:T(8,128)S(1)} %get-tuple-element.25), channel_id=1, source_target_pairs={{0,4},{4,0},{2,6},{6,2},{8,12},{12,8},{10,14},{14,10},{16,20},{20,... | collective-permute-start | bytes 98312 | tf_op jit(solution)/shard_map/ppermute | solution.py:472
  16.6 0.8 %copy-start.1 = (s32[2,64,128]{2,1,0:T(8,128)S(1)}, s32[2,64,128]{2,1,0:T(8,128)}, u32[]{:S(2)}) copy-start(s32[2,64,128]{2,1,0:T(8,128)} %port_ref.3) | copy-start | bytes 196612
  17.4 7.8 %collective-permute-start.3 = (f32[5,64,128]{2,1,0:T(8,128)S(1)}, f32[5,64,128]{2,1,0:T(8,128)S(1)}, u32[]{:S(2)}, u32[]{:S(2)}) collective-permute-start(f32[5,64,128]{2,1,0:T(8,128)S(1)} %get-tuple-element.22), channel_id=1, source_target_pairs={{2,4},{4,2},{6,8},{8,6},{10,12},{12,10},{14,16},{16,14},{18,20},{2... | collective-permute-start | bytes 491528 | tf_op jit(solution)/shard_map/ppermute | solution.py:471
  18.1 9.3 %collective-permute-start.1 = (f32[5,64,128]{2,1,0:T(8,128)S(1)}, f32[5,64,128]{2,1,0:T(8,128)S(1)}, u32[]{:S(2)}, u32[]{:S(2)}) collective-permute-start(f32[5,64,128]{2,1,0:T(8,128)S(1)} %get-tuple-element.23), channel_id=1, source_target_pairs={{0,2},{2,0},{4,6},{6,4},{8,10},{10,8},{12,14},{14,12},{16,18},{18,... | collective-permute-start | bytes 491528 | tf_op jit(solution)/shard_map/ppermute | solution.py:470
  20.9 8.0 %collective-permute-start = (f32[6,64,128]{2,1,0:T(8,128)S(1)}, f32[6,64,128]{2,1,0:T(8,128)S(1)}, u32[]{:S(2)}, u32[]{:S(2)}) collective-permute-start(f32[6,64,128]{2,1,0:T(8,128)S(1)} %pad_maximum_fusion), channel_id=1, source_target_pairs={{0,1},{1,0},{2,3},{3,2},{4,5},{5,4},{6,7},{7,6},{8,9},{9,8},{10,11... | collective-permute-start | bytes 589832 | tf_op jit(solution)/shard_map/ppermute | solution.py:36
  21.0 0.6 %copy-start.2 = (f32[16,3,256]{2,1,0:T(4,128)}, f32[16,3,256]{2,1,0:T(4,128)S(1)}, u32[]{:S(2)}) copy-start(f32[16,3,256]{2,1,0:T(4,128)S(1)} %all-to-all-done.entries_ref) | copy-start | bytes 147460
  24.7 4.3 %collective-permute-start.8 = (f32[8,64,128]{2,1,0:T(8,128)}, f32[8,64,128]{2,1,0:T(8,128)S(1)}, u32[]{:S(2)}, u32[]{:S(2)}) collective-permute-start(f32[8,64,128]{2,1,0:T(8,128)} %heater_scatter.1.heat_ref), channel_id=1, source_target_pairs={{0,1},{1,0},{2,3},{3,2},{4,5},{5,4},{6,7},{7,6},{8,9},{9,8},{10,11... | collective-permute-start | bytes 786440 | tf_op jit(solution)/shard_map/ppermute | solution.py:36
  25.2 3.8 %copy-start.6 = (f32[5,64,128]{2,1,0:T(8,128)}, f32[5,64,128]{2,1,0:T(8,128)S(1)}, u32[]{:S(2)}) copy-start(f32[5,64,128]{2,1,0:T(8,128)S(1)} %collective-permute-done.3.second_ref) | copy-start | bytes 491524
  25.2 3.7 %collective-permute-start.4 = (f32[5,64,128]{2,1,0:T(8,128)S(1)}, f32[5,64,128]{2,1,0:T(8,128)S(1)}, u32[]{:S(2)}, u32[]{:S(2)}) collective-permute-start(f32[5,64,128]{2,1,0:T(8,128)S(1)} %collective-permute-done.3.second_ref), channel_id=1, source_target_pairs={{0,1},{1,0},{2,3},{3,2},{4,5},{5,4},{6,7},{7,6},{8,9},{9,8},{10,11... | collective-permute-start | bytes 491528 | tf_op jit(solution)/shard_map/ppermute | solution.py:36
  27.4 1.6 %copy-start.7 = (f32[5,64,128]{2,1,0:T(8,128)}, f32[5,64,128]{2,1,0:T(8,128)S(1)}, u32[]{:S(2)}) copy-start(f32[5,64,128]{2,1,0:T(8,128)S(1)} %collective-permute-done.1.first_ref) | copy-start | bytes 491524
  27.4 1.5 %collective-permute-start.2 = (f32[5,64,128]{2,1,0:T(8,128)S(1)}, f32[5,64,128]{2,1,0:T(8,128)S(1)}, u32[]{:S(2)}, u32[]{:S(2)}) collective-permute-start(f32[5,64,128]{2,1,0:T(8,128)S(1)} %collective-permute-done.1.first_ref), channel_id=1, source_target_pairs={{0,1},{1,0},{2,3},{3,2},{4,5},{5,4},{6,7},{7,6},{8,9},{9,8},{10,11... | collective-permute-start | bytes 491528 | tf_op jit(solution)/shard_map/ppermute | solution.py:36
  27.4 1.5 %copy-start.10 = (f32[2,64,128]{2,1,0:T(8,128)}, f32[2,64,128]{2,1,0:T(8,128)S(1)}, u32[]{:S(2)}) copy-start(f32[2,64,128]{2,1,0:T(8,128)S(1)} %constant_dynamic-update-slice_fusion.far_ref) | copy-start | bytes 196612
  27.5 1.5 %collective-permute-start.7 = (f32[2,64,128]{2,1,0:T(8,128)S(1)}, f32[2,64,128]{2,1,0:T(8,128)S(1)}, u32[]{:S(2)}, u32[]{:S(2)}) collective-permute-start(f32[2,64,128]{2,1,0:T(8,128)S(1)} %constant_dynamic-update-slice_fusion.far_ref), channel_id=1, source_target_pairs={{0,1},{1,0},{2,3},{3,2},{4,5},{5,4},{6,7},{7,6},{8,9},{9,8},{10,11... | collective-permute-start | bytes 196616 | tf_op jit(solution)/shard_map/ppermute | solution.py:36
  28.9 0.6 %copy-start.11 = (f32[2,64,128]{2,1,0:T(8,128)}, f32[2,64,128]{2,1,0:T(8,128)S(1)}, u32[]{:S(2)}) copy-start(f32[2,64,128]{2,1,0:T(8,128)S(1)} %collective-permute-done.7.far_z_ref) | copy-start | bytes 196612
  28.9 0.7 %copy-start.5 = (f32[6,64,128]{2,1,0:T(8,128)}, f32[6,64,128]{2,1,0:T(8,128)S(1)}, u32[]{:S(2)}) copy-start(f32[6,64,128]{2,1,0:T(8,128)S(1)} %collective-permute-done.own_z_ref) | copy-start | bytes 589828
  28.9 0.7 %copy-start.8 = (f32[5,64,128]{2,1,0:T(8,128)}, f32[5,64,128]{2,1,0:T(8,128)S(1)}, u32[]{:S(2)}) copy-start(f32[5,64,128]{2,1,0:T(8,128)S(1)} %collective-permute-done.4.second_z_ref) | copy-start | bytes 491524
  29.0 0.8 %copy-start.9 = (f32[5,64,128]{2,1,0:T(8,128)}, f32[5,64,128]{2,1,0:T(8,128)S(1)}, u32[]{:S(2)}) copy-start(f32[5,64,128]{2,1,0:T(8,128)S(1)} %collective-permute-done.2.first_z_ref) | copy-start | bytes 491524
  29.7 0.7 %copy-start.3 = (f32[8,64,128]{2,1,0:T(8,128)}, f32[8,64,128]{2,1,0:T(8,128)S(1)}, u32[]{:S(2)}) copy-start(f32[8,64,128]{2,1,0:T(8,128)S(1)} %collective-permute-done.8.heat_z_ref) | copy-start | bytes 786436

commit v2 on v1

--- a/solution.py
+++ b/solution.py
@@ -6,6 +6,7 @@
 from jax.experimental import pallas as pl
 from jax.experimental.pallas import tpu as pltpu
 from jax.sharding import PartitionSpec as P
+
 
 KAPPA_MIN = 0.05
 MODULUS_MINIMUM = 0.02
@@ -19,6 +20,7 @@
 HALO = 3
 WIDTH = 128
 EDGE = 8
+VMEM_LIMIT = 16 << 20
 F32 = jnp.float32
 
 
@@ -38,6 +40,72 @@
     lower = lax.ppermute(values, "gz", [(i, i + 1) for i in range(count - 1)])
     lanes = lax.broadcasted_iota(jnp.int32, values.shape, values.ndim - 1)
     return jnp.where(lanes < WIDTH // 2, upper, lower)
+
+
+def prepare_kernel(
+    density_hbm, anchor_hbm, port_hbm, owner_hbm, cell_hbm, power_hbm,
+    first_ref, second_ref, far_one_ref, far_two_ref, own_ref, entries_ref,
+    density_ref, anchor_ref, port_ref, owner_ref, cell_ref, power_ref, arrived,
+):
+    layers = density_ref.shape[0]
+    sources = (owner_hbm, cell_hbm, power_hbm, density_hbm, port_hbm, anchor_hbm)
+    targets = (owner_ref, cell_ref, power_ref, density_ref, port_ref, anchor_ref)
+    copies = [
+        pltpu.make_async_copy(source, target, arrived.at[k])
+        for k, (source, target) in enumerate(zip(sources, targets))
+    ]
+    for copy in copies:
+        copy.start()
+    gx = lax.axis_index("gx")
+    even = gx % 2 == 0
+    low_pair = gx % 4 < 2
+    for copy in copies[:3]:
+        copy.wait()
+    owner = owner_ref[...].astype(F32)
+    cell = cell_ref[...].astype(F32)
+    power = power_ref[...]
+    for k in range(entries_ref.shape[0]):
+        entries_ref[k, 0:1] = owner
+        entries_ref[k, 1:2] = cell
+        entries_ref[k, 2:3] = power
+    copies[3].wait()
+    for layer in range(layers):
+        density = density_ref[layer]
+        for ref in (first_ref, second_ref, own_ref):
+            ref[layer] = density
+    below, above = density_ref[0], density_ref[layers - 1]
+    far_one_ref[0] = jnp.where(low_pair, above, below)
+    far_two_ref[0] = jnp.where(low_pair, below, above)
+    copies[4].wait()
+    for layer in range(layers):
+        port = port_ref[layer].astype(F32)
+        for ref in (first_ref, second_ref, own_ref):
+            ref[layers + layer] = port
+    copies[5].wait()
+    for layer in range(layers):
+        own_ref[2 * layers + layer] = anchor_ref[layer].astype(F32)
+    below, above = anchor_ref[0].astype(F32), anchor_ref[layers - 1].astype(F32)
+    first_ref[2 * layers] = jnp.where(even, above, below)
+    second_ref[2 * layers] = jnp.where(even, below, above)
+
+
+def prepare(arguments, sources):
+    layers, height, _ = arguments[0].shape
+    plane = (height, WIDTH)
+    shapes = [
+        (2 * layers + 1,) + plane, (2 * layers + 1,) + plane, (1,) + plane, (1,) + plane,
+        (3 * layers,) + plane, (sources, 3, arguments[-1].shape[1]),
+    ]
+    return pl.pallas_call(
+        prepare_kernel,
+        out_shape=[jax.ShapeDtypeStruct(s, F32) for s in shapes],
+        in_specs=[pl.BlockSpec(memory_space=pltpu.HBM)] * len(arguments),
+        out_specs=[pl.BlockSpec(memory_space=pltpu.VMEM)] * len(shapes),
+        scratch_shapes=[pltpu.VMEM(a.shape, a.dtype) for a in arguments]
+        + [pltpu.SemaphoreType.DMA((len(arguments),))],
+        compiler_params=pltpu.CompilerParams(vmem_limit_bytes=VMEM_LIMIT),
+        name="prepare",
+    )(*arguments)
 
 
 def heater_kernel(entries_ref, heat_ref, rows_ref, lanes_ref, total_ref, *, layers, height, block):
@@ -96,17 +164,18 @@
             pltpu.VMEM((2 * WIDTH, block * count), jnp.bfloat16),
             pltpu.VMEM((slabs * height, 2 * WIDTH), F32),
         ],
+        compiler_params=pltpu.CompilerParams(vmem_limit_bytes=VMEM_LIMIT),
         name="heater_scatter",
     )(entries)
 
 
 def main_kernel(
-    density_ref, anchor_ref, port_ref, own_z_ref, first_ref, first_z_ref, second_ref, second_z_ref,
+    own_ref, own_z_ref, first_ref, first_z_ref, second_ref, second_z_ref,
     far_ref, far_z_ref, heat_ref, heat_z_ref,
     source_ref, applied_ref, force_ref, image_ref, image2_ref, pimage_ref, pimage2_ref, sums_ref,
     cub, stress, src, prt, force, image,
 ):
-    height = density_ref.shape[1]
+    height = own_ref.shape[1]
     gx = lax.axis_index("gx")
     gz = lax.axis_index("gz")
     last_x = lax.axis_size("gx") - 1
@@ -177,21 +246,21 @@
             return lower(side, layer - 1)
         if layer in (5, 6):
             return upper(side, layer - 5)
-        return own_z_ref[layer - 3] if side else density_ref[layer - 3]
+        return (own_z_ref if side else own_ref)[layer - 3]
 
     def port_of(side, layer):
         if layer in (1, 2):
             return lower(side, layer + 1)
         if layer in (5, 6):
             return upper(side, layer - 3)
-        return own_z_ref[layer - 1] if side else port_ref[layer - 3].astype(F32)
+        return (own_z_ref if side else own_ref)[layer - 1]
 
     def anchor_of(side, layer):
         if layer == 2:
             return lower(side, 4)
         if layer == 5:
             return upper(side, 4)
-        return own_z_ref[layer + 1] if side else anchor_ref[layer - 3].astype(F32)
+        return (own_z_ref if side else own_ref)[layer + 1]
 
     for layer in range(8):
         for side in range(2):
@@ -377,12 +446,13 @@
         in_specs=[vmem] * len(arguments),
         out_specs=[vmem] * len(shapes),
         scratch_shapes=[field(8), field(8), field(4), field(6), field(18), field(16)],
+        compiler_params=pltpu.CompilerParams(vmem_limit_bytes=VMEM_LIMIT),
         name="operators",
     )(*arguments)
 
 
 def final_kernel(
-    table_ref, source_ref, port_ref, applied_ref, force_ref, image_ref, image2_ref, pimage_ref, pimage2_ref,
+    table_ref, source_ref, own_ref, applied_ref, force_ref, image_ref, image2_ref, pimage_ref, pimage2_ref,
     temperature_ref, adjoint_ref, displacement_ref, displacement_adjoint_ref, thermal_ref, elastic_ref,
 ):
     table = table_ref[...].reshape(table_ref.shape[0], WIDTH)
@@ -419,7 +489,7 @@
     forward, adjoint = solve(4), solve(9)
     for layer in range(source_ref.shape[0]):
         source = source_ref[layer]
-        port = port_ref[layer].astype(F32)
+        port = own_ref[source_ref.shape[0] + layer]
         temperature_ref[layer] = step0 * source
         adjoint_ref[layer] = step1 * port
         thermal_ref[0, layer] = source - step0 * applied_ref[0, layer]
@@ -443,6 +513,7 @@
         out_shape=[jax.ShapeDtypeStruct(s, F32) for s in shapes],
         in_specs=[vmem] * len(arguments),
         out_specs=[vmem] * len(shapes),
+        compiler_params=pltpu.CompilerParams(vmem_limit_bytes=VMEM_LIMIT),
         name="outputs",
     )(*arguments)
 
@@ -451,41 +522,29 @@
     layers, height, _ = density.shape
     count = lax.axis_size("gx")
     devices = count * lax.axis_size("gz")
-    gx = lax.axis_index("gx")
-    entries = jnp.stack(
-        [heater_owner.reshape(-1).astype(F32), heater_cell.reshape(-1).astype(F32), heater_power.reshape(-1)]
-    )
-    entries = lax.all_to_all(
-        jnp.broadcast_to(entries[None], (count,) + entries.shape), "gx", 0, 0, tiled=True
-    )
-    port = port_mask.astype(F32)
-    anchor = anchor_mask.astype(F32)
-    even = gx % 2 == 0
-    low_pair = gx % 4 < 2
-    core = jnp.concatenate([density, port])
-    first = jnp.concatenate([core, jnp.where(even, anchor[1:2], anchor[0:1])])
-    second = jnp.concatenate([core, jnp.where(even, anchor[0:1], anchor[1:2])])
-    far_one = jnp.where(low_pair, density[1:2], density[0:1])
-    far_two = jnp.where(low_pair, density[0:1], density[1:2])
+    heaters = tuple(a.reshape(1, -1) for a in (heater_owner, heater_cell, heater_power))
+    heaters = tuple(pltpu.with_memory_space_constraint(a, pltpu.HBM) for a in (density, anchor_mask, port_mask) + heaters)
+    first, second, far_one, far_two, own, entries = prepare(heaters, count)
     first = lax.ppermute(first, "gx", swap_pairs(count, 0, 1))
     second = lax.ppermute(second, "gx", swap_pairs(count, 1, 1))
+    entries = lax.all_to_all(entries, "gx", 0, 0, tiled=True)
     far_one = lax.ppermute(far_one, "gx", swap_pairs(count, 0, 2))
     far_two = lax.ppermute(far_two, "gx", swap_pairs(count, 2, 2))
     far = jnp.concatenate([far_one, far_two])
-    own_z = across_z(jnp.concatenate([core, anchor]))
+    own_z = across_z(own)
     first_z = across_z(first)
     second_z = across_z(second)
     far_z = across_z(far)
     heat = scatter_heat(entries, layers, height)
     heat_z = across_z(heat)
     source, applied, force, image, image2, pimage, pimage2, sums = main_stage(
-        (density, anchor_mask, port_mask, own_z, first, first_z, second, second_z, far, far_z, heat, heat_z),
+        (own, own_z, first, first_z, second, second_z, far, far_z, heat, heat_z),
         devices, layers, height,
     )
     table = lax.all_to_all(sums, ("gx", "gz"), 0, 0, tiled=True)
     return tuple(
         final_stage(
-            (table, source, port_mask, applied, force, image, image2, pimage, pimage2), layers, height
+            (table, source, own, applied, force, image, image2, pimage, pimage2), layers, height
         )
     )
 
@@ -507,6 +566,4 @@
         P(None, "gx", None, "gz"),
         P(None, None, "gx", None, "gz"),
     )
-    return jax.shard_map(
-        per_device, mesh=mesh, in_specs=in_specs, out_specs=out_specs, check_vma=False
-    )
+    return jax.shard_map(per_device, mesh=mesh, in_specs=in_specs, out_specs=out_specs, check_vma=False)

time: 49.3 us -> 39.5 us (0.80)
  local copies, waits for them, and re-layouts: 4.26 us -> 0.01 us
  Pallas kernels: 9.6 us -> 6.3 us
  starting transfers between devices: 18.5 us -> 15.6 us
  blocking collectives: 11.8 us -> 13.6 us
  other arithmetic: 0.77 us -> 0 us
    unnamed x29 -> x1, local copies, waits for them, and re-layouts: 3.61 us -> 0.01 us
    ppermute x1, waiting for transfers between devices: 2.13 us -> 0.01 us  [per_device(): first = lax.ppermute(first, 'gx', swap_pairs(count, 0, 1))]
    pallas_call x1, Pallas kernels: 3.97 us -> 1.84 us  [main_stage(): pl.pallas_call(main_kernel, out_shape=[jax.ShapeDtypeStruct(s, F32) for s...]
    all_to_all x1, blocking collectives: 11.8 us -> 13.6 us  [per_device(): table = lax.all_to_all(sums, ('gx', 'gz'), 0, 0, tiled=True)]
    ppermute x1, starting transfers between devices: 4.68 us -> 2.93 us  [per_device(): far_one = lax.ppermute(far_one, 'gx', swap_pairs(count, 0, 2))]
    pallas_call x0 -> x1, Pallas kernels: none -> 1.63 us  [prepare(): pl.pallas_call(prepare_kernel, out_shape=[jax.ShapeDtypeStruct(s, F32) fo...]
    pallas_call x1, Pallas kernels: 3.03 us -> 1.49 us  [scatter_heat(): pl.pallas_call(functools.partial(heater_kernel, layers=layers, height=hei...]
    all_to_all x1, waiting for transfers between devices: 0.01 us -> 1.27 us  [per_device(): entries = lax.all_to_all(entries, 'gx', 0, 0, tiled=True)]
  transfers between devices with their start and end apart: 10 -> 10, of which waited for: 2 -> 3; matrix products, arithmetic and copies ran while one was open for 0% -> 0% of each run, Pallas kernels for 6% -> 4%
where the time goes in v2:
time: 39.5 us; the launch traced here: 39.2 us
  starting transfers between devices  15.6 us (39%)
  blocking collectives  13.6 us (34%)
  Pallas kernels  6.3 us (16%)
  waiting for transfers between devices  3.01 us (8%)
  between operations  0.71 us (2%)
    all_to_all x1, blocking collectives, per_device(): table = lax.all_to_all(sums, ('gx', 'gz'), 0, 0, tiled=True)  13.6 us
    all_to_all x1, starting transfers between devices, per_device(): entries = lax.all_to_all(entries, 'gx', 0, 0, tiled=True)  8.35 us
    ppermute x1, starting transfers between devices, per_device(): far_one = lax.ppermute(far_one, 'gx', swap_pairs(count, 0, 2))  2.93 us
    ppermute x1, starting transfers between devices, per_device(): first = lax.ppermute(first, 'gx', swap_pairs(count, 0, 1))  1.93 us
    pallas_call x1, Pallas kernels, main_stage(): pl.pallas_call(main_kernel, out_shape=[jax.ShapeDtypeStruct(s, F32) for s...  1.84 us
    pallas_call x1, Pallas kernels, prepare(): pl.pallas_call(prepare_kernel, out_shape=[jax.ShapeDtypeStruct(s, F32) fo...  1.63 us
    pallas_call x1, Pallas kernels, scatter_heat(): pl.pallas_call(functools.partial(heater_kernel, layers=layers, height=hei...  1.49 us
    pallas_call x1, Pallas kernels, final_stage(): pl.pallas_call(final_kernel, out_shape=[jax.ShapeDtypeStruct(s, F32) for...  1.33 us
  transfers between devices with their start and end apart: 10, of which 3 were waited for; matrix products, arithmetic and copies ran while one was open for 0% of the time, Pallas kernels for 4%

profile of v2, /device:TPU:0, one launch (start us, length us, event | category | flops | bytes accessed | tf_op | source)
XLA Modules:
  0.0 39.2 jit_solution(5507583106790373322)
XLA Ops:
  0.6 1.6 %prepare.1 = (f32[5,64,128]{2,1,0:T(8,128)S(1)}, f32[5,64,128]{2,1,0:T(8,128)S(1)}, f32[1,64,128]{2,1,0:T(8,128)S(1)}, f32[1,64,128]{2,1,0:T(8,128)S(1)}, f32[6,...) custom-call(f32[2,64,128]{2,1,0:T(8,128)} %density_hbm.1, s32[2,64,128]{2,1,0:T(8,128)} %anchor_hbm.1, s32[2,64,128]{2,1,0:T(8,128)} %port_hbm.1, ...), custom_call_target="tpu_custom_call" | custom-call | tf_op jit(solution)/shard_map/prepare/pallas_call | solution.py:99
  2.3 8.4 %all-to-all-start = ((f32[16,3,256]{2,1,0:T(4,128)}), f32[16,3,256]{2,1,0:T(4,128)S(1)}, u32[]{:S(2)}, u32[]{:S(2)}) async-start(f32[16,3,256]{2,1,0:T(4,128)} %get-tuple-element.25), calls=%async_computation | async-start | bytes 131072 | tf_op jit(solution)/shard_map/all_to_all | solution.py:530
  10.6 1.9 %collective-permute-start.1 = (f32[5,64,128]{2,1,0:T(8,128)S(1)}, f32[5,64,128]{2,1,0:T(8,128)S(1)}, u32[]{:S(2)}, u32[]{:S(2)}) collective-permute-start(f32[5,64,128]{2,1,0:T(8,128)S(1)} %get-tuple-element.21), channel_id=1, source_target_pairs={{0,2},{2,0},{4,6},{6,4},{8,10},{10,8},{12,14},{14,12},{16,18},{18,... | collective-permute-start | bytes 491528 | tf_op jit(solution)/shard_map/ppermute | solution.py:528
  12.6 0.7 %collective-permute-start.3 = (f32[5,64,128]{2,1,0:T(8,128)S(1)}, f32[5,64,128]{2,1,0:T(8,128)S(1)}, u32[]{:S(2)}, u32[]{:S(2)}) collective-permute-start(f32[5,64,128]{2,1,0:T(8,128)S(1)} %get-tuple-element.22), channel_id=1, source_target_pairs={{2,4},{4,2},{6,8},{8,6},{10,12},{12,10},{14,16},{16,14},{18,20},{2... | collective-permute-start | bytes 491528 | tf_op jit(solution)/shard_map/ppermute | solution.py:529
  13.2 2.9 %collective-permute-start.5 = (f32[1,64,128]{2,1,0:T(8,128)S(1)}, f32[1,64,128]{2,1,0:T(8,128)S(1)}, u32[]{:S(2)}, u32[]{:S(2)}) collective-permute-start(f32[1,64,128]{2,1,0:T(8,128)S(1)} %get-tuple-element.23), channel_id=1, source_target_pairs={{0,4},{4,0},{2,6},{6,2},{8,12},{12,8},{10,14},{14,10},{16,20},{20,... | collective-permute-start | bytes 98312 | tf_op jit(solution)/shard_map/ppermute | solution.py:531
  16.2 0.7 %collective-permute-start.6 = (f32[1,64,128]{2,1,0:T(8,128)S(1)}, f32[1,64,128]{2,1,0:T(8,128)S(1)}, u32[]{:S(2)}, u32[]{:S(2)}) collective-permute-start(f32[1,64,128]{2,1,0:T(8,128)S(1)} %get-tuple-element.24), channel_id=1, source_target_pairs={{4,8},{8,4},{6,10},{10,6},{12,16},{16,12},{14,18},{18,14},{20,24},... | collective-permute-start | bytes 98312 | tf_op jit(solution)/shard_map/ppermute | solution.py:532
  16.8 0.1 collective-permute-start
  16.9 1.3 %all-to-all-done.entries_ref = f32[16,3,256]{2,1,0:T(4,128)S(1)} async-done(((f32[16,3,256]{2,1,0:T(4,128)}), f32[16,3,256]{2,1,0:T(4,128)S(1)}, u32[]{:S(2)}, u32[]{:S(2)}) %all-to-all-start) | async-done | bytes 49184 | tf_op jit(solution)/shard_map/all_to_all | solution.py:530
  18.2 1.5 %heater_scatter.1.heat_ref = f32[8,64,128]{2,1,0:T(8,128)S(1)} custom-call(f32[16,3,256]{2,1,0:T(4,128)S(1)} %all-to-all-done.entries_ref), custom_call_target="tpu_custom_call" | custom-call | tf_op jit(solution)/shard_map/heater_scatter/pallas_call | solution.py:157
  19.7 0.7 %collective-permute-done.5 = f32[1,64,128]{2,1,0:T(8,128)S(1)} collective-permute-done((f32[1,64,128]{2,1,0:T(8,128)S(1)}, f32[1,64,128]{2,1,0:T(8,128)S(1)}, u32[]{:S(2)}, u32[]{:S(2)}) %collective-permute-start.5) | collective-permute-done | bytes 32800 | tf_op jit(solution)/shard_map/ppermute | solution.py:531
  20.3 0.0 collective-permute-start.8
  20.3 0.0 collective-permute-done.1.first_ref
  20.3 0.5 %collective-permute-start.2 = (f32[5,64,128]{2,1,0:T(8,128)S(1)}, f32[5,64,128]{2,1,0:T(8,128)S(1)}, u32[]{:S(2)}, u32[]{:S(2)}) collective-permute-start(f32[5,64,128]{2,1,0:T(8,128)S(1)} %collective-permute-done.1.first_ref), channel_id=1, source_target_pairs={{0,1},{1,0},{2,3},{3,2},{4,5},{5,4},{6,7},{7,6},{8,9},{9,8},{10,11... | collective-permute-start | bytes 491528 | tf_op jit(solution)/shard_map/ppermute | solution.py:38
  20.8 0.0 collective-permute-done.3.second_ref
  20.9 0.1 collective-permute-start.4
  20.9 0.0 collective-permute-done.6
  20.9 0.4 %collective-permute-start.7 = (f32[2,64,128]{2,1,0:T(8,128)S(1)}, f32[2,64,128]{2,1,0:T(8,128)S(1)}, u32[]{:S(2)}, u32[]{:S(2)}) collective-permute-start(f32[2,64,128]{2,1,0:T(8,128)S(1)} %constant_dynamic-update-slice_fusion.far_ref), channel_id=1, source_target_pairs={{0,1},{1,0},{2,3},{3,2},{4,5},{5,4},{6,7},{7,6},{8,9},{9,8},{10,11... | collective-permute-start | bytes 196616 | tf_op jit(solution)/shard_map/ppermute | solution.py:38
  21.4 1.1 %collective-permute-done.7.far_z_ref = f32[2,64,128]{2,1,0:T(8,128)S(1)} collective-permute-done((f32[2,64,128]{2,1,0:T(8,128)S(1)}, f32[2,64,128]{2,1,0:T(8,128)S(1)}, u32[]{:S(2)}, u32[]{:S(2)}) %collective-permute-start.7) | collective-permute-done | bytes 65568 | tf_op jit(solution)/shard_map/ppermute | solution.py:38
  22.4 0.0 collective-permute-done.own_z_ref
  22.4 0.0 collective-permute-done.2.first_z_ref
  22.4 0.0 collective-permute-done.4.second_z_ref
  22.5 1.8 %operators.1 = (f32[2,64,128]{2,1,0:T(8,128)S(1)}, f32[2,2,64,128]{3,2,1,0:T(8,128)S(1)}, f32[3,2,64,128]{3,2,1,0:T(8,128)S(1)}, f32[3,2,64,128]{3,2,1,0:T(8,128...) custom-call(f32[6,64,128]{2,1,0:T(8,128)S(1)} %get-tuple-element.20., ...), custom_call_target="tpu_custom_call" | custom-call | tf_op jit(solution)/shard_map/operators/pallas_call | solution.py:443
  24.3 13.6 %all_to_all.10.table_ref = f32[32,1,128]{2,1,0:T(1,128)S(1)} all-to-all(f32[32,1,128]{2,1,0:T(1,128)S(1)} %get-tuple-element.26), channel_id=1, replica_groups=mesh['gx'=16,'gz'=2] {'gx','gz'}, dimensions={0} | all-to-all | bytes 32768 | tf_op jit(solution)/shard_map/all_to_all | solution.py:544
  37.9 1.3 %outputs.1 = (f32[2,64,128]{2,1,0:T(8,128)}, f32[2,64,128]{2,1,0:T(8,128)}, f32[3,2,64,128]{3,2,1,0:T(8,128)}, f32[3,2,64,128]{3,2,1,0:T(8,128)}, f32[2,2,64,128...) custom-call(f32[32,1,128]{2,1,0:T(1,128)S(1)} %all_to_all.10.table_ref, f32[2,64,128]{2,1,0:T(8,128)S(1)} %get-tuple-element.27.source_ref, ...), custom_call_target="tpu_custom_call" | custom-call | tf_op jit(solution)/shard_map/outputs/pallas_call | solution.py:511
  (3 shorter events, 0.0 us)
Async XLA Ops:
  2.3 15.9 %all-to-all-start = ((f32[16,3,256]{2,1,0:T(4,128)}), f32[16,3,256]{2,1,0:T(4,128)S(1)}, u32[]{:S(2)}, u32[]{:S(2)}) async-start(f32[16,3,256]{2,1,0:T(4,128)} %get-tuple-element.25), calls=%async_computation | async-start | bytes 131072 | tf_op jit(solution)/shard_map/all_to_all | solution.py:530
  10.6 9.7 %collective-permute-start.1 = (f32[5,64,128]{2,1,0:T(8,128)S(1)}, f32[5,64,128]{2,1,0:T(8,128)S(1)}, u32[]{:S(2)}, u32[]{:S(2)}) collective-permute-start(f32[5,64,128]{2,1,0:T(8,128)S(1)} %get-tuple-element.21), channel_id=1, source_target_pairs={{0,2},{2,0},{4,6},{6,4},{8,10},{10,8},{12,14},{14,12},{16,18},{18,... | collective-permute-start | bytes 491528 | tf_op jit(solution)/shard_map/ppermute | solution.py:528
  12.6 8.3 %collective-permute-start.3 = (f32[5,64,128]{2,1,0:T(8,128)S(1)}, f32[5,64,128]{2,1,0:T(8,128)S(1)}, u32[]{:S(2)}, u32[]{:S(2)}) collective-permute-start(f32[5,64,128]{2,1,0:T(8,128)S(1)} %get-tuple-element.22), channel_id=1, source_target_pairs={{2,4},{4,2},{6,8},{8,6},{10,12},{12,10},{14,16},{16,14},{18,20},{2... | collective-permute-start | bytes 491528 | tf_op jit(solution)/shard_map/ppermute | solution.py:529
  13.2 7.1 %collective-permute-start.5 = (f32[1,64,128]{2,1,0:T(8,128)S(1)}, f32[1,64,128]{2,1,0:T(8,128)S(1)}, u32[]{:S(2)}, u32[]{:S(2)}) collective-permute-start(f32[1,64,128]{2,1,0:T(8,128)S(1)} %get-tuple-element.23), channel_id=1, source_target_pairs={{0,4},{4,0},{2,6},{6,2},{8,12},{12,8},{10,14},{14,10},{16,20},{20,... | collective-permute-start | bytes 98312 | tf_op jit(solution)/shard_map/ppermute | solution.py:531
  16.2 4.8 %collective-permute-start.6 = (f32[1,64,128]{2,1,0:T(8,128)S(1)}, f32[1,64,128]{2,1,0:T(8,128)S(1)}, u32[]{:S(2)}, u32[]{:S(2)}) collective-permute-start(f32[1,64,128]{2,1,0:T(8,128)S(1)} %get-tuple-element.24), channel_id=1, source_target_pairs={{4,8},{8,4},{6,10},{10,6},{12,16},{16,12},{14,18},{18,14},{20,24},... | collective-permute-start | bytes 98312 | tf_op jit(solution)/shard_map/ppermute | solution.py:532
  16.8 5.6 %collective-permute-start = (f32[6,64,128]{2,1,0:T(8,128)S(1)}, f32[6,64,128]{2,1,0:T(8,128)S(1)}, u32[]{:S(2)}, u32[]{:S(2)}) collective-permute-start(f32[6,64,128]{2,1,0:T(8,128)S(1)} %get-tuple-element.20.own_ref), channel_id=1, source_target_pairs={{0,1},{1,0},{2,3},{3,2},{4,5},{5,4},{6,7},{7,6},{8,9},{9,8},{10,11... | collective-permute-start | bytes 589832 | tf_op jit(solution)/shard_map/ppermute | solution.py:38
  20.3 2.1 %collective-permute-start.8 = (f32[8,64,128]{2,1,0:T(8,128)S(1)}, f32[8,64,128]{2,1,0:T(8,128)S(1)}, u32[]{:S(2)}, u32[]{:S(2)}) collective-permute-start(f32[8,64,128]{2,1,0:T(8,128)S(1)} %heater_scatter.1.heat_ref), channel_id=1, source_target_pairs={{0,1},{1,0},{2,3},{3,2},{4,5},{5,4},{6,7},{7,6},{8,9},{9,8},{10,11... | collective-permute-start | bytes 786440 | tf_op jit(solution)/shard_map/ppermute | solution.py:38
  20.3 2.1 %collective-permute-start.2 = (f32[5,64,128]{2,1,0:T(8,128)S(1)}, f32[5,64,128]{2,1,0:T(8,128)S(1)}, u32[]{:S(2)}, u32[]{:S(2)}) collective-permute-start(f32[5,64,128]{2,1,0:T(8,128)S(1)} %collective-permute-done.1.first_ref), channel_id=1, source_target_pairs={{0,1},{1,0},{2,3},{3,2},{4,5},{5,4},{6,7},{7,6},{8,9},{9,8},{10,11... | collective-permute-start | bytes 491528 | tf_op jit(solution)/shard_map/ppermute | solution.py:38
  20.9 1.6 %collective-permute-start.4 = (f32[5,64,128]{2,1,0:T(8,128)S(1)}, f32[5,64,128]{2,1,0:T(8,128)S(1)}, u32[]{:S(2)}, u32[]{:S(2)}) collective-permute-start(f32[5,64,128]{2,1,0:T(8,128)S(1)} %collective-permute-done.3.second_ref), channel_id=1, source_target_pairs={{0,1},{1,0},{2,3},{3,2},{4,5},{5,4},{6,7},{7,6},{8,9},{9,8},{10,11... | collective-permute-start | bytes 491528 | tf_op jit(solution)/shard_map/ppermute | solution.py:38
  20.9 1.5 %collective-permute-start.7 = (f32[2,64,128]{2,1,0:T(8,128)S(1)}, f32[2,64,128]{2,1,0:T(8,128)S(1)}, u32[]{:S(2)}, u32[]{:S(2)}) collective-permute-start(f32[2,64,128]{2,1,0:T(8,128)S(1)} %constant_dynamic-update-slice_fusion.far_ref), channel_id=1, source_target_pairs={{0,1},{1,0},{2,3},{3,2},{4,5},{5,4},{6,7},{7,6},{8,9},{9,8},{10,11... | collective-permute-start | bytes 196616 | tf_op jit(solution)/shard_map/ppermute | solution.py:38

commit v3 on v2

--- a/solution.py
+++ b/solution.py
@@ -16,6 +16,7 @@
 SIGMA_MIN = 0.1
 EXPANSION = 4.0
 PORT_DIRECTION = (1.0, 0.5, -0.5)
+
 
 HALO = 3
 WIDTH = 128
@@ -108,7 +109,7 @@
     )(*arguments)
 
 
-def heater_kernel(entries_ref, heat_ref, rows_ref, lanes_ref, total_ref, *, layers, height, block):
+def heater_kernel(entries_ref, heat_ref, far_ref, rows_ref, lanes_ref, total_ref, *, layers, height, block):
     sources = entries_ref.shape[0]
     entries = entries_ref.shape[2]
     slabs = layers + 2 * HALO
@@ -147,7 +148,10 @@
 
         total = total_ref[...]
     heat = total[:, :WIDTH] + total[:, WIDTH:]
-    heat_ref[...] = heat.reshape(heat_ref.shape)
+    heat = heat.reshape(slabs, height, WIDTH)
+    heat_ref[...] = heat[1 : slabs - 1]
+    far_ref[0] = heat[0]
+    far_ref[1] = heat[slabs - 1]
 
 
 def scatter_heat(entries, layers, height):
@@ -156,9 +160,9 @@
     slabs = layers + 2 * HALO
     return pl.pallas_call(
         functools.partial(heater_kernel, layers=layers, height=height, block=block),
-        out_shape=jax.ShapeDtypeStruct((slabs, height, WIDTH), F32),
+        out_shape=[jax.ShapeDtypeStruct((k, height, WIDTH), F32) for k in (slabs - 2, 2)],
         in_specs=[pl.BlockSpec(memory_space=pltpu.VMEM)],
-        out_specs=pl.BlockSpec(memory_space=pltpu.VMEM),
+        out_specs=[pl.BlockSpec(memory_space=pltpu.VMEM)] * 2,
         scratch_shapes=[
             pltpu.VMEM((slabs * height, block * count), jnp.bfloat16),
             pltpu.VMEM((2 * WIDTH, block * count), jnp.bfloat16),
@@ -171,7 +175,7 @@
 
 def main_kernel(
     own_ref, own_z_ref, first_ref, first_z_ref, second_ref, second_z_ref,
-    far_ref, far_z_ref, heat_ref, heat_z_ref,
+    far_one_ref, far_two_ref, heat_ref, heat_z_ref, heat_far_ref,
     source_ref, applied_ref, force_ref, image_ref, image2_ref, pimage_ref, pimage2_ref, sums_ref,
     cub, stress, src, prt, force, image,
 ):
@@ -233,15 +237,15 @@
         a, b = (first_z_ref, second_z_ref) if side else (first_ref, second_ref)
         return jnp.where(even, a[k], b[k])
 
-    def far(side, low):
-        ref = far_z_ref if side else far_ref
-        return jnp.where(low_pair, ref[1], ref[0]) if low else jnp.where(low_pair, ref[0], ref[1])
+    def far(low):
+        one, two = far_one_ref[0], far_two_ref[0]
+        return jnp.where(low_pair, two, one) if low else jnp.where(low_pair, one, two)
 
     def density_of(side, layer):
         if layer == 0:
-            return far(side, True)
+            return far(True)
         if layer == 7:
-            return far(side, False)
+            return far(False)
         if layer in (1, 2):
             return lower(side, layer - 1)
         if layer in (5, 6):
@@ -263,10 +267,11 @@
         return (own_z_ref if side else own_ref)[layer + 1]
 
     for layer in range(8):
-        for side in range(2):
+        outermost = layer in (0, 7)
+        for side in range(1 if outermost else 2):
             d = masked(side, layer, density_of(side, layer))
             c = d * d * d
-            heat = (heat_z_ref if side else heat_ref)[layer]
+            heat = heat_far_ref[layer // 7] if outermost else (heat_z_ref if side else heat_ref)[layer - 1]
             s = masked(side, layer, JOULE_GAIN * (SIGMA_MIN + c) + heat)
             store(cub, side, layer, c)
             store(stress, side, layer, (MODULUS_MINIMUM + c) * s)
@@ -276,6 +281,8 @@
                 source_ref[layer - 3] = s
             if 1 <= layer <= 6:
                 store(prt, side, layer - 1, masked(side, layer, port_of(side, layer)))
+    store(stress, 1, 0, jnp.zeros(tile, F32))
+    store(stress, 1, 7, jnp.zeros(tile, F32))
     for side in range(2):
         for layer, block in ((0, 1), (2, 0)):
             mirrored = jnp.where(gx == block, load(stress, side, layer + 1), load(stress, side, layer))
@@ -530,15 +537,13 @@
     entries = lax.all_to_all(entries, "gx", 0, 0, tiled=True)
     far_one = lax.ppermute(far_one, "gx", swap_pairs(count, 0, 2))
     far_two = lax.ppermute(far_two, "gx", swap_pairs(count, 2, 2))
-    far = jnp.concatenate([far_one, far_two])
     own_z = across_z(own)
     first_z = across_z(first)
     second_z = across_z(second)
-    far_z = across_z(far)
-    heat = scatter_heat(entries, layers, height)
+    heat, heat_far = scatter_heat(entries, layers, height)
     heat_z = across_z(heat)
     source, applied, force, image, image2, pimage, pimage2, sums = main_stage(
-        (own, own_z, first, first_z, second, second_z, far, far_z, heat, heat_z),
+        (own, own_z, first, first_z, second, second_z, far_one, far_two, heat, heat_z, heat_far),
         devices, layers, height,
     )
     table = lax.all_to_all(sums, ("gx", "gz"), 0, 0, tiled=True)

time: 39.5 us -> 46.6 us (1.18)
  waiting for transfers between devices: 3.01 us -> 10.7 us
  starting transfers between devices: 15.6 us -> 14.4 us
  blocking collectives: 13.6 us -> 14.3 us
    all_to_all x1, waiting for transfers between devices: 1.27 us -> 7.45 us  [per_device(): entries = lax.all_to_all(entries, 'gx', 0, 0, tiled=True)]
    ppermute x1, waiting for transfers between devices: 0.67 us -> 3.26 us  [per_device(): far_one = lax.ppermute(far_one, 'gx', swap_pairs(count, 0, 2))]
    ppermute x1, starting transfers between devices: 2.93 us -> 0.65 us  [per_device(): far_one = lax.ppermute(far_one, 'gx', swap_pairs(count, 0, 2))]
    ppermute x1, starting transfers between devices: 1.93 us -> 3.03 us  [per_device(): first = lax.ppermute(first, 'gx', swap_pairs(count, 0, 1))]
    ppermute x5 -> x4, waiting for transfers between devices: 1.07 us -> 0.01 us  [across_z(): return lax.ppermute(values, 'gz', [(0, 1), (1, 0)])]
    all_to_all x1, blocking collectives: 13.6 us -> 14.3 us  [per_device(): table = lax.all_to_all(sums, ('gx', 'gz'), 0, 0, tiled=True)]
    ppermute x5 -> x4, starting transfers between devices: 1.09 us -> 0.72 us  [across_z(): return lax.ppermute(values, 'gz', [(0, 1), (1, 0)])]
  transfers between devices with their start and end apart: 10 -> 9, of which waited for: 3 -> 2; matrix products, arithmetic and copies ran while one was open for 0% -> 0% of each run, Pallas kernels for 4% -> 3%
where the time goes in v3:
time: 46.6 us; the launch traced here: 46.4 us
  starting transfers between devices  14.4 us (31%)
  blocking collectives  14.3 us (31%)
  waiting for transfers between devices  10.7 us (23%)
  Pallas kernels  6.26 us (13%)
  between operations  0.75 us (2%)
    all_to_all x1, blocking collectives, per_device(): table = lax.all_to_all(sums, ('gx', 'gz'), 0, 0, tiled=True)  14.3 us
    all_to_all x1, starting transfers between devices, per_device(): entries = lax.all_to_all(entries, 'gx', 0, 0, tiled=True)  8.65 us
    all_to_all x1, waiting for transfers between devices, per_device(): entries = lax.all_to_all(entries, 'gx', 0, 0, tiled=True)  7.45 us
    ppermute x1, waiting for transfers between devices, per_device(): far_one = lax.ppermute(far_one, 'gx', swap_pairs(count, 0, 2))  3.26 us
    ppermute x1, starting transfers between devices, per_device(): first = lax.ppermute(first, 'gx', swap_pairs(count, 0, 1))  3.03 us
    pallas_call x1, Pallas kernels, main_stage(): pl.pallas_call(main_kernel, out_shape=[jax.ShapeDtypeStruct(s, F32) for s...  1.8 us
    pallas_call x1, Pallas kernels, prepare(): pl.pallas_call(prepare_kernel, out_shape=[jax.ShapeDtypeStruct(s, F32) fo...  1.63 us
    pallas_call x1, Pallas kernels, scatter_heat(): pl.pallas_call(functools.partial(heater_kernel, layers=layers, height=hei...  1.49 us
  transfers between devices with their start and end apart: 9, of which 2 were waited for; matrix products, arithmetic and copies ran while one was open for 0% of the time, Pallas kernels for 3%

profile of v3, /device:TPU:0, one launch (start us, length us, event | category | flops | bytes accessed | tf_op | source)
XLA Modules:
  0.0 46.4 jit_solution(12451398703550587076)
XLA Ops:
  0.6 1.6 %prepare.1 = (f32[5,64,128]{2,1,0:T(8,128)S(1)}, f32[5,64,128]{2,1,0:T(8,128)S(1)}, f32[1,64,128]{2,1,0:T(8,128)S(1)}, f32[1,64,128]{2,1,0:T(8,128)S(1)}, f32[6,...) custom-call(f32[2,64,128]{2,1,0:T(8,128)} %density_hbm.1, s32[2,64,128]{2,1,0:T(8,128)} %anchor_hbm.1, s32[2,64,128]{2,1,0:T(8,128)} %port_hbm.1, ...), custom_call_target="tpu_custom_call" | custom-call | tf_op jit(solution)/shard_map/prepare/pallas_call | solution.py:100
  2.3 3.0 %collective-permute-start.1 = (f32[5,64,128]{2,1,0:T(8,128)S(1)}, f32[5,64,128]{2,1,0:T(8,128)S(1)}, u32[]{:S(2)}, u32[]{:S(2)}) collective-permute-start(f32[5,64,128]{2,1,0:T(8,128)S(1)} %get-tuple-element.23), channel_id=1, source_target_pairs={{0,2},{2,0},{4,6},{6,4},{8,10},{10,8},{12,14},{14,12},{16,18},{18,... | collective-permute-start | bytes 491528 | tf_op jit(solution)/shard_map/ppermute | solution.py:535
  5.3 0.7 %collective-permute-start.3 = (f32[5,64,128]{2,1,0:T(8,128)S(1)}, f32[5,64,128]{2,1,0:T(8,128)S(1)}, u32[]{:S(2)}, u32[]{:S(2)}) collective-permute-start(f32[5,64,128]{2,1,0:T(8,128)S(1)} %get-tuple-element.24), channel_id=1, source_target_pairs={{2,4},{4,2},{6,8},{8,6},{10,12},{12,10},{14,16},{16,14},{18,20},{2... | collective-permute-start | bytes 491528 | tf_op jit(solution)/shard_map/ppermute | solution.py:536
  6.0 8.7 %all-to-all-start = ((f32[16,3,256]{2,1,0:T(4,128)}), f32[16,3,256]{2,1,0:T(4,128)S(1)}, u32[]{:S(2)}, u32[]{:S(2)}) async-start(f32[16,3,256]{2,1,0:T(4,128)} %get-tuple-element.27), calls=%async_computation | async-start | bytes 131072 | tf_op jit(solution)/shard_map/all_to_all | solution.py:537
  14.6 0.1 collective-permute-start
  14.7 7.5 %all-to-all-done.entries_ref = f32[16,3,256]{2,1,0:T(4,128)S(1)} async-done(((f32[16,3,256]{2,1,0:T(4,128)}), f32[16,3,256]{2,1,0:T(4,128)S(1)}, u32[]{:S(2)}, u32[]{:S(2)}) %all-to-all-start) | async-done | bytes 49184 | tf_op jit(solution)/shard_map/all_to_all | solution.py:537
  22.2 1.5 %heater_scatter.1 = (f32[6,64,128]{2,1,0:T(8,128)S(1)}, f32[2,64,128]{2,1,0:T(8,128)S(1)}) custom-call(f32[16,3,256]{2,1,0:T(4,128)S(1)} %all-to-all-done.entries_ref), custom_call_target="tpu_custom_call" | custom-call | tf_op jit(solution)/shard_map/heater_scatter/pallas_call | solution.py:161
  23.7 0.1 collective-permute-start.7
  23.7 0.0 collective-permute-done.1.first_ref
  23.7 0.5 %collective-permute-start.2 = (f32[5,64,128]{2,1,0:T(8,128)S(1)}, f32[5,64,128]{2,1,0:T(8,128)S(1)}, u32[]{:S(2)}, u32[]{:S(2)}) collective-permute-start(f32[5,64,128]{2,1,0:T(8,128)S(1)} %collective-permute-done.1.first_ref), channel_id=1, source_target_pairs={{0,1},{1,0},{2,3},{3,2},{4,5},{5,4},{6,7},{7,6},{8,9},{9,8},{10,11... | collective-permute-start | bytes 491528 | tf_op jit(solution)/shard_map/ppermute | solution.py:39
  24.2 0.0 collective-permute-done.3.second_ref
  24.2 0.1 collective-permute-start.4
  24.3 0.7 %collective-permute-start.5 = (f32[1,64,128]{2,1,0:T(8,128)S(1)}, f32[1,64,128]{2,1,0:T(8,128)S(1)}, u32[]{:S(2)}, u32[]{:S(2)}) collective-permute-start(f32[1,64,128]{2,1,0:T(8,128)S(1)} %get-tuple-element.25), channel_id=1, source_target_pairs={{0,4},{4,0},{2,6},{6,2},{8,12},{12,8},{10,14},{14,10},{16,20},{20,... | collective-permute-start | bytes 98312 | tf_op jit(solution)/shard_map/ppermute | solution.py:538
  25.0 3.3 %collective-permute-done.5.far_one_ref = f32[1,64,128]{2,1,0:T(8,128)S(1)} collective-permute-done((f32[1,64,128]{2,1,0:T(8,128)S(1)}, f32[1,64,128]{2,1,0:T(8,128)S(1)}, u32[]{:S(2)}, u32[]{:S(2)}) %collective-permute-start.5) | collective-permute-done | bytes 32800 | tf_op jit(solution)/shard_map/ppermute | solution.py:538
  28.2 0.7 %collective-permute-start.6 = (f32[1,64,128]{2,1,0:T(8,128)S(1)}, f32[1,64,128]{2,1,0:T(8,128)S(1)}, u32[]{:S(2)}, u32[]{:S(2)}) collective-permute-start(f32[1,64,128]{2,1,0:T(8,128)S(1)} %get-tuple-element.26), channel_id=1, source_target_pairs={{4,8},{8,4},{6,10},{10,6},{12,16},{16,12},{14,18},{18,14},{20,24},... | collective-permute-start | bytes 98312 | tf_op jit(solution)/shard_map/ppermute | solution.py:539
  28.9 0.0 collective-permute-done.6.far_two_ref
  28.9 0.0 collective-permute-done.own_z_ref
  28.9 0.0 collective-permute-done.7.heat_z_ref
  28.9 0.0 collective-permute-done.2.first_z_ref
  28.9 0.0 collective-permute-done.4.second_z_ref
  29.0 1.8 %operators.1 = (f32[2,64,128]{2,1,0:T(8,128)S(1)}, f32[2,2,64,128]{3,2,1,0:T(8,128)S(1)}, f32[3,2,64,128]{3,2,1,0:T(8,128)S(1)}, f32[3,2,64,128]{3,2,1,0:T(8,128...) custom-call(f32[6,64,128]{2,1,0:T(8,128)S(1)} %get-tuple-element.22., ...), custom_call_target="tpu_custom_call" | custom-call | tf_op jit(solution)/shard_map/operators/pallas_call | solution.py:450
  30.8 14.3 %all_to_all.10.table_ref = f32[32,1,128]{2,1,0:T(1,128)S(1)} all-to-all(f32[32,1,128]{2,1,0:T(1,128)S(1)} %get-tuple-element.30), channel_id=1, replica_groups=mesh['gx'=16,'gz'=2] {'gx','gz'}, dimensions={0} | all-to-all | bytes 32768 | tf_op jit(solution)/shard_map/all_to_all | solution.py:549
  45.0 1.3 %outputs.1 = (f32[2,64,128]{2,1,0:T(8,128)}, f32[2,64,128]{2,1,0:T(8,128)}, f32[3,2,64,128]{3,2,1,0:T(8,128)}, f32[3,2,64,128]{3,2,1,0:T(8,128)}, f32[2,2,64,128...) custom-call(f32[32,1,128]{2,1,0:T(1,128)S(1)} %all_to_all.10.table_ref, f32[2,64,128]{2,1,0:T(8,128)S(1)} %get-tuple-element.31.source_ref, ...), custom_call_target="tpu_custom_call" | custom-call | tf_op jit(solution)/shard_map/outputs/pallas_call | solution.py:518
Async XLA Ops:
  2.3 21.5 %collective-permute-start.1 = (f32[5,64,128]{2,1,0:T(8,128)S(1)}, f32[5,64,128]{2,1,0:T(8,128)S(1)}, u32[]{:S(2)}, u32[]{:S(2)}) collective-permute-start(f32[5,64,128]{2,1,0:T(8,128)S(1)} %get-tuple-element.23), channel_id=1, source_target_pairs={{0,2},{2,0},{4,6},{6,4},{8,10},{10,8},{12,14},{14,12},{16,18},{18,... | collective-permute-start | bytes 491528 | tf_op jit(solution)/shard_map/ppermute | solution.py:535
  5.3 18.9 %collective-permute-start.3 = (f32[5,64,128]{2,1,0:T(8,128)S(1)}, f32[5,64,128]{2,1,0:T(8,128)S(1)}, u32[]{:S(2)}, u32[]{:S(2)}) collective-permute-start(f32[5,64,128]{2,1,0:T(8,128)S(1)} %get-tuple-element.24), channel_id=1, source_target_pairs={{2,4},{4,2},{6,8},{8,6},{10,12},{12,10},{14,16},{16,14},{18,20},{2... | collective-permute-start | bytes 491528 | tf_op jit(solution)/shard_map/ppermute | solution.py:536
  6.0 16.2 %all-to-all-start = ((f32[16,3,256]{2,1,0:T(4,128)}), f32[16,3,256]{2,1,0:T(4,128)S(1)}, u32[]{:S(2)}, u32[]{:S(2)}) async-start(f32[16,3,256]{2,1,0:T(4,128)} %get-tuple-element.27), calls=%async_computation | async-start | bytes 131072 | tf_op jit(solution)/shard_map/all_to_all | solution.py:537
  14.6 14.3 %collective-permute-start = (f32[6,64,128]{2,1,0:T(8,128)S(1)}, f32[6,64,128]{2,1,0:T(8,128)S(1)}, u32[]{:S(2)}, u32[]{:S(2)}) collective-permute-start(f32[6,64,128]{2,1,0:T(8,128)S(1)} %get-tuple-element.22.own_ref), channel_id=1, source_target_pairs={{0,1},{1,0},{2,3},{3,2},{4,5},{5,4},{6,7},{7,6},{8,9},{9,8},{10,11... | collective-permute-start | bytes 589832 | tf_op jit(solution)/shard_map/ppermute | solution.py:39
  23.7 5.3 %collective-permute-start.7 = (f32[6,64,128]{2,1,0:T(8,128)S(1)}, f32[6,64,128]{2,1,0:T(8,128)S(1)}, u32[]{:S(2)}, u32[]{:S(2)}) collective-permute-start(f32[6,64,128]{2,1,0:T(8,128)S(1)} %get-tuple-element.28.heat_ref), channel_id=1, source_target_pairs={{0,1},{1,0},{2,3},{3,2},{4,5},{5,4},{6,7},{7,6},{8,9},{9,8},{10,11... | collective-permute-start | bytes 589832 | tf_op jit(solution)/shard_map/ppermute | solution.py:39
  23.7 5.2 %collective-permute-start.2 = (f32[5,64,128]{2,1,0:T(8,128)S(1)}, f32[5,64,128]{2,1,0:T(8,128)S(1)}, u32[]{:S(2)}, u32[]{:S(2)}) collective-permute-start(f32[5,64,128]{2,1,0:T(8,128)S(1)} %collective-permute-done.1.first_ref), channel_id=1, source_target_pairs={{0,1},{1,0},{2,3},{3,2},{4,5},{5,4},{6,7},{7,6},{8,9},{9,8},{10,11... | collective-permute-start | bytes 491528 | tf_op jit(solution)/shard_map/ppermute | solution.py:39
  24.2 4.7 %collective-permute-start.4 = (f32[5,64,128]{2,1,0:T(8,128)S(1)}, f32[5,64,128]{2,1,0:T(8,128)S(1)}, u32[]{:S(2)}, u32[]{:S(2)}) collective-permute-start(f32[5,64,128]{2,1,0:T(8,128)S(1)} %collective-permute-done.3.second_ref), channel_id=1, source_target_pairs={{0,1},{1,0},{2,3},{3,2},{4,5},{5,4},{6,7},{7,6},{8,9},{9,8},{10,11... | collective-permute-start | bytes 491528 | tf_op jit(solution)/shard_map/ppermute | solution.py:39
  24.3 3.9 %collective-permute-start.5 = (f32[1,64,128]{2,1,0:T(8,128)S(1)}, f32[1,64,128]{2,1,0:T(8,128)S(1)}, u32[]{:S(2)}, u32[]{:S(2)}) collective-permute-start(f32[1,64,128]{2,1,0:T(8,128)S(1)} %get-tuple-element.25), channel_id=1, source_target_pairs={{0,4},{4,0},{2,6},{6,2},{8,12},{12,8},{10,14},{14,10},{16,20},{20,... | collective-permute-start | bytes 98312 | tf_op jit(solution)/shard_map/ppermute | solution.py:538
  28.2 0.7 %collective-permute-start.6 = (f32[1,64,128]{2,1,0:T(8,128)S(1)}, f32[1,64,128]{2,1,0:T(8,128)S(1)}, u32[]{:S(2)}, u32[]{:S(2)}) collective-permute-start(f32[1,64,128]{2,1,0:T(8,128)S(1)} %get-tuple-element.26), channel_id=1, source_target_pairs={{4,8},{8,4},{6,10},{10,6},{12,16},{16,12},{14,18},{18,14},{20,24},... | collective-permute-start | bytes 98312 | tf_op jit(solution)/shard_map/ppermute | solution.py:539

commit v4 on v3

v4 whole, which is shorter than its diff:
```python
import functools

import jax
import jax.numpy as jnp
from jax import lax
from jax.experimental import pallas as pl
from jax.experimental.pallas import tpu as pltpu
from jax.sharding import PartitionSpec as P


KAPPA_MIN = 0.05
MODULUS_MINIMUM = 0.02
CONVECTION = 0.2
PENALTY = 10.0
JOULE_GAIN = 1.0
SIGMA_MIN = 0.1
EXPANSION = 4.0
PORT_DIRECTION = (1.0, 0.5, -0.5)


HALO = 3
WIDTH = 128
EDGE = 8
STRIP = 8
VMEM_LIMIT = 16 << 20
F32 = jnp.float32


def swap_pairs(count, offset, distance):
    pairs = []
    for low in range(offset, count - distance):
        if ((low - offset) // distance) % 2 == 0:
            pairs += [(low, low + distance), (low + distance, low)]
    return pairs


def across_z(values):
    count = lax.axis_size("gz")
    if count == 2:
        return lax.ppermute(values, "gz", [(0, 1), (1, 0)])
    upper = lax.ppermute(values, "gz", [(i + 1, i) for i in range(count - 1)])
    lower = lax.ppermute(values, "gz", [(i, i + 1) for i in range(count - 1)])
    lanes = lax.broadcasted_iota(jnp.int32, values.shape, values.ndim - 1)
    return jnp.where(lanes < WIDTH // 2, upper, lower)


def prepare_kernel(
    density_hbm, anchor_hbm, port_hbm, owner_hbm, cell_hbm, power_hbm,
    first_ref, second_ref, far_one_ref, far_two_ref, own_ref, entries_hbm,
    density_ref, anchor_ref, port_ref, owner_ref, cell_ref, power_ref, entries_ref, arrived,
):
    layers = density_ref.shape[0]
    sources = (owner_hbm, cell_hbm, power_hbm, density_hbm, port_hbm, anchor_hbm)
    targets = (owner_ref, cell_ref, power_ref, density_ref, port_ref, anchor_ref)
    copies = [
        pltpu.make_async_copy(source, target, arrived.at[k])
        for k, (source, target) in enumerate(zip(sources, targets))
    ]
    for copy in copies:
        copy.start()
    gx = lax.axis_index("gx")
    even = gx % 2 == 0
    low_pair = gx % 4 < 2
    for copy in copies[:3]:
        copy.wait()
    owner = owner_ref[...].astype(F32)
    cell = cell_ref[...].astype(F32)
    power = power_ref[...]
    for k in range(entries_ref.shape[0]):
        entries_ref[k, 0:1] = owner
        entries_ref[k, 1:2] = cell
        entries_ref[k, 2:3] = power
    leaving = pltpu.make_async_copy(entries_ref, entries_hbm, arrived.at[len(copies)])
    leaving.start()
    copies[3].wait()
    for layer in range(layers):
        density = density_ref[layer]
        for ref in (first_ref, second_ref, own_ref):
            ref[layer] = density
    below, above = density_ref[0], density_ref[layers - 1]
    far_one_ref[0] = jnp.where(low_pair, above, below)
    far_two_ref[0] = jnp.where(low_pair, below, above)
    copies[4].wait()
    for layer in range(layers):
        port = port_ref[layer].astype(F32)
        for ref in (first_ref, second_ref, own_ref):
            ref[layers + layer] = port
    copies[5].wait()
    for layer in range(layers):
        own_ref[2 * layers + layer] = anchor_ref[layer].astype(F32)
    below, above = anchor_ref[0].astype(F32), anchor_ref[layers - 1].astype(F32)
    first_ref[2 * layers] = jnp.where(even, above, below)
    second_ref[2 * layers] = jnp.where(even, below, above)
    leaving.wait()


def prepare(arguments, sources):
    layers, height, _ = arguments[0].shape
    plane = (height, WIDTH)
    shapes = [
        (2 * layers + 1,) + plane, (2 * layers + 1,) + plane, (1,) + plane, (1,) + plane,
        (3 * layers,) + plane, (sources, 3, arguments[-1].shape[1]),
    ]
    return pl.pallas_call(
        prepare_kernel,
        out_shape=[jax.ShapeDtypeStruct(s, F32) for s in shapes],
        in_specs=[pl.BlockSpec(memory_space=pltpu.HBM)] * len(arguments),
        out_specs=[pl.BlockSpec(memory_space=pltpu.VMEM)] * (len(shapes) - 1)
        + [pl.BlockSpec(memory_space=pltpu.HBM)],
        scratch_shapes=[pltpu.VMEM(a.shape, a.dtype) for a in arguments]
        + [pltpu.VMEM(shapes[-1], F32), pltpu.SemaphoreType.DMA((len(arguments) + 1,))],
        compiler_params=pltpu.CompilerParams(vmem_limit_bytes=VMEM_LIMIT),
        name="prepare",
    )(*arguments)


def heater_kernel(entries_ref, heat_ref, far_ref, rows_ref, lanes_ref, *total_refs, layers, height, block):
    sources = entries_ref.shape[0]
    entries = entries_ref.shape[2]
    slabs = layers + 2 * HALO
    base = lax.axis_index("gx") * layers - HALO
    plane_bits = (height * WIDTH).bit_length() - 1
    lane_bits = WIDTH.bit_length() - 1
    height_bits = height.bit_length() - 1
    group = slabs * height
    row_ids = lax.broadcasted_iota(jnp.int32, (group, entries), 0)
    lane_ids = lax.broadcasted_iota(jnp.int32, (WIDTH, entries), 0)

    def one_block(start, keep):
        rows = []
        for k in range(block):
            table = entries_ref[start + k]
            owner = table[0:1].astype(jnp.int32)
            cell = table[1:2].astype(jnp.int32)
            power = table[2:3]
            slab = owner * layers + (cell >> plane_bits) - base
            rows.append((slab << height_bits) + ((cell >> lane_bits) & (height - 1)))
            high = power.astype(jnp.bfloat16).astype(F32)
            low = power - high
            here = slice(k * entries, (k + 1) * entries)
            match = lane_ids == (cell & (WIDTH - 1))
            lanes_ref[0:WIDTH, here] = jnp.where(match, high, 0.0).astype(jnp.bfloat16)
            lanes_ref[WIDTH:, here] = jnp.where(match, low, 0.0).astype(jnp.bfloat16)
            rows_ref[:, here] = jnp.where(row_ids == rows[k], 1.0, 0.0).astype(jnp.bfloat16)
        both = None
        width = block * entries // 1
        for k in range(1):
            here = slice(k * width, (k + 1) * width)
            part = lax.dot_general(
                rows_ref[:, here], lanes_ref[:, here], (((1,), (1,)), ((), ())), preferred_element_type=F32
            )
            both = part if both is None else both + part
        keep(0, both[:, :WIDTH] + both[:, WIDTH:])

    def write(first, part):
        for k in range(group // height):
            slab = first // height + k
            value = part[k * height : (k + 1) * height]
            if slab in (0, slabs - 1):
                far_ref[slab // (slabs - 1)] = value
            else:
                heat_ref[slab - 1] = value

    if sources == block:
        one_block(0, write)
        return
    total_ref = total_refs[0]
    total_ref[...] = jnp.zeros_like(total_ref)

    def add(first, part):
        total_ref[first : first + group, :] += part

    @pl.loop(0, sources // block)
    def _(step):
        one_block(step * block, add)

    for first in range(0, slabs * height, group):
        write(first, total_ref[first : first + group, :])


def scatter_heat(entries, layers, height):
    sources, _, count = entries.shape
    block = min(sources, 16)
    slabs = layers + 2 * HALO
    if height & (height - 1) or sources % block:
        raise ValueError("unsupported sizes")
    scratch = [
        pltpu.VMEM((slabs * height, block * count), jnp.bfloat16),
        pltpu.VMEM((2 * WIDTH, block * count), jnp.bfloat16),
    ]
    if sources > block:
        scratch.append(pltpu.VMEM((slabs * height, WIDTH), F32))
    return pl.pallas_call(
        functools.partial(heater_kernel, layers=layers, height=height, block=block),
        out_shape=[jax.ShapeDtypeStruct((k, height, WIDTH), F32) for k in (slabs - 2, 2)],
        in_specs=[pl.BlockSpec(memory_space=pltpu.VMEM)],
        out_specs=[pl.BlockSpec(memory_space=pltpu.VMEM)] * 2,
        scratch_shapes=scratch,
        compiler_params=pltpu.CompilerParams(vmem_limit_bytes=VMEM_LIMIT),
        name="heater_scatter",
    )(entries)


class Block:
    def __init__(self, height):
        gx, gz = lax.axis_index("gx"), lax.axis_index("gz")
        last_x, last_z = lax.axis_size("gx") - 1, lax.axis_size("gz") - 1

        def flag(condition):
            return jnp.where(condition, 1.0, 0.0).astype(F32)

        self.gx = gx
        self.height = height
        self.start = 0
        self.even = gx % 2 == 0
        self.low_pair = gx % 4 < 2
        lanes = lax.broadcasted_iota(jnp.int32, (STRIP, WIDTH), 1)
        self.is_last = lanes == WIDTH - 1
        self.is_first = lanes == 0
        self.z_valid = jnp.where(lanes < WIDTH // 2, flag(gz < last_z), flag(gz > 0))
        self.x_valid = [
            flag(gx >= 2), flag(gx >= 1), flag(gx >= 1), None, None,
            flag(gx < last_x), flag(gx < last_x), flag(gx < last_x - 1),
        ]
        self.symmetry = flag(gx > 0)
        self.sums = {}

    def strips(self):
        for start in range(0, self.height, STRIP):
            self.start = start
            yield start

    def masked(self, side, layer, value):
        if side:
            value = value * self.z_valid
        if self.x_valid[layer] is not None:
            value = value * self.x_valid[layer]
        return value

    def load(self, ref, side, layer, shift=0):
        first = EDGE + self.start + shift
        return ref[side, layer, first : first + STRIP, :]

    def store(self, ref, side, layer, value):
        first = EDGE + self.start
        ref[side, layer, first : first + STRIP, :] = value

    def read(self, ref, *index):
        return ref[index + (slice(self.start, self.start + STRIP), slice(None))]

    def write(self, ref, value, *index):
        ref[index + (slice(self.start, self.start + STRIP), slice(None))] = value

    def clear_edges(self, *refs):
        edge_rows = jnp.zeros((EDGE, WIDTH), F32)
        for ref in refs:
            for side in range(2):
                for layer in range(ref.shape[1]):
                    ref[side, layer, 0:EDGE, :] = edge_rows
                    ref[side, layer, EDGE + self.height :, :] = edge_rows

    def z_pair(self, ref, layer, side):
        value, other = self.load(ref, side, layer), self.load(ref, 1 - side, layer)
        down = pltpu.roll(jnp.where(self.is_last, other, value), 1, 1)
        up = pltpu.roll(jnp.where(self.is_first, other, value), WIDTH - 1, 1)
        return value, down, up

    def pick(self, own, first, second, layer, own_tile, near_tile):
        if layer in (3, 4):
            return self.read(own, own_tile + layer - 3)
        one, two = (second, first) if layer < 3 else (first, second)
        return jnp.where(self.even, self.read(one, near_tile), self.read(two, near_tile))

    def weights_of(self, cub, layer, side):
        def face(a, b):
            return MODULUS_MINIMUM + 0.5 * (a + b)

        index = layer - 1
        c, down, up = self.z_pair(cub, index, side)
        x_low = face(self.load(cub, side, index - 1), c)
        if layer == 3:
            x_low = x_low * self.symmetry
        return (
            x_low,
            face(self.load(cub, side, index + 1), c),
            face(self.load(cub, side, index, -1), c),
            face(self.load(cub, side, index, 1), c),
            face(down, c),
            face(up, c),
        )

    def differences(self, ref, index, side):
        v, down, up = self.z_pair(ref, index, side)
        parts = (
            v - self.load(ref, side, index - 1),
            v - self.load(ref, side, index + 1),
            v - self.load(ref, side, index, -1),
            v - self.load(ref, side, index, 1),
            v - down,
            v - up,
        )
        return v, parts

    def weighted(self, weights, parts):
        total = weights[0] * parts[0]
        for w, p in zip(weights[1:], parts[1:]):
            total = total + w * p
        return total

    def accumulate(self, name, value):
        value = jnp.sum(value.reshape(STRIP // 8, 8, WIDTH), axis=0)
        self.sums[name] = self.sums[name] + value if name in self.sums else value

    def total(self, name):
        return jnp.sum(jnp.sum(self.sums[name], axis=0, keepdims=True), axis=1, keepdims=True)

    def row(self, columns):
        lane = lax.broadcasted_iota(jnp.int32, (1, WIDTH), 1)
        row = jnp.zeros((1, WIDTH), F32)
        for k, column in columns.items():
            row = jnp.where(lane == k, column, row)
        return row


def ratio(m, n):
    return jnp.where(n > 0.0, m / jnp.where(n > 0.0, n, 1.0), 0.0)


SPREAD = KAPPA_MIN - MODULUS_MINIMUM


def port_kernel(
    own_ref, own_z_ref, first_ref, first_z_ref, second_ref, second_z_ref,
    cub, applied_ref, image_ref, image2_ref, row_ref,
    prt, image, kept,
):
    block = Block(own_ref.shape[1])
    block.clear_edges(cub, prt, image)
    near = ((own_ref, first_ref, second_ref), (own_z_ref, first_z_ref, second_z_ref))
    for layer in range(1, 7):
        tile = (layer - 1) % 4
        for side in range(2):
            for _ in block.strips():
                d = block.masked(side, layer, block.pick(*near[side], layer, 0, tile))
                block.store(cub, side, layer - 1, d * d * d)
                if 2 <= layer <= 5 or side == 0:
                    port = block.masked(side, layer, block.pick(*near[side], layer, 2, 2 + tile))
                    block.store(prt, side, layer - 1, port)
    for layer in range(2, 6):
        own = layer in (3, 4)
        for side in range(2 if own else 1):
            for _ in block.strips():
                weights = block.weights_of(cub, layer, side)
                v, parts = block.differences(prt, layer - 1, side)
                flux = block.weighted(weights, parts)
                anchor = PENALTY * block.pick(*near[side], layer, 4, 4)
                value = block.masked(side, layer, flux + anchor * v)
                block.store(image, side, layer - 2, value)
                if own and side == 0:
                    for k, weight in enumerate(weights):
                        block.write(kept, weight, layer - 3, k)
                    block.write(image_ref, value, layer - 3)
                    block.accumulate("n", v * v)
                    block.accumulate("m", v * value)
                    low = parts[0] * block.symmetry if layer == 3 else parts[0]
                    plain = low + parts[1] + parts[2] + parts[3] + parts[4] + parts[5]
                    heat_image = flux + SPREAD * plain + CONVECTION * v
                    block.write(applied_ref, heat_image, layer - 3)
                    block.accumulate("k", v * heat_image)
    n, m, k = (block.total(name) for name in "nmk")
    theta = ratio(m, n)
    for layer in (3, 4):
        for _ in block.strips():
            v, parts = block.differences(image, layer - 2, 0)
            weights = [block.read(kept, layer - 3, k6) for k6 in range(6)]
            anchor = PENALTY * block.read(own_ref, layer + 1)
            value = block.weighted(weights, parts) + anchor * v
            block.write(image2_ref, value, layer - 3)
            start = block.load(prt, 0, layer - 1)
            r = v - theta * start
            y = value - theta * v
            block.accumulate("s", r * r)
            block.accumulate("t", r * y)
            block.accumulate("c", start * y)
    s, t, c = (block.total(name) for name in "stc")
    row_ref[...] = block.row({2: n, 3: k, 9: n, 10: m, 11: s, 12: t, 13: c + s})


def force_kernel(
    own_ref, own_z_ref, first_ref, second_ref, far_one_ref, far_two_ref, heat_ref, heat_z_ref, heat_far_ref,
    cub, row_ref,
    source_ref, applied_ref, force_ref, image_ref, image2_ref, sums_ref,
    stress, src, force, image, kept,
):
    block = Block(own_ref.shape[1])
    block.clear_edges(stress, src, force, image)
    near = ((own_ref, first_ref, second_ref), (own_z_ref, None, None))

    def heated(side, layer, c, heat):
        s = block.masked(side, layer, JOULE_GAIN * (SIGMA_MIN + c) + heat)
        block.store(stress, side, layer, (MODULUS_MINIMUM + c) * s)
        return s

    for layer in range(1, 7):
        for side in range(2):
            for _ in block.strips():
                heat = block.read(heat_z_ref if side else heat_ref, layer - 1)
                s = heated(side, layer, block.load(cub, side, layer - 1), heat)
                if 2 <= layer <= 5:
                    block.store(src, side, layer - 2, s)
                if side == 0 and layer in (3, 4):
                    block.write(source_ref, s, layer - 3)
    for _ in block.strips():
        one, two = block.read(far_one_ref, 0), block.read(far_two_ref, 0)
        for layer, d in ((0, jnp.where(block.low_pair, two, one)), (7, jnp.where(block.low_pair, one, two))):
            heated(0, layer, d * d * d, block.read(heat_far_ref, layer // 7))
        for side, layer, index in ((0, 0, 1), (0, 2, 0), (1, 2, 0)):
            mirrored = jnp.where(
                block.gx == index, block.load(stress, side, layer + 1), block.load(stress, side, layer)
            )
            block.store(stress, side, layer, mirrored)

    half = EXPANSION * 0.5
    for layer in range(1, 7):
        for side in range(1 if layer in (1, 6) else 2):
            for _ in block.strips():
                _, down, up = block.z_pair(stress, layer, side)
                parts = (
                    block.load(stress, side, layer + 1) - block.load(stress, side, layer - 1),
                    block.load(stress, side, layer, 1) - block.load(stress, side, layer, -1),
                    up - down,
                )
                for k in range(3):
                    value = block.masked(side, layer, half * parts[k])
                    block.store(force, side, k * 6 + layer - 1, value)
                    if side == 0 and layer in (3, 4):
                        block.write(force_ref, value, k, layer - 3)

    for layer in range(2, 6):
        own = layer in (3, 4)
        for side in range(2 if own else 1):
            for _ in block.strips():
                weights = block.weights_of(cub, layer, side)
                anchor = PENALTY * block.pick(*near[side], layer, 4, 4)
                mine = own and side == 0
                for k in range(3):
                    v, parts = block.differences(force, k * 6 + layer - 1, side)
                    value = block.masked(side, layer, block.weighted(weights, parts) + anchor * v)
                    block.store(image, side, k * 4 + layer - 2, value)
                    if mine:
                        block.write(image_ref, value, k, layer - 3)
                        block.accumulate("n", v * v)
                        block.accumulate("m", v * value)
                if mine:
                    for k, weight in enumerate(weights):
                        block.write(kept, weight, layer - 3, k)
                    v, parts = block.differences(src, layer - 2, 0)
                    heat_weights = [w + SPREAD for w in weights]
                    if layer == 3:
                        heat_weights[0] = weights[0] + SPREAD * block.symmetry
                    heat_image = block.weighted(heat_weights, parts) + CONVECTION * v
                    block.write(applied_ref, heat_image, layer - 3)
                    block.accumulate("k", v * heat_image)
                    block.accumulate("q", v * v)
    n, m, k, q = (block.total(name) for name in "nmkq")
    theta = ratio(m, n)
    for layer in (3, 4):
        for _ in block.strips():
            weights = [block.read(kept, layer - 3, k6) for k6 in range(6)]
            anchor = PENALTY * block.read(own_ref, layer + 1)
            for k3 in range(3):
                v, parts = block.differences(image, k3 * 4 + layer - 2, 0)
                value = block.weighted(weights, parts) + anchor * v
                block.write(image2_ref, value, k3, layer - 3)
                start = block.load(force, 0, k3 * 6 + layer - 1)
                r = v - theta * start
                y = value - theta * v
                block.accumulate("s", r * r)
                block.accumulate("t", r * y)
                block.accumulate("c", start * y)
    s, t, c = (block.total(name) for name in "stc")
    row = row_ref[...] + block.row({0: q, 1: k, 4: n, 5: m, 6: s, 7: t, 8: c + s})
    sums_ref[...] = jnp.broadcast_to(row[None], sums_ref.shape)


def field(count, height):
    return (2, count, height + 2 * EDGE, WIDTH)


def in_memory(kernel, arguments, shapes, scratch):
    vmem = pl.BlockSpec(memory_space=pltpu.VMEM)
    return pl.pallas_call(
        kernel,
        out_shape=[jax.ShapeDtypeStruct(s, F32) for s in shapes],
        in_specs=[vmem] * len(arguments),
        out_specs=[vmem] * len(shapes),
        scratch_shapes=[pltpu.VMEM(s, F32) for s in scratch],
        compiler_params=pltpu.CompilerParams(vmem_limit_bytes=VMEM_LIMIT),
    )(*arguments)


def port_stage(arguments, layers, height):
    own = (layers, height, WIDTH)
    shapes = [field(6, height), own, own, own, (1, WIDTH)]
    return in_memory(port_kernel, arguments, shapes, [field(6, height), field(4, height), (2, 6, height, WIDTH)])


def force_stage(arguments, devices, layers, height):
    own = (layers, height, WIDTH)
    vectors = (3,) + own
    shapes = [own, own, vectors, vectors, vectors, (devices, 1, WIDTH)]
    scratch = [field(8, height), field(4, height), field(18, height), field(12, height), (2, 6, height, WIDTH)]
    return in_memory(force_kernel, arguments, shapes, scratch)


def final_kernel(
    table_ref, source_ref, own_ref, applied_ref, papplied_ref, force_ref, image_ref, image2_ref,
    pimage_ref, pimage2_ref,
    temperature_ref, adjoint_ref, displacement_ref, displacement_adjoint_ref, thermal_ref, elastic_ref,
):
    table = table_ref[...].reshape(table_ref.shape[0], WIDTH)

    def column(k):
        return table[:, k : k + 1]

    def total(value):
        return jnp.sum(value, axis=0, keepdims=True)

    step0 = total(column(0)) / total(column(1))
    step1 = total(column(2)) / total(column(3))

    def solve(first):
        n_all, m_all = column(first), column(first + 1)
        n, m = total(n_all), total(m_all)
        theta = m / n
        local = jnp.where(n_all > 0.0, m_all / jnp.where(n_all > 0.0, n_all, 1.0), 0.0)
        gap = local - theta
        s = total(column(first + 2) + gap * gap * n_all)
        t = total(column(first + 3) + gap * column(first + 4) + gap * gap * m_all)
        alpha0 = n / m
        beta = s * alpha0 * alpha0 / n
        alpha1 = s / (t - s * s / m)
        return alpha0, beta, alpha1

    def outcome(coefficients, b, w, u):
        alpha0, beta, alpha1 = coefficients
        r = b - alpha0 * w
        x = alpha0 * b + alpha1 * (r + beta * b)
        r = r - alpha1 * ((w - alpha0 * u) + beta * w)
        return x, r

    forward, adjoint = solve(4), solve(9)
    for layer in range(source_ref.shape[0]):
        source = source_ref[layer]
        port = own_ref[source_ref.shape[0] + layer]
        temperature_ref[layer] = step0 * source
        adjoint_ref[layer] = step1 * port
        thermal_ref[0, layer] = source - step0 * applied_ref[layer]
        thermal_ref[1, layer] = port - step1 * papplied_ref[layer]
        for k in range(3):
            x, r = outcome(forward, force_ref[k, layer], image_ref[k, layer], image2_ref[k, layer])
            displacement_ref[k, layer] = step0 * x
            elastic_ref[0, k, layer] = step0 * r
        x, r = outcome(adjoint, port, pimage_ref[layer], pimage2_ref[layer])
        for k in range(3):
            displacement_adjoint_ref[k, layer] = PORT_DIRECTION[k] * x
            elastic_ref[1, k, layer] = PORT_DIRECTION[k] * r


def final_stage(arguments, layers, height):
    own = (layers, height, WIDTH)
    shapes = [own, own, (3,) + own, (3,) + own, (2,) + own, (2, 3) + own]
    vmem = pl.BlockSpec(memory_space=pltpu.VMEM)
    return pl.pallas_call(
        final_kernel,
        out_shape=[jax.ShapeDtypeStruct(s, F32) for s in shapes],
        in_specs=[vmem] * len(arguments),
        out_specs=[vmem] * len(shapes),
        compiler_params=pltpu.CompilerParams(vmem_limit_bytes=VMEM_LIMIT),
        name="outputs",
    )(*arguments)


def per_device(density, anchor_mask, port_mask, heater_owner, heater_cell, heater_power):
    layers, height, _ = density.shape
    count = lax.axis_size("gx")
    devices = count * lax.axis_size("gz")
    heaters = tuple(a.reshape(1, -1) for a in (heater_owner, heater_cell, heater_power))
    heaters = tuple(pltpu.with_memory_space_constraint(a, pltpu.HBM) for a in (density, anchor_mask, port_mask) + heaters)
    first, second, far_one, far_two, own, entries = prepare(heaters, count)
    first = lax.ppermute(first, "gx", swap_pairs(count, 0, 1))
    second = lax.ppermute(second, "gx", swap_pairs(count, 1, 1))
    entries = lax.all_to_all(entries, "gx", 0, 0, tiled=True)
    far_one = lax.ppermute(far_one, "gx", swap_pairs(count, 0, 2))
    far_two = lax.ppermute(far_two, "gx", swap_pairs(count, 2, 2))
    own_z = across_z(own)
    first_z = across_z(first)
    second_z = across_z(second)
    heat, heat_far = scatter_heat(entries, layers, height)
    heat_z = across_z(heat)
    cub, papplied, pimage, pimage2, row = port_stage(
        (own, own_z, first, first_z, second, second_z), layers, height
    )
    source, applied, force, image, image2, sums = force_stage(
        (own, own_z, first, second, far_one, far_two, heat, heat_z, heat_far, cub, row), devices, layers, height
    )
    table = lax.all_to_all(sums, ("gx", "gz"), 0, 0, tiled=True)
    return tuple(
        final_stage(
            (table, source, own, applied, papplied, force, image, image2, pimage, pimage2), layers, height
        )
    )


def solution(mesh):
    in_specs = (
        P("gx", None, "gz"),
        P("gx", None, "gz"),
        P("gx", None, "gz"),
        P("gx", "gz", None, None),
        P("gx", "gz", None),
        P("gx", "gz", None),
    )
    out_specs = (
        P("gx", None, "gz"),
        P("gx", None, "gz"),
        P(None, "gx", None, "gz"),
        P(None, "gx", None, "gz"),
        P(None, "gx", None, "gz"),
        P(None, None, "gx", None, "gz"),
    )
    return jax.shard_map(per_device, mesh=mesh, in_specs=in_specs, out_specs=out_specs, check_vma=False)
```

time: 46.6 us -> 43.3 us (0.929)
  blocking collectives: 14.3 us -> 12.4 us
  waiting for transfers between devices: 10.7 us -> 9.47 us
    all_to_all x1, blocking collectives: 14.3 us -> 12.4 us  [per_device(): table = lax.all_to_all(sums, ('gx', 'gz'), 0, 0, tiled=True)]
    ppermute x1, waiting for transfers between devices: 3.26 us -> 2 us  [per_device(): far_one = lax.ppermute(far_one, 'gx', swap_pairs(count, 0, 2))]
    pallas_call x1 -> x2, Pallas kernels: 1.8 us -> 1.85 us  [in_memory(): pl.pallas_call(kernel, out_shape=[jax.ShapeDtypeStruct(s, F32) for s in s...]
  transfers between devices with their start and end apart: 9 -> 9, of which waited for: 2 -> 2; matrix products, arithmetic and copies ran while one was open for 0% -> 0% of each run, Pallas kernels for 3% -> 5%
where the time goes in v4:
time: 43.3 us; the launch traced here: 43 us
  starting transfers between devices  14.4 us (33%)
  blocking collectives  12.4 us (29%)
  waiting for transfers between devices  9.47 us (22%)
  Pallas kernels  6.03 us (14%)
  between operations  0.72 us (2%)
    all_to_all x1, blocking collectives, per_device(): table = lax.all_to_all(sums, ('gx', 'gz'), 0, 0, tiled=True)  12.4 us
    all_to_all x1, starting transfers between devices, per_device(): entries = lax.all_to_all(entries, 'gx', 0, 0, tiled=True)  8.65 us
    all_to_all x1, waiting for transfers between devices, per_device(): entries = lax.all_to_all(entries, 'gx', 0, 0, tiled=True)  7.45 us
    ppermute x1, starting transfers between devices, per_device(): first = lax.ppermute(first, 'gx', swap_pairs(count, 0, 1))  3.03 us
    ppermute x1, waiting for transfers between devices, per_device(): far_one = lax.ppermute(far_one, 'gx', swap_pairs(count, 0, 2))  2 us
    pallas_call x2, Pallas kernels, in_memory(): pl.pallas_call(kernel, out_shape=[jax.ShapeDtypeStruct(s, F32) for s in s...  1.85 us
    pallas_call x1, Pallas kernels, scatter_heat(): pl.pallas_call(functools.partial(heater_kernel, layers=layers, height=hei...  1.44 us
    pallas_call x1, Pallas kernels, prepare(): pl.pallas_call(prepare_kernel, out_shape=[jax.ShapeDtypeStruct(s, F32) fo...  1.42 us
  transfers between devices with their start and end apart: 9, of which 2 were waited for; matrix products, arithmetic and copies ran while one was open for 0% of the time, Pallas kernels for 5%

profile of v4, /device:TPU:0, one launch (start us, length us, event | category | flops | bytes accessed | tf_op | source)
XLA Modules:
  0.0 43.0 jit_solution(1444388852409991876)
XLA Ops:
  0.6 1.4 %prepare.1 = (f32[5,64,128]{2,1,0:T(8,128)S(1)}, f32[5,64,128]{2,1,0:T(8,128)S(1)}, f32[1,64,128]{2,1,0:T(8,128)S(1)}, f32[1,64,128]{2,1,0:T(8,128)S(1)}, f32[6,...) custom-call(f32[2,64,128]{2,1,0:T(8,128)} %density_hbm.1, s32[2,64,128]{2,1,0:T(8,128)} %anchor_hbm.1, s32[2,64,128]{2,1,0:T(8,128)} %port_hbm.1, ...), custom_call_target="tpu_custom_call" | custom-call | tf_op jit(solution)/shard_map/prepare/pallas_call | solution.py:104
  2.1 3.0 %collective-permute-start.1 = (f32[5,64,128]{2,1,0:T(8,128)S(1)}, f32[5,64,128]{2,1,0:T(8,128)S(1)}, u32[]{:S(2)}, u32[]{:S(2)}) collective-permute-start(f32[5,64,128]{2,1,0:T(8,128)S(1)} %get-tuple-element.26), channel_id=1, source_target_pairs={{0,2},{2,0},{4,6},{6,4},{8,10},{10,8},{12,14},{14,12},{16,18},{18,... | collective-permute-start | bytes 491528 | tf_op jit(solution)/shard_map/ppermute | solution.py:591
  5.1 0.7 %collective-permute-start.2 = (f32[5,64,128]{2,1,0:T(8,128)S(1)}, f32[5,64,128]{2,1,0:T(8,128)S(1)}, u32[]{:S(2)}, u32[]{:S(2)}) collective-permute-start(f32[5,64,128]{2,1,0:T(8,128)S(1)} %get-tuple-element.27), channel_id=1, source_target_pairs={{2,4},{4,2},{6,8},{8,6},{10,12},{12,10},{14,16},{16,14},{18,20},{2... | collective-permute-start | bytes 491528 | tf_op jit(solution)/shard_map/ppermute | solution.py:592
  5.8 8.7 %all-to-all-start = ((f32[16,3,256]{2,1,0:T(4,128)}), f32[16,3,256]{2,1,0:T(4,128)S(1)}, u32[]{:S(2)}, u32[]{:S(2)}) async-start(f32[16,3,256]{2,1,0:T(4,128)} %get-tuple-element.30), calls=%async_computation | async-start | bytes 131072 | tf_op jit(solution)/shard_map/all_to_all | solution.py:593
  14.4 0.1 collective-permute-start
  14.5 7.5 %all-to-all-done.entries_ref = f32[16,3,256]{2,1,0:T(4,128)S(1)} async-done(((f32[16,3,256]{2,1,0:T(4,128)}), f32[16,3,256]{2,1,0:T(4,128)S(1)}, u32[]{:S(2)}, u32[]{:S(2)}) %all-to-all-start) | async-done | bytes 49184 | tf_op jit(solution)/shard_map/all_to_all | solution.py:593
  21.9 1.4 %heater_scatter.1 = (f32[6,64,128]{2,1,0:T(8,128)S(1)}, f32[2,64,128]{2,1,0:T(8,128)S(1)}) custom-call(f32[16,3,256]{2,1,0:T(4,128)S(1)} %all-to-all-done.entries_ref), custom_call_target="tpu_custom_call" | custom-call | tf_op jit(solution)/shard_map/heater_scatter/pallas_call | solution.py:193
  23.4 0.1 collective-permute-start.5
  23.5 0.0 collective-permute-done.1.first_ref
  23.5 0.5 %collective-permute-start.6 = (f32[5,64,128]{2,1,0:T(8,128)S(1)}, f32[5,64,128]{2,1,0:T(8,128)S(1)}, u32[]{:S(2)}, u32[]{:S(2)}) collective-permute-start(f32[5,64,128]{2,1,0:T(8,128)S(1)} %collective-permute-done.1.first_ref), channel_id=1, source_target_pairs={{0,1},{1,0},{2,3},{3,2},{4,5},{5,4},{6,7},{7,6},{8,9},{9,8},{10,11... | collective-permute-start | bytes 491528 | tf_op jit(solution)/shard_map/ppermute | solution.py:40
  24.0 0.0 collective-permute-done.2.second_ref
  24.0 0.1 collective-permute-start.7
  24.1 0.7 %collective-permute-start.3 = (f32[1,64,128]{2,1,0:T(8,128)S(1)}, f32[1,64,128]{2,1,0:T(8,128)S(1)}, u32[]{:S(2)}, u32[]{:S(2)}) collective-permute-start(f32[1,64,128]{2,1,0:T(8,128)S(1)} %get-tuple-element.28), channel_id=1, source_target_pairs={{0,4},{4,0},{2,6},{6,2},{8,12},{12,8},{10,14},{14,10},{16,20},{20,... | collective-permute-start | bytes 98312 | tf_op jit(solution)/shard_map/ppermute | solution.py:594
  24.7 0.0 collective-permute-done.own_z_ref
  24.7 0.7 %collective-permute-start.4 = (f32[1,64,128]{2,1,0:T(8,128)S(1)}, f32[1,64,128]{2,1,0:T(8,128)S(1)}, u32[]{:S(2)}, u32[]{:S(2)}) collective-permute-start(f32[1,64,128]{2,1,0:T(8,128)S(1)} %get-tuple-element.29), channel_id=1, source_target_pairs={{4,8},{8,4},{6,10},{10,6},{12,16},{16,12},{14,18},{18,14},{20,24},... | collective-permute-start | bytes 98312 | tf_op jit(solution)/shard_map/ppermute | solution.py:595
  25.4 0.0 collective-permute-done.6.first_z_ref
  25.4 0.0 collective-permute-done.7.second_z_ref
  25.4 0.6 %shard_map.109 = (f32[2,6,80,128]{3,2,1,0:T(8,128)S(1)}, f32[2,64,128]{2,1,0:T(8,128)S(1)}, f32[2,64,128]{2,1,0:T(8,128)S(1)}, f32[2,64,128]{2,1,0:T(8,128)S(1)}, f32[1,128]{1,0:T(1,128)S(1)}) custom-call(f32[6,64,128]{2,1,0:T(8,128)S(1)} %get-tuple-element.25.own_ref, f32[6,64,128]{2,1,0:T(8,128)S(1)} %collective-permute-done.own_z_ref, ...), custom_call_target="tpu_custom_call" | custom-call | tf_op jit(solution)/shard_map/pallas_call | solution.py:492
  26.0 2.0 %collective-permute-done.3.far_one_ref = f32[1,64,128]{2,1,0:T(8,128)S(1)} collective-permute-done((f32[1,64,128]{2,1,0:T(8,128)S(1)}, f32[1,64,128]{2,1,0:T(8,128)S(1)}, u32[]{:S(2)}, u32[]{:S(2)}) %collective-permute-start.3) | collective-permute-done | bytes 32800 | tf_op jit(solution)/shard_map/ppermute | solution.py:594
  28.0 0.0 collective-permute-done.4.far_two_ref
  28.0 0.0 collective-permute-done.5.heat_z_ref
  28.0 1.3 %shard_map.110 = (f32[2,64,128]{2,1,0:T(8,128)S(1)}, f32[2,64,128]{2,1,0:T(8,128)S(1)}, f32[3,2,64,128]{3,2,1,0:T(8,128)S(1)}, f32[3,2,64,128]{3,2,1,0:T(8,128)S...) custom-call(f32[6,64,128]{2,1,0:T(8,128)S(1)} %get-tuple-element.25.own_ref, ...), custom_call_target="tpu_custom_call" | custom-call | tf_op jit(solution)/shard_map/pallas_call | solution.py:492
  29.3 12.4 %all_to_all.10.table_ref = f32[32,1,128]{2,1,0:T(1,128)S(1)} all-to-all(f32[32,1,128]{2,1,0:T(1,128)S(1)} %get-tuple-element.35), channel_id=1, replica_groups=mesh['gx'=16,'gz'=2] {'gx','gz'}, dimensions={0} | all-to-all | bytes 32768 | tf_op jit(solution)/shard_map/all_to_all | solution.py:607
  41.7 1.3 %outputs.1 = (f32[2,64,128]{2,1,0:T(8,128)}, f32[2,64,128]{2,1,0:T(8,128)}, f32[3,2,64,128]{3,2,1,0:T(8,128)}, f32[3,2,64,128]{3,2,1,0:T(8,128)}, f32[2,2,64,128...) custom-call(f32[32,1,128]{2,1,0:T(1,128)S(1)} %all_to_all.10.table_ref, f32[2,64,128]{2,1,0:T(8,128)S(1)} %get-tuple-element.36.source_ref, ...), custom_call_target="tpu_custom_call" | custom-call | tf_op jit(solution)/shard_map/outputs/pallas_call | solution.py:574
Async XLA Ops:
  2.1 21.4 %collective-permute-start.1 = (f32[5,64,128]{2,1,0:T(8,128)S(1)}, f32[5,64,128]{2,1,0:T(8,128)S(1)}, u32[]{:S(2)}, u32[]{:S(2)}) collective-permute-start(f32[5,64,128]{2,1,0:T(8,128)S(1)} %get-tuple-element.26), channel_id=1, source_target_pairs={{0,2},{2,0},{4,6},{6,4},{8,10},{10,8},{12,14},{14,12},{16,18},{18,... | collective-permute-start | bytes 491528 | tf_op jit(solution)/shard_map/ppermute | solution.py:591
  5.1 18.9 %collective-permute-start.2 = (f32[5,64,128]{2,1,0:T(8,128)S(1)}, f32[5,64,128]{2,1,0:T(8,128)S(1)}, u32[]{:S(2)}, u32[]{:S(2)}) collective-permute-start(f32[5,64,128]{2,1,0:T(8,128)S(1)} %get-tuple-element.27), channel_id=1, source_target_pairs={{2,4},{4,2},{6,8},{8,6},{10,12},{12,10},{14,16},{16,14},{18,20},{2... | collective-permute-start | bytes 491528 | tf_op jit(solution)/shard_map/ppermute | solution.py:592
  5.8 16.2 %all-to-all-start = ((f32[16,3,256]{2,1,0:T(4,128)}), f32[16,3,256]{2,1,0:T(4,128)S(1)}, u32[]{:S(2)}, u32[]{:S(2)}) async-start(f32[16,3,256]{2,1,0:T(4,128)} %get-tuple-element.30), calls=%async_computation | async-start | bytes 131072 | tf_op jit(solution)/shard_map/all_to_all | solution.py:593
  14.4 10.3 %collective-permute-start = (f32[6,64,128]{2,1,0:T(8,128)S(1)}, f32[6,64,128]{2,1,0:T(8,128)S(1)}, u32[]{:S(2)}, u32[]{:S(2)}) collective-permute-start(f32[6,64,128]{2,1,0:T(8,128)S(1)} %get-tuple-element.25.own_ref), channel_id=1, source_target_pairs={{0,1},{1,0},{2,3},{3,2},{4,5},{5,4},{6,7},{7,6},{8,9},{9,8},{10,11... | collective-permute-start | bytes 589832 | tf_op jit(solution)/shard_map/ppermute | solution.py:40
  23.4 4.6 %collective-permute-start.5 = (f32[6,64,128]{2,1,0:T(8,128)S(1)}, f32[6,64,128]{2,1,0:T(8,128)S(1)}, u32[]{:S(2)}, u32[]{:S(2)}) collective-permute-start(f32[6,64,128]{2,1,0:T(8,128)S(1)} %get-tuple-element.31.heat_ref), channel_id=1, source_target_pairs={{0,1},{1,0},{2,3},{3,2},{4,5},{5,4},{6,7},{7,6},{8,9},{9,8},{10,11... | collective-permute-start | bytes 589832 | tf_op jit(solution)/shard_map/ppermute | solution.py:40
  23.5 1.9 %collective-permute-start.6 = (f32[5,64,128]{2,1,0:T(8,128)S(1)}, f32[5,64,128]{2,1,0:T(8,128)S(1)}, u32[]{:S(2)}, u32[]{:S(2)}) collective-permute-start(f32[5,64,128]{2,1,0:T(8,128)S(1)} %collective-permute-done.1.first_ref), channel_id=1, source_target_pairs={{0,1},{1,0},{2,3},{3,2},{4,5},{5,4},{6,7},{7,6},{8,9},{9,8},{10,11... | collective-permute-start | bytes 491528 | tf_op jit(solution)/shard_map/ppermute | solution.py:40
  24.0 1.4 %collective-permute-start.7 = (f32[5,64,128]{2,1,0:T(8,128)S(1)}, f32[5,64,128]{2,1,0:T(8,128)S(1)}, u32[]{:S(2)}, u32[]{:S(2)}) collective-permute-start(f32[5,64,128]{2,1,0:T(8,128)S(1)} %collective-permute-done.2.second_ref), channel_id=1, source_target_pairs={{0,1},{1,0},{2,3},{3,2},{4,5},{5,4},{6,7},{7,6},{8,9},{9,8},{10,11... | collective-permute-start | bytes 491528 | tf_op jit(solution)/shard_map/ppermute | solution.py:40
  24.1 3.9 %collective-permute-start.3 = (f32[1,64,128]{2,1,0:T(8,128)S(1)}, f32[1,64,128]{2,1,0:T(8,128)S(1)}, u32[]{:S(2)}, u32[]{:S(2)}) collective-permute-start(f32[1,64,128]{2,1,0:T(8,128)S(1)} %get-tuple-element.28), channel_id=1, source_target_pairs={{0,4},{4,0},{2,6},{6,2},{8,12},{12,8},{10,14},{14,10},{16,20},{20,... | collective-permute-start | bytes 98312 | tf_op jit(solution)/shard_map/ppermute | solution.py:594
  24.7 3.3 %collective-permute-start.4 = (f32[1,64,128]{2,1,0:T(8,128)S(1)}, f32[1,64,128]{2,1,0:T(8,128)S(1)}, u32[]{:S(2)}, u32[]{:S(2)}) collective-permute-start(f32[1,64,128]{2,1,0:T(8,128)S(1)} %get-tuple-element.29), channel_id=1, source_target_pairs={{4,8},{8,4},{6,10},{10,6},{12,16},{16,12},{14,18},{18,14},{20,24},... | collective-permute-start | bytes 98312 | tf_op jit(solution)/shard_map/ppermute | solution.py:595

commit v5 on v4

--- a/solution.py
+++ b/solution.py
@@ -387,9 +387,8 @@
 
 
 def force_kernel(
-    own_ref, own_z_ref, first_ref, second_ref, far_one_ref, far_two_ref, heat_ref, heat_z_ref, heat_far_ref,
-    cub, row_ref,
-    source_ref, applied_ref, force_ref, image_ref, image2_ref, sums_ref,
+    own_ref, own_z_ref, first_ref, second_ref, heat_ref, heat_z_ref, cub, partial_ref,
+    source_ref, applied_ref, force_ref, image_ref, image2_ref, row_ref,
     stress, src, force, image, kept,
 ):
     block = Block(own_ref.shape[1])
@@ -411,14 +410,12 @@
                 if side == 0 and layer in (3, 4):
                     block.write(source_ref, s, layer - 3)
     for _ in block.strips():
-        one, two = block.read(far_one_ref, 0), block.read(far_two_ref, 0)
-        for layer, d in ((0, jnp.where(block.low_pair, two, one)), (7, jnp.where(block.low_pair, one, two))):
-            heated(0, layer, d * d * d, block.read(heat_far_ref, layer // 7))
-        for side, layer, index in ((0, 0, 1), (0, 2, 0), (1, 2, 0)):
-            mirrored = jnp.where(
-                block.gx == index, block.load(stress, side, layer + 1), block.load(stress, side, layer)
-            )
-            block.store(stress, side, layer, mirrored)
+        zero = jnp.zeros((STRIP, WIDTH), F32)
+        block.store(stress, 0, 0, jnp.where(block.gx == 1, block.load(stress, 0, 1), zero))
+        block.store(stress, 0, 7, zero)
+        for side in range(2):
+            mirrored = jnp.where(block.gx == 0, block.load(stress, side, 3), block.load(stress, side, 2))
+            block.store(stress, side, 2, mirrored)
 
     half = EXPANSION * 0.5
     for layer in range(1, 7):
@@ -479,7 +476,37 @@
                 block.accumulate("t", r * y)
                 block.accumulate("c", start * y)
     s, t, c = (block.total(name) for name in "stc")
-    row = row_ref[...] + block.row({0: q, 1: k, 4: n, 5: m, 6: s, 7: t, 8: c + s})
+    row_ref[...] = partial_ref[...] + block.row({0: q, 1: k, 4: n, 5: m, 6: s, 7: t, 8: c + s})
+
+
+def far_kernel(
+    far_one_ref, far_two_ref, heat_ref, cub, force_ref, image_ref, image2_ref, partial_ref,
+    corrected_ref, sums_ref,
+):
+    block = Block(force_ref.shape[2])
+    partial = partial_ref[...]
+    theta = ratio(partial[:, 5:6], partial[:, 4:5])
+
+    def face(a, b):
+        return MODULUS_MINIMUM + 0.5 * (a + b)
+
+    for _ in block.strips():
+        one, two = block.read(far_one_ref, 0), block.read(far_two_ref, 0)
+        for own, outer, d in (
+            (0, 0, jnp.where(block.low_pair, two, one)),
+            (1, 7, jnp.where(block.low_pair, one, two)),
+        ):
+            c = d * d * d
+            stress = (MODULUS_MINIMUM + c) * (JOULE_GAIN * (SIGMA_MIN + c) + block.read(heat_ref, own))
+            stress = block.masked(0, outer, stress)
+            chain = [block.load(cub, 0, k) for k in ((0, 1, 2) if own == 0 else (5, 4, 3))]
+            sign = -EXPANSION * 0.5 if own == 0 else EXPANSION * 0.5
+            change = sign * face(chain[0], chain[1]) * face(chain[1], chain[2]) * stress
+            block.write(corrected_ref, block.read(image2_ref, 0, own) + change, own)
+            start = block.read(force_ref, 0, own)
+            block.accumulate("t", (block.read(image_ref, 0, own) - theta * start) * change)
+            block.accumulate("c", start * change)
+    row = partial + block.row({7: block.total("t"), 8: block.total("c")})
     sums_ref[...] = jnp.broadcast_to(row[None], sums_ref.shape)
 
 
@@ -505,17 +532,21 @@
     return in_memory(port_kernel, arguments, shapes, [field(6, height), field(4, height), (2, 6, height, WIDTH)])
 
 
-def force_stage(arguments, devices, layers, height):
+def far_stage(arguments, devices, layers, height):
+    return in_memory(far_kernel, arguments, [(layers, height, WIDTH), (devices, 1, WIDTH)], [])
+
+
+def force_stage(arguments, layers, height):
     own = (layers, height, WIDTH)
     vectors = (3,) + own
-    shapes = [own, own, vectors, vectors, vectors, (devices, 1, WIDTH)]
+    shapes = [own, own, vectors, vectors, vectors, (1, WIDTH)]
     scratch = [field(8, height), field(4, height), field(18, height), field(12, height), (2, 6, height, WIDTH)]
     return in_memory(force_kernel, arguments, shapes, scratch)
 
 
 def final_kernel(
     table_ref, source_ref, own_ref, applied_ref, papplied_ref, force_ref, image_ref, image2_ref,
-    pimage_ref, pimage2_ref,
+    corrected_ref, pimage_ref, pimage2_ref,
     temperature_ref, adjoint_ref, displacement_ref, displacement_adjoint_ref, thermal_ref, elastic_ref,
 ):
     table = table_ref[...].reshape(table_ref.shape[0], WIDTH)
@@ -558,7 +589,8 @@
         thermal_ref[0, layer] = source - step0 * applied_ref[layer]
         thermal_ref[1, layer] = port - step1 * papplied_ref[layer]
         for k in range(3):
-            x, r = outcome(forward, force_ref[k, layer], image_ref[k, layer], image2_ref[k, layer])
+            second = image2_ref[k, layer] if k else corrected_ref[layer]
+            x, r = outcome(forward, force_ref[k, layer], image_ref[k, layer], second)
             displacement_ref[k, layer] = step0 * x
             elastic_ref[0, k, layer] = step0 * r
         x, r = outcome(adjoint, port, pimage_ref[layer], pimage2_ref[layer])
@@ -601,13 +633,16 @@
     cub, papplied, pimage, pimage2, row = port_stage(
         (own, own_z, first, first_z, second, second_z), layers, height
     )
-    source, applied, force, image, image2, sums = force_stage(
-        (own, own_z, first, second, far_one, far_two, heat, heat_z, heat_far, cub, row), devices, layers, height
+    source, applied, force, image, image2, row = force_stage(
+        (own, own_z, first, second, heat, heat_z, cub, row), layers, height
+    )
+    corrected, sums = far_stage(
+        (far_one, far_two, heat_far, cub, force, image, image2, row), devices, layers, height
     )
     table = lax.all_to_all(sums, ("gx", "gz"), 0, 0, tiled=True)
     return tuple(
         final_stage(
-            (table, source, own, applied, papplied, force, image, image2, pimage, pimage2), layers, height
+            (table, source, own, applied, papplied, force, image, image2, corrected, pimage, pimage2), layers, height
         )
     )
 

time: 43.3 us -> 42.3 us (0.977)
  waiting for transfers between devices: 9.47 us -> 8.19 us
    ppermute x1, waiting for transfers between devices: 2 us -> 0.72 us  [per_device(): far_one = lax.ppermute(far_one, 'gx', swap_pairs(count, 0, 2))]
    pallas_call x2 -> x3, Pallas kernels: 1.85 us -> 2.17 us  [in_memory(): pl.pallas_call(kernel, out_shape=[jax.ShapeDtypeStruct(s, F32) for s in s...]
  transfers between devices with their start and end apart: 9 -> 9, of which waited for: 2 -> 2; matrix products, arithmetic and copies ran while one was open for 0% -> 0% of each run, Pallas kernels for 5% -> 8%
where the time goes in v5:
time: 42.3 us; the launch traced here: 42.1 us
  starting transfers between devices  14.4 us (34%)
  blocking collectives  12.4 us (29%)
  waiting for transfers between devices  8.19 us (19%)
  Pallas kernels  6.36 us (15%)
  between operations  0.73 us (2%)
    all_to_all x1, blocking collectives, per_device(): table = lax.all_to_all(sums, ('gx', 'gz'), 0, 0, tiled=True)  12.4 us
    all_to_all x1, starting transfers between devices, per_device(): entries = lax.all_to_all(entries, 'gx', 0, 0, tiled=True)  8.65 us
    all_to_all x1, waiting for transfers between devices, per_device(): entries = lax.all_to_all(entries, 'gx', 0, 0, tiled=True)  7.45 us
    ppermute x1, starting transfers between devices, per_device(): first = lax.ppermute(first, 'gx', swap_pairs(count, 0, 1))  3.03 us
    pallas_call x3, Pallas kernels, in_memory(): pl.pallas_call(kernel, out_shape=[jax.ShapeDtypeStruct(s, F32) for s in s...  2.17 us
    pallas_call x1, Pallas kernels, scatter_heat(): pl.pallas_call(functools.partial(heater_kernel, layers=layers, height=hei...  1.44 us
    pallas_call x1, Pallas kernels, prepare(): pl.pallas_call(prepare_kernel, out_shape=[jax.ShapeDtypeStruct(s, F32) fo...  1.42 us
    pallas_call x1, Pallas kernels, final_stage(): pl.pallas_call(final_kernel, out_shape=[jax.ShapeDtypeStruct(s, F32) for...  1.34 us
  transfers between devices with their start and end apart: 9, of which 2 were waited for; matrix products, arithmetic and copies ran while one was open for 0% of the time, Pallas kernels for 8%

profile of v5, /device:TPU:0, one launch (start us, length us, event | category | flops | bytes accessed | tf_op | source)
XLA Modules:
  0.0 42.1 jit_solution(8378418489416580812)
XLA Ops:
  0.6 1.4 %prepare.1 = (f32[5,64,128]{2,1,0:T(8,128)S(1)}, f32[5,64,128]{2,1,0:T(8,128)S(1)}, f32[1,64,128]{2,1,0:T(8,128)S(1)}, f32[1,64,128]{2,1,0:T(8,128)S(1)}, f32[6,...) custom-call(f32[2,64,128]{2,1,0:T(8,128)} %density_hbm.1, s32[2,64,128]{2,1,0:T(8,128)} %anchor_hbm.1, s32[2,64,128]{2,1,0:T(8,128)} %port_hbm.1, ...), custom_call_target="tpu_custom_call" | custom-call | tf_op jit(solution)/shard_map/prepare/pallas_call | solution.py:104
  2.1 3.0 %collective-permute-start.3 = (f32[5,64,128]{2,1,0:T(8,128)S(1)}, f32[5,64,128]{2,1,0:T(8,128)S(1)}, u32[]{:S(2)}, u32[]{:S(2)}) collective-permute-start(f32[5,64,128]{2,1,0:T(8,128)S(1)} %get-tuple-element.32), channel_id=1, source_target_pairs={{0,2},{2,0},{4,6},{6,4},{8,10},{10,8},{12,14},{14,12},{16,18},{18,... | collective-permute-start | bytes 491528 | tf_op jit(solution)/shard_map/ppermute | solution.py:623
  5.1 0.7 %collective-permute-start.5 = (f32[5,64,128]{2,1,0:T(8,128)S(1)}, f32[5,64,128]{2,1,0:T(8,128)S(1)}, u32[]{:S(2)}, u32[]{:S(2)}) collective-permute-start(f32[5,64,128]{2,1,0:T(8,128)S(1)} %get-tuple-element.33), channel_id=1, source_target_pairs={{2,4},{4,2},{6,8},{8,6},{10,12},{12,10},{14,16},{16,14},{18,20},{2... | collective-permute-start | bytes 491528 | tf_op jit(solution)/shard_map/ppermute | solution.py:624
  5.8 8.7 %all-to-all-start = ((f32[16,3,256]{2,1,0:T(4,128)}), f32[16,3,256]{2,1,0:T(4,128)S(1)}, u32[]{:S(2)}, u32[]{:S(2)}) async-start(f32[16,3,256]{2,1,0:T(4,128)} %get-tuple-element.29), calls=%async_computation | async-start | bytes 131072 | tf_op jit(solution)/shard_map/all_to_all | solution.py:625
  14.4 0.1 collective-permute-start.2
  14.5 7.5 %all-to-all-done.entries_ref = f32[16,3,256]{2,1,0:T(4,128)S(1)} async-done(((f32[16,3,256]{2,1,0:T(4,128)}), f32[16,3,256]{2,1,0:T(4,128)S(1)}, u32[]{:S(2)}, u32[]{:S(2)}) %all-to-all-start) | async-done | bytes 49184 | tf_op jit(solution)/shard_map/all_to_all | solution.py:625
  21.9 1.4 %heater_scatter.1 = (f32[6,64,128]{2,1,0:T(8,128)S(1)}, f32[2,64,128]{2,1,0:T(8,128)S(1)}) custom-call(f32[16,3,256]{2,1,0:T(4,128)S(1)} %all-to-all-done.entries_ref), custom_call_target="tpu_custom_call" | custom-call | tf_op jit(solution)/shard_map/heater_scatter/pallas_call | solution.py:193
  23.4 0.1 collective-permute-start.7
  23.5 0.0 collective-permute-done.3.first_ref
  23.5 0.5 %collective-permute-start.4 = (f32[5,64,128]{2,1,0:T(8,128)S(1)}, f32[5,64,128]{2,1,0:T(8,128)S(1)}, u32[]{:S(2)}, u32[]{:S(2)}) collective-permute-start(f32[5,64,128]{2,1,0:T(8,128)S(1)} %collective-permute-done.3.first_ref), channel_id=1, source_target_pairs={{0,1},{1,0},{2,3},{3,2},{4,5},{5,4},{6,7},{7,6},{8,9},{9,8},{10,11... | collective-permute-start | bytes 491528 | tf_op jit(solution)/shard_map/ppermute | solution.py:40
  24.0 0.0 collective-permute-done.5.second_ref
  24.0 0.1 collective-permute-start.6
  24.1 0.7 %collective-permute-start = (f32[1,64,128]{2,1,0:T(8,128)S(1)}, f32[1,64,128]{2,1,0:T(8,128)S(1)}, u32[]{:S(2)}, u32[]{:S(2)}) collective-permute-start(f32[1,64,128]{2,1,0:T(8,128)S(1)} %get-tuple-element.27), channel_id=1, source_target_pairs={{0,4},{4,0},{2,6},{6,2},{8,12},{12,8},{10,14},{14,10},{16,20},{20,... | collective-permute-start | bytes 98312 | tf_op jit(solution)/shard_map/ppermute | solution.py:626
  24.7 0.0 collective-permute-done.2.own_z_ref
  24.7 0.7 %collective-permute-start.1 = (f32[1,64,128]{2,1,0:T(8,128)S(1)}, f32[1,64,128]{2,1,0:T(8,128)S(1)}, u32[]{:S(2)}, u32[]{:S(2)}) collective-permute-start(f32[1,64,128]{2,1,0:T(8,128)S(1)} %get-tuple-element.28), channel_id=1, source_target_pairs={{4,8},{8,4},{6,10},{10,6},{12,16},{16,12},{14,18},{18,14},{20,24},... | collective-permute-start | bytes 98312 | tf_op jit(solution)/shard_map/ppermute | solution.py:627
  25.4 0.0 collective-permute-done.4.first_z_ref
  25.4 0.0 collective-permute-done.6.second_z_ref
  25.4 0.6 %shard_map.109 = (f32[2,6,80,128]{3,2,1,0:T(8,128)S(1)}, f32[2,64,128]{2,1,0:T(8,128)S(1)}, f32[2,64,128]{2,1,0:T(8,128)S(1)}, f32[2,64,128]{2,1,0:T(8,128)S(1)}, f32[1,128]{1,0:T(1,128)S(1)}) custom-call(f32[6,64,128]{2,1,0:T(8,128)S(1)} %get-tuple-element.31.own_ref, f32[6,64,128]{2,1,0:T(8,128)S(1)} %collective-permute-done.2.own_z_ref, ...), custom_call_target="tpu_custom_call" | custom-call | tf_op jit(solution)/shard_map/pallas_call | solution.py:519
  26.0 0.0 collective-permute-done.7.heat_z_ref
  26.0 1.3 %shard_map.110 = (f32[2,64,128]{2,1,0:T(8,128)S(1)}, f32[2,64,128]{2,1,0:T(8,128)S(1)}, f32[3,2,64,128]{3,2,1,0:T(8,128)S(1)}, f32[3,2,64,128]{3,2,1,0:T(8,128)S...) custom-call(f32[6,64,128]{2,1,0:T(8,128)S(1)} %get-tuple-element.31.own_ref, ...), custom_call_target="tpu_custom_call" | custom-call | tf_op jit(solution)/shard_map/pallas_call | solution.py:519
  27.3 0.7 %collective-permute-done.far_one_ref = f32[1,64,128]{2,1,0:T(8,128)S(1)} collective-permute-done((f32[1,64,128]{2,1,0:T(8,128)S(1)}, f32[1,64,128]{2,1,0:T(8,128)S(1)}, u32[]{:S(2)}, u32[]{:S(2)}) %collective-permute-start) | collective-permute-done | bytes 32800 | tf_op jit(solution)/shard_map/ppermute | solution.py:626
  28.0 0.3 shard_map.111
  28.3 12.4 %all_to_all.10.table_ref = f32[32,1,128]{2,1,0:T(1,128)S(1)} all-to-all(f32[32,1,128]{2,1,0:T(1,128)S(1)} %get-tuple-element.41), channel_id=1, replica_groups=mesh['gx'=16,'gz'=2] {'gx','gz'}, dimensions={0} | all-to-all | bytes 32768 | tf_op jit(solution)/shard_map/all_to_all | solution.py:642
  40.7 1.3 %outputs.1 = (f32[2,64,128]{2,1,0:T(8,128)}, f32[2,64,128]{2,1,0:T(8,128)}, f32[3,2,64,128]{3,2,1,0:T(8,128)}, f32[3,2,64,128]{3,2,1,0:T(8,128)}, f32[2,2,64,128...) custom-call(f32[32,1,128]{2,1,0:T(1,128)S(1)} %all_to_all.10.table_ref, f32[2,64,128]{2,1,0:T(8,128)S(1)} %get-tuple-element.42.source_ref, ...), custom_call_target="tpu_custom_call" | custom-call | tf_op jit(solution)/shard_map/outputs/pallas_call | solution.py:606
  (1 shorter events, 0.0 us)
Async XLA Ops:
  2.1 21.4 %collective-permute-start.3 = (f32[5,64,128]{2,1,0:T(8,128)S(1)}, f32[5,64,128]{2,1,0:T(8,128)S(1)}, u32[]{:S(2)}, u32[]{:S(2)}) collective-permute-start(f32[5,64,128]{2,1,0:T(8,128)S(1)} %get-tuple-element.32), channel_id=1, source_target_pairs={{0,2},{2,0},{4,6},{6,4},{8,10},{10,8},{12,14},{14,12},{16,18},{18,... | collective-permute-start | bytes 491528 | tf_op jit(solution)/shard_map/ppermute | solution.py:623
  5.1 18.9 %collective-permute-start.5 = (f32[5,64,128]{2,1,0:T(8,128)S(1)}, f32[5,64,128]{2,1,0:T(8,128)S(1)}, u32[]{:S(2)}, u32[]{:S(2)}) collective-permute-start(f32[5,64,128]{2,1,0:T(8,128)S(1)} %get-tuple-element.33), channel_id=1, source_target_pairs={{2,4},{4,2},{6,8},{8,6},{10,12},{12,10},{14,16},{16,14},{18,20},{2... | collective-permute-start | bytes 491528 | tf_op jit(solution)/shard_map/ppermute | solution.py:624
  5.8 16.2 %all-to-all-start = ((f32[16,3,256]{2,1,0:T(4,128)}), f32[16,3,256]{2,1,0:T(4,128)S(1)}, u32[]{:S(2)}, u32[]{:S(2)}) async-start(f32[16,3,256]{2,1,0:T(4,128)} %get-tuple-element.29), calls=%async_computation | async-start | bytes 131072 | tf_op jit(solution)/shard_map/all_to_all | solution.py:625
  14.4 10.3 %collective-permute-start.2 = (f32[6,64,128]{2,1,0:T(8,128)S(1)}, f32[6,64,128]{2,1,0:T(8,128)S(1)}, u32[]{:S(2)}, u32[]{:S(2)}) collective-permute-start(f32[6,64,128]{2,1,0:T(8,128)S(1)} %get-tuple-element.31.own_ref), channel_id=1, source_target_pairs={{0,1},{1,0},{2,3},{3,2},{4,5},{5,4},{6,7},{7,6},{8,9},{9,8},{10,11... | collective-permute-start | bytes 589832 | tf_op jit(solution)/shard_map/ppermute | solution.py:40
  23.4 2.6 %collective-permute-start.7 = (f32[6,64,128]{2,1,0:T(8,128)S(1)}, f32[6,64,128]{2,1,0:T(8,128)S(1)}, u32[]{:S(2)}, u32[]{:S(2)}) collective-permute-start(f32[6,64,128]{2,1,0:T(8,128)S(1)} %get-tuple-element.35.heat_ref), channel_id=1, source_target_pairs={{0,1},{1,0},{2,3},{3,2},{4,5},{5,4},{6,7},{7,6},{8,9},{9,8},{10,11... | collective-permute-start | bytes 589832 | tf_op jit(solution)/shard_map/ppermute | solution.py:40
  23.5 1.9 %collective-permute-start.4 = (f32[5,64,128]{2,1,0:T(8,128)S(1)}, f32[5,64,128]{2,1,0:T(8,128)S(1)}, u32[]{:S(2)}, u32[]{:S(2)}) collective-permute-start(f32[5,64,128]{2,1,0:T(8,128)S(1)} %collective-permute-done.3.first_ref), channel_id=1, source_target_pairs={{0,1},{1,0},{2,3},{3,2},{4,5},{5,4},{6,7},{7,6},{8,9},{9,8},{10,11... | collective-permute-start | bytes 491528 | tf_op jit(solution)/shard_map/ppermute | solution.py:40
  24.0 1.4 %collective-permute-start.6 = (f32[5,64,128]{2,1,0:T(8,128)S(1)}, f32[5,64,128]{2,1,0:T(8,128)S(1)}, u32[]{:S(2)}, u32[]{:S(2)}) collective-permute-start(f32[5,64,128]{2,1,0:T(8,128)S(1)} %collective-permute-done.5.second_ref), channel_id=1, source_target_pairs={{0,1},{1,0},{2,3},{3,2},{4,5},{5,4},{6,7},{7,6},{8,9},{9,8},{10,11... | collective-permute-start | bytes 491528 | tf_op jit(solution)/shard_map/ppermute | solution.py:40
  24.1 3.9 %collective-permute-start = (f32[1,64,128]{2,1,0:T(8,128)S(1)}, f32[1,64,128]{2,1,0:T(8,128)S(1)}, u32[]{:S(2)}, u32[]{:S(2)}) collective-permute-start(f32[1,64,128]{2,1,0:T(8,128)S(1)} %get-tuple-element.27), channel_id=1, source_target_pairs={{0,4},{4,0},{2,6},{6,2},{8,12},{12,8},{10,14},{14,10},{16,20},{20,... | collective-permute-start | bytes 98312 | tf_op jit(solution)/shard_map/ppermute | solution.py:626
  24.7 3.3 %collective-permute-start.1 = (f32[1,64,128]{2,1,0:T(8,128)S(1)}, f32[1,64,128]{2,1,0:T(8,128)S(1)}, u32[]{:S(2)}, u32[]{:S(2)}) collective-permute-start(f32[1,64,128]{2,1,0:T(8,128)S(1)} %get-tuple-element.28), channel_id=1, source_target_pairs={{4,8},{8,4},{6,10},{10,6},{12,16},{16,12},{14,18},{18,14},{20,24},... | collective-permute-start | bytes 98312 | tf_op jit(solution)/shard_map/ppermute | solution.py:627

commit v6 on v5

--- a/solution.py
+++ b/solution.py
@@ -114,74 +114,60 @@
     )(*arguments)
 
 
-def heater_kernel(entries_ref, heat_ref, far_ref, rows_ref, lanes_ref, *total_refs, layers, height, block):
+def heater_kernel(entries_ref, heat_ref, rows_ref, lanes_ref, *total_refs, layers, block, outermost):
     sources = entries_ref.shape[0]
     entries = entries_ref.shape[2]
-    slabs = layers + 2 * HALO
+    slabs, height, _ = heat_ref.shape
     base = lax.axis_index("gx") * layers - HALO
+    last = layers + 2 * HALO - 1
     plane_bits = (height * WIDTH).bit_length() - 1
     lane_bits = WIDTH.bit_length() - 1
     height_bits = height.bit_length() - 1
-    group = slabs * height
-    row_ids = lax.broadcasted_iota(jnp.int32, (group, entries), 0)
+    row_ids = lax.broadcasted_iota(jnp.int32, (slabs * height, entries), 0)
     lane_ids = lax.broadcasted_iota(jnp.int32, (WIDTH, entries), 0)
 
-    def one_block(start, keep):
-        rows = []
+    def one_block(start):
         for k in range(block):
             table = entries_ref[start + k]
             owner = table[0:1].astype(jnp.int32)
             cell = table[1:2].astype(jnp.int32)
             power = table[2:3]
             slab = owner * layers + (cell >> plane_bits) - base
-            rows.append((slab << height_bits) + ((cell >> lane_bits) & (height - 1)))
+            if outermost:
+                place = jnp.where(slab == 0, 0, jnp.where(slab == last, 1, -1))
+            else:
+                place = slab - 1
+            row = (place << height_bits) + ((cell >> lane_bits) & (height - 1))
             high = power.astype(jnp.bfloat16).astype(F32)
             low = power - high
             here = slice(k * entries, (k + 1) * entries)
             match = lane_ids == (cell & (WIDTH - 1))
             lanes_ref[0:WIDTH, here] = jnp.where(match, high, 0.0).astype(jnp.bfloat16)
             lanes_ref[WIDTH:, here] = jnp.where(match, low, 0.0).astype(jnp.bfloat16)
-            rows_ref[:, here] = jnp.where(row_ids == rows[k], 1.0, 0.0).astype(jnp.bfloat16)
-        both = None
-        width = block * entries // 1
-        for k in range(1):
-            here = slice(k * width, (k + 1) * width)
-            part = lax.dot_general(
-                rows_ref[:, here], lanes_ref[:, here], (((1,), (1,)), ((), ())), preferred_element_type=F32
-            )
-            both = part if both is None else both + part
-        keep(0, both[:, :WIDTH] + both[:, WIDTH:])
-
-    def write(first, part):
-        for k in range(group // height):
-            slab = first // height + k
-            value = part[k * height : (k + 1) * height]
-            if slab in (0, slabs - 1):
-                far_ref[slab // (slabs - 1)] = value
-            else:
-                heat_ref[slab - 1] = value
+            rows_ref[:, here] = jnp.where(row_ids == row, 1.0, 0.0).astype(jnp.bfloat16)
+        both = lax.dot_general(
+            rows_ref[...], lanes_ref[...], (((1,), (1,)), ((), ())), preferred_element_type=F32
+        )
+        return both[:, :WIDTH] + both[:, WIDTH:]
 
     if sources == block:
-        one_block(0, write)
-        return
-    total_ref = total_refs[0]
-    total_ref[...] = jnp.zeros_like(total_ref)
-
-    def add(first, part):
-        total_ref[first : first + group, :] += part
-
-    @pl.loop(0, sources // block)
-    def _(step):
-        one_block(step * block, add)
-
-    for first in range(0, slabs * height, group):
-        write(first, total_ref[first : first + group, :])
-
-
-def scatter_heat(entries, layers, height):
+        total = one_block(0)
+    else:
+        total_ref = total_refs[0]
+        total_ref[...] = jnp.zeros_like(total_ref)
+
+        @pl.loop(0, sources // block)
+        def _(step):
+            total_ref[...] += one_block(step * block)
+
+        total = total_ref[...]
+    heat_ref[...] = total.reshape(slabs, height, WIDTH)
+
+
+def scatter_heat(entries, layers, height, outermost):
     sources, _, count = entries.shape
     block = min(sources, 16)
-    slabs = layers + 2 * HALO
+    slabs = 2 if outermost else layers + 2 * HALO - 2
     if height & (height - 1) or sources % block:
         raise ValueError("unsupported sizes")
     scratch = [
@@ -191,13 +177,13 @@
     if sources > block:
         scratch.append(pltpu.VMEM((slabs * height, WIDTH), F32))
     return pl.pallas_call(
-        functools.partial(heater_kernel, layers=layers, height=height, block=block),
-        out_shape=[jax.ShapeDtypeStruct((k, height, WIDTH), F32) for k in (slabs - 2, 2)],
+        functools.partial(heater_kernel, layers=layers, block=block, outermost=outermost),
+        out_shape=jax.ShapeDtypeStruct((slabs, height, WIDTH), F32),
         in_specs=[pl.BlockSpec(memory_space=pltpu.VMEM)],
-        out_specs=[pl.BlockSpec(memory_space=pltpu.VMEM)] * 2,
+        out_specs=pl.BlockSpec(memory_space=pltpu.VMEM),
         scratch_shapes=scratch,
         compiler_params=pltpu.CompilerParams(vmem_limit_bytes=VMEM_LIMIT),
-        name="heater_scatter",
+        name="far_scatter" if outermost else "heater_scatter",
     )(entries)
 
 
@@ -628,7 +614,8 @@
     own_z = across_z(own)
     first_z = across_z(first)
     second_z = across_z(second)
-    heat, heat_far = scatter_heat(entries, layers, height)
+    heat = scatter_heat(entries, layers, height, False)
+    heat_far = scatter_heat(entries, layers, height, True)
     heat_z = across_z(heat)
     cub, papplied, pimage, pimage2, row = port_stage(
         (own, own_z, first, first_z, second, second_z), layers, height

time: 42.3 us -> 42.1 us (level)
  waiting for transfers between devices: 8.19 us -> 7.47 us
  Pallas kernels: 6.36 us -> 6.97 us
    ppermute x1, waiting for transfers between devices: 0.72 us -> 0.01 us  [per_device(): far_one = lax.ppermute(far_one, 'gx', swap_pairs(count, 0, 2))]
    pallas_call x1 -> x2, Pallas kernels: 1.44 us -> 2.04 us  [scatter_heat(): pl.pallas_call(functools.partial(heater_kernel, layers=layers, block=bloc...]
  transfers between devices with their start and end apart: 9 -> 9, of which waited for: 2 -> 1; matrix products, arithmetic and copies ran while one was open for 0% -> 0% of each run, Pallas kernels for 8% -> 9%
where the time goes in v6:
time: 42.1 us; the launch traced here: 41.8 us
  starting transfers between devices  14.4 us (34%)
  blocking collectives  12.2 us (29%)
  waiting for transfers between devices  7.47 us (18%)
  Pallas kernels  6.97 us (17%)
  between operations  0.73 us (2%)
    all_to_all x1, blocking collectives, per_device(): table = lax.all_to_all(sums, ('gx', 'gz'), 0, 0, tiled=True)  12.2 us
    all_to_all x1, starting transfers between devices, per_device(): entries = lax.all_to_all(entries, 'gx', 0, 0, tiled=True)  8.65 us
    all_to_all x1, waiting for transfers between devices, per_device(): entries = lax.all_to_all(entries, 'gx', 0, 0, tiled=True)  7.45 us
    ppermute x1, starting transfers between devices, per_device(): first = lax.ppermute(first, 'gx', swap_pairs(count, 0, 1))  3.03 us
    pallas_call x3, Pallas kernels, in_memory(): pl.pallas_call(kernel, out_shape=[jax.ShapeDtypeStruct(s, F32) for s in s...  2.19 us
    pallas_call x2, Pallas kernels, scatter_heat(): pl.pallas_call(functools.partial(heater_kernel, layers=layers, block=bloc...  2.04 us
    pallas_call x1, Pallas kernels, prepare(): pl.pallas_call(prepare_kernel, out_shape=[jax.ShapeDtypeStruct(s, F32) fo...  1.42 us
    pallas_call x1, Pallas kernels, final_stage(): pl.pallas_call(final_kernel, out_shape=[jax.ShapeDtypeStruct(s, F32) for...  1.34 us
  transfers between devices with their start and end apart: 9, of which 1 were waited for; matrix products, arithmetic and copies ran while one was open for 0% of the time, Pallas kernels for 9%

profile of v6, /device:TPU:0, one launch (start us, length us, event | category | flops | bytes accessed | tf_op | source)
XLA Modules:
  0.0 41.8 jit_solution(7425212001863672319)
XLA Ops:
  0.6 1.4 %prepare.1 = (f32[5,64,128]{2,1,0:T(8,128)S(1)}, f32[5,64,128]{2,1,0:T(8,128)S(1)}, f32[1,64,128]{2,1,0:T(8,128)S(1)}, f32[1,64,128]{2,1,0:T(8,128)S(1)}, f32[6,...) custom-call(f32[2,64,128]{2,1,0:T(8,128)} %density_hbm.1, s32[2,64,128]{2,1,0:T(8,128)} %anchor_hbm.1, s32[2,64,128]{2,1,0:T(8,128)} %port_hbm.1, ...), custom_call_target="tpu_custom_call" | custom-call | tf_op jit(solution)/shard_map/prepare/pallas_call | solution.py:104
  2.1 3.0 %collective-permute-start.3 = (f32[5,64,128]{2,1,0:T(8,128)S(1)}, f32[5,64,128]{2,1,0:T(8,128)S(1)}, u32[]{:S(2)}, u32[]{:S(2)}) collective-permute-start(f32[5,64,128]{2,1,0:T(8,128)S(1)} %get-tuple-element.29), channel_id=1, source_target_pairs={{0,2},{2,0},{4,6},{6,4},{8,10},{10,8},{12,14},{14,12},{16,18},{18,... | collective-permute-start | bytes 491528 | tf_op jit(solution)/shard_map/ppermute | solution.py:609
  5.1 0.7 %collective-permute-start.5 = (f32[5,64,128]{2,1,0:T(8,128)S(1)}, f32[5,64,128]{2,1,0:T(8,128)S(1)}, u32[]{:S(2)}, u32[]{:S(2)}) collective-permute-start(f32[5,64,128]{2,1,0:T(8,128)S(1)} %get-tuple-element.30), channel_id=1, source_target_pairs={{2,4},{4,2},{6,8},{8,6},{10,12},{12,10},{14,16},{16,14},{18,20},{2... | collective-permute-start | bytes 491528 | tf_op jit(solution)/shard_map/ppermute | solution.py:610
  5.8 8.7 %all-to-all-start = ((f32[16,3,256]{2,1,0:T(4,128)}), f32[16,3,256]{2,1,0:T(4,128)S(1)}, u32[]{:S(2)}, u32[]{:S(2)}) async-start(f32[16,3,256]{2,1,0:T(4,128)} %get-tuple-element.27), calls=%async_computation | async-start | bytes 131072 | tf_op jit(solution)/shard_map/all_to_all | solution.py:611
  14.4 0.1 collective-permute-start.2
  14.5 7.5 %all-to-all-done.entries_ref = f32[16,3,256]{2,1,0:T(4,128)S(1)} async-done(((f32[16,3,256]{2,1,0:T(4,128)}), f32[16,3,256]{2,1,0:T(4,128)S(1)}, u32[]{:S(2)}, u32[]{:S(2)}) %all-to-all-start) | async-done | bytes 49184 | tf_op jit(solution)/shard_map/all_to_all | solution.py:611
  21.9 1.1 %heater_scatter.1.heat_ref = f32[6,64,128]{2,1,0:T(8,128)S(1)} custom-call(f32[16,3,256]{2,1,0:T(4,128)S(1)} %all-to-all-done.entries_ref), custom_call_target="tpu_custom_call" | custom-call | tf_op jit(solution)/shard_map/heater_scatter/pallas_call | solution.py:179
  23.1 0.1 collective-permute-start.7
  23.2 0.0 collective-permute-done.3.first_ref
  23.2 0.5 %collective-permute-start.4 = (f32[5,64,128]{2,1,0:T(8,128)S(1)}, f32[5,64,128]{2,1,0:T(8,128)S(1)}, u32[]{:S(2)}, u32[]{:S(2)}) collective-permute-start(f32[5,64,128]{2,1,0:T(8,128)S(1)} %collective-permute-done.3.first_ref), channel_id=1, source_target_pairs={{0,1},{1,0},{2,3},{3,2},{4,5},{5,4},{6,7},{7,6},{8,9},{9,8},{10,11... | collective-permute-start | bytes 491528 | tf_op jit(solution)/shard_map/ppermute | solution.py:40
  23.7 0.0 collective-permute-done.5.second_ref
  23.7 0.1 collective-permute-start.6
  23.8 0.6 %collective-permute-start = (f32[1,64,128]{2,1,0:T(8,128)S(1)}, f32[1,64,128]{2,1,0:T(8,128)S(1)}, u32[]{:S(2)}, u32[]{:S(2)}) collective-permute-start(f32[1,64,128]{2,1,0:T(8,128)S(1)} %get-tuple-element.25), channel_id=1, source_target_pairs={{0,4},{4,0},{2,6},{6,2},{8,12},{12,8},{10,14},{14,10},{16,20},{20,... | collective-permute-start | bytes 98312 | tf_op jit(solution)/shard_map/ppermute | solution.py:612
  24.4 0.0 collective-permute-done.2.own_z_ref
  24.4 0.7 %collective-permute-start.1 = (f32[1,64,128]{2,1,0:T(8,128)S(1)}, f32[1,64,128]{2,1,0:T(8,128)S(1)}, u32[]{:S(2)}, u32[]{:S(2)}) collective-permute-start(f32[1,64,128]{2,1,0:T(8,128)S(1)} %get-tuple-element.26), channel_id=1, source_target_pairs={{4,8},{8,4},{6,10},{10,6},{12,16},{16,12},{14,18},{18,14},{20,24},... | collective-permute-start | bytes 98312 | tf_op jit(solution)/shard_map/ppermute | solution.py:613
  25.1 0.9 %far_scatter.1.heat_ref = f32[2,64,128]{2,1,0:T(8,128)S(1)} custom-call(f32[16,3,256]{2,1,0:T(4,128)S(1)} %all-to-all-done.entries_ref), custom_call_target="tpu_custom_call" | custom-call | tf_op jit(solution)/shard_map/far_scatter/pallas_call | solution.py:179
  26.0 0.0 collective-permute-done.4.first_z_ref
  26.0 0.0 collective-permute-done.6.second_z_ref
  26.0 0.6 %shard_map.109 = (f32[2,6,80,128]{3,2,1,0:T(8,128)S(1)}, f32[2,64,128]{2,1,0:T(8,128)S(1)}, f32[2,64,128]{2,1,0:T(8,128)S(1)}, f32[2,64,128]{2,1,0:T(8,128)S(1)}, f32[1,128]{1,0:T(1,128)S(1)}) custom-call(f32[6,64,128]{2,1,0:T(8,128)S(1)} %get-tuple-element.28.own_ref, f32[6,64,128]{2,1,0:T(8,128)S(1)} %collective-permute-done.2.own_z_ref, ...), custom_call_target="tpu_custom_call" | custom-call | tf_op jit(solution)/shard_map/pallas_call | solution.py:505
  26.6 0.0 collective-permute-done.7.heat_z_ref
  26.6 1.3 %shard_map.110 = (f32[2,64,128]{2,1,0:T(8,128)S(1)}, f32[2,64,128]{2,1,0:T(8,128)S(1)}, f32[3,2,64,128]{3,2,1,0:T(8,128)S(1)}, f32[3,2,64,128]{3,2,1,0:T(8,128)S...) custom-call(f32[6,64,128]{2,1,0:T(8,128)S(1)} %get-tuple-element.28.own_ref, ...), custom_call_target="tpu_custom_call" | custom-call | tf_op jit(solution)/shard_map/pallas_call | solution.py:505
  27.9 0.3 shard_map.111
  28.2 12.2 %all_to_all.10.table_ref = f32[32,1,128]{2,1,0:T(1,128)S(1)} all-to-all(f32[32,1,128]{2,1,0:T(1,128)S(1)} %get-tuple-element.37), channel_id=1, replica_groups=mesh['gx'=16,'gz'=2] {'gx','gz'}, dimensions={0} | all-to-all | bytes 32768 | tf_op jit(solution)/shard_map/all_to_all | solution.py:629
  40.4 1.3 %outputs.1 = (f32[2,64,128]{2,1,0:T(8,128)}, f32[2,64,128]{2,1,0:T(8,128)}, f32[3,2,64,128]{3,2,1,0:T(8,128)}, f32[3,2,64,128]{3,2,1,0:T(8,128)}, f32[2,2,64,128...) custom-call(f32[32,1,128]{2,1,0:T(1,128)S(1)} %all_to_all.10.table_ref, f32[2,64,128]{2,1,0:T(8,128)S(1)} %get-tuple-element.38.source_ref, ...), custom_call_target="tpu_custom_call" | custom-call | tf_op jit(solution)/shard_map/outputs/pallas_call | solution.py:592
  (2 shorter events, 0.0 us)
Async XLA Ops:
  2.1 21.1 %collective-permute-start.3 = (f32[5,64,128]{2,1,0:T(8,128)S(1)}, f32[5,64,128]{2,1,0:T(8,128)S(1)}, u32[]{:S(2)}, u32[]{:S(2)}) collective-permute-start(f32[5,64,128]{2,1,0:T(8,128)S(1)} %get-tuple-element.29), channel_id=1, source_target_pairs={{0,2},{2,0},{4,6},{6,4},{8,10},{10,8},{12,14},{14,12},{16,18},{18,... | collective-permute-start | bytes 491528 | tf_op jit(solution)/shard_map/ppermute | solution.py:609
  5.1 18.6 %collective-permute-start.5 = (f32[5,64,128]{2,1,0:T(8,128)S(1)}, f32[5,64,128]{2,1,0:T(8,128)S(1)}, u32[]{:S(2)}, u32[]{:S(2)}) collective-permute-start(f32[5,64,128]{2,1,0:T(8,128)S(1)} %get-tuple-element.30), channel_id=1, source_target_pairs={{2,4},{4,2},{6,8},{8,6},{10,12},{12,10},{14,16},{16,14},{18,20},{2... | collective-permute-start | bytes 491528 | tf_op jit(solution)/shard_map/ppermute | solution.py:610
  5.8 16.2 %all-to-all-start = ((f32[16,3,256]{2,1,0:T(4,128)}), f32[16,3,256]{2,1,0:T(4,128)S(1)}, u32[]{:S(2)}, u32[]{:S(2)}) async-start(f32[16,3,256]{2,1,0:T(4,128)} %get-tuple-element.27), calls=%async_computation | async-start | bytes 131072 | tf_op jit(solution)/shard_map/all_to_all | solution.py:611
  14.4 10.0 %collective-permute-start.2 = (f32[6,64,128]{2,1,0:T(8,128)S(1)}, f32[6,64,128]{2,1,0:T(8,128)S(1)}, u32[]{:S(2)}, u32[]{:S(2)}) collective-permute-start(f32[6,64,128]{2,1,0:T(8,128)S(1)} %get-tuple-element.28.own_ref), channel_id=1, source_target_pairs={{0,1},{1,0},{2,3},{3,2},{4,5},{5,4},{6,7},{7,6},{8,9},{9,8},{10,11... | collective-permute-start | bytes 589832 | tf_op jit(solution)/shard_map/ppermute | solution.py:40
  23.1 3.5 %collective-permute-start.7 = (f32[6,64,128]{2,1,0:T(8,128)S(1)}, f32[6,64,128]{2,1,0:T(8,128)S(1)}, u32[]{:S(2)}, u32[]{:S(2)}) collective-permute-start(f32[6,64,128]{2,1,0:T(8,128)S(1)} %heater_scatter.1.heat_ref), channel_id=1, source_target_pairs={{0,1},{1,0},{2,3},{3,2},{4,5},{5,4},{6,7},{7,6},{8,9},{9,8},{10,11... | collective-permute-start | bytes 589832 | tf_op jit(solution)/shard_map/ppermute | solution.py:40
  23.2 2.8 %collective-permute-start.4 = (f32[5,64,128]{2,1,0:T(8,128)S(1)}, f32[5,64,128]{2,1,0:T(8,128)S(1)}, u32[]{:S(2)}, u32[]{:S(2)}) collective-permute-start(f32[5,64,128]{2,1,0:T(8,128)S(1)} %collective-permute-done.3.first_ref), channel_id=1, source_target_pairs={{0,1},{1,0},{2,3},{3,2},{4,5},{5,4},{6,7},{7,6},{8,9},{9,8},{10,11... | collective-permute-start | bytes 491528 | tf_op jit(solution)/shard_map/ppermute | solution.py:40
  23.7 2.3 %collective-permute-start.6 = (f32[5,64,128]{2,1,0:T(8,128)S(1)}, f32[5,64,128]{2,1,0:T(8,128)S(1)}, u32[]{:S(2)}, u32[]{:S(2)}) collective-permute-start(f32[5,64,128]{2,1,0:T(8,128)S(1)} %collective-permute-done.5.second_ref), channel_id=1, source_target_pairs={{0,1},{1,0},{2,3},{3,2},{4,5},{5,4},{6,7},{7,6},{8,9},{9,8},{10,11... | collective-permute-start | bytes 491528 | tf_op jit(solution)/shard_map/ppermute | solution.py:40
  23.8 4.1 %collective-permute-start = (f32[1,64,128]{2,1,0:T(8,128)S(1)}, f32[1,64,128]{2,1,0:T(8,128)S(1)}, u32[]{:S(2)}, u32[]{:S(2)}) collective-permute-start(f32[1,64,128]{2,1,0:T(8,128)S(1)} %get-tuple-element.25), channel_id=1, source_target_pairs={{0,4},{4,0},{2,6},{6,2},{8,12},{12,8},{10,14},{14,10},{16,20},{20,... | collective-permute-start | bytes 98312 | tf_op jit(solution)/shard_map/ppermute | solution.py:612
  24.4 3.5 %collective-permute-start.1 = (f32[1,64,128]{2,1,0:T(8,128)S(1)}, f32[1,64,128]{2,1,0:T(8,128)S(1)}, u32[]{:S(2)}, u32[]{:S(2)}) collective-permute-start(f32[1,64,128]{2,1,0:T(8,128)S(1)} %get-tuple-element.26), channel_id=1, source_target_pairs={{4,8},{8,4},{6,10},{10,6},{12,16},{16,12},{14,18},{18,14},{20,24},... | collective-permute-start | bytes 98312 | tf_op jit(solution)/shard_map/ppermute | solution.py:613
